TPU v7x, 32 devices: a whole 2x2x4 slice. The times are simulated.
32 devices in a mesh: groups: 2 (over x), tm: 8 (over z, y), rep: 2 (over core).
Axes of the slice: x: 2, y: 2, z: 4, core: 2. Of those that a mesh axis runs over, the one named last changes fastest.
Arguments:
- signal: bfloat16 [32768, 1024], P(('groups', 'tm')), parts along dimension 0, may hold values from -6 to 6
- embed_weight: bfloat16 [1024, 512], P('rep'), may hold values from -0.1875 to 0.1875
- norm_gain: float32 [512], replicated, may hold values from 0.5 to 1.5
- qkv_weight: bfloat16 [512, 3, 512], P(None, None, 'rep'), may hold values from -0.25 to 0.25
- conv_weight: float32 [4, 3, 512], P(None, None, 'rep'), may hold values from -1.5 to 1.5
- feature_weight: bfloat16 [8, 64, 128], P('rep'), may hold values from -2.5 to 2.5
- out_weight: bfloat16 [512, 512], P('rep'), may hold values from -0.25 to 0.25
Outputs:
- mixed_out: bfloat16 [32768, 512], P(('groups', 'tm', 'rep')), parts along dimension 0
There are 2 independent parts, one for each index of `groups`. A program takes and returns all parts, laid end to end along the dimension named above; an argument that names none is the same for every part. Nothing has to cross between parts.
All inputs are finite; a program needn't handle non-finite values.
Results may differ from a plain program's by a relative error of at most 0.0085.
Values may be sent and summed in bfloat16 or wider, within the bound.
No kernel may reach another device: no remote copies, remote signals or barrier semaphores. Data moves between devices by JAX's collectives and lax.ppermute only.
A program may use at most 64 MiB of HBM per device.

v0:
```python
import jax
import jax.numpy as jnp
from jax import lax
from jax.sharding import PartitionSpec as P

BLOCK = 512


def shifted(array, axis, by):
    devices = lax.axis_size(axis)
    pairs = [(i, i + by) for i in range(devices) if 0 <= i + by < devices]
    return lax.ppermute(array, axis, pairs)


def prefix(array, axis, join, neutral):
    place = lax.axis_index(axis)
    gathered = jax.tree.map(
        lambda a, kind: lax.all_gather(a.astype(kind), axis), array, (jnp.bfloat16, jnp.bfloat16)
    )
    state = jax.tree.map(lambda a, e: jnp.zeros_like(a) + jnp.asarray(e, a.dtype), array, neutral)

    def one(hop, state):
        return join(
            state,
            jax.tree.map(
                lambda a, own: lax.dynamic_index_in_dim(a, hop, 0, False).astype(own.dtype),
                gathered,
                array,
            ),
        )

    return lax.fori_loop(0, place, one, state)


def local_block(query_blk, key_blk, value_blk):
    scores = jnp.einsum("thf,shf->hts", query_blk, key_blk, preferred_element_type=jnp.float32)
    causal = jnp.arange(BLOCK)[:, None] >= jnp.arange(BLOCK)[None, :]
    weights = jnp.where(causal[None], scores, 0.0).astype(jnp.bfloat16)
    numer = jnp.einsum("hts,shd->thd", weights, value_blk, preferred_element_type=jnp.float32)
    denom = jnp.sum(weights, -1, dtype=jnp.float32).T
    return (numer, denom)


def add_pair(earlier, later):
    return (earlier[0] + later[0], earlier[1] + later[1])


def embed_norm(sig_rows, embed_weight, norm_gain):
    embedded = jnp.dot(
        sig_rows,
        lax.all_gather(embed_weight, "rep", axis=0, tiled=True),
        preferred_element_type=jnp.float32,
    )
    return (
        embedded * lax.rsqrt(jnp.mean(embedded * embedded, -1, keepdims=True) + 1e-05) * norm_gain
    ).astype(jnp.bfloat16)


def feature_map(part, feat_weights):
    high = lax.Precision.HIGHEST
    part_f = part.astype(jnp.float32)
    unit = (
        part_f
        * lax.rsqrt(jnp.mean(part_f * part_f, -1, keepdims=True) + 1e-05)
        / jnp.sqrt(jnp.float32(part.shape[-1]))
    )
    return jnp.exp(jnp.einsum("thd,hdf->thf", unit, feat_weights, precision=high)).astype(
        jnp.bfloat16
    )


def shards(signal, embed_weight, norm_gain, qkv_weight, conv_weight, feature_weight, out_weight):
    high = lax.Precision.HIGHEST
    rows = signal.shape[0]
    width = embed_weight.shape[1]
    normed = embed_norm(signal, embed_weight, norm_gain)
    local_cols = qkv_weight.shape[2]
    heads = feature_weight.shape[0]
    head_dim = feature_weight.shape[1]
    feat = feature_weight.shape[2]
    projected = jnp.dot(
        normed, qkv_weight.reshape(width, 3 * local_cols), preferred_element_type=jnp.float32
    ).astype(jnp.bfloat16)
    taps = conv_weight.shape[0]
    rim_rows = shifted(projected[rows - (taps - 1) :], "tm", 1)
    padded = jnp.concatenate([rim_rows, projected], 0)
    kernel = conv_weight.reshape(taps, 3 * local_cols)
    convolved = jnp.zeros((rows, 3 * local_cols), jnp.float32)
    for tap in range(taps):
        convolved = convolved + kernel[tap] * padded[tap : tap + rows].astype(jnp.float32)
    query = convolved[:, :local_cols].astype(jnp.bfloat16).reshape(rows, heads, head_dim)
    key = (
        convolved[:, local_cols : 2 * local_cols]
        .astype(jnp.bfloat16)
        .reshape(rows, heads, head_dim)
    )
    value = convolved[:, 2 * local_cols :].astype(jnp.bfloat16).reshape(rows, heads, head_dim)
    feat_weights = feature_weight.astype(jnp.float32)
    query_feat = feature_map(query, feat_weights)
    key_feat = feature_map(key, feat_weights)
    nblocks = rows // BLOCK
    query_blks = query_feat.reshape(nblocks, BLOCK, heads, feat)
    key_blks = key_feat.reshape(nblocks, BLOCK, heads, feat)
    value_blks = value.reshape(nblocks, BLOCK, heads, head_dim)
    block_kv = jnp.einsum(
        "nshf,nshd->nhfd", key_blks, value_blks, preferred_element_type=jnp.float32
    )
    block_tot = jnp.sum(key_blks, 1, dtype=jnp.float32)
    zero_state = jnp.zeros((heads, feat, head_dim), jnp.float32)
    zero_total = jnp.zeros((heads, feat), jnp.float32)
    state_in, total_in = prefix(
        (jnp.sum(block_kv, 0), jnp.sum(block_tot, 0)), "tm", add_pair, (zero_state, zero_total)
    )

    def advance(carry, items):
        state, total = carry
        query_blk, key_blk, value_blk, kv_blk, tot_blk = items
        numer, denom = local_block(query_blk, key_blk, value_blk)
        numer = numer + jnp.einsum(
            "thf,hfd->thd", query_blk, state, precision=high, preferred_element_type=jnp.float32
        )
        denom = denom + jnp.einsum(
            "thf,hf->th", query_blk, total, precision=high, preferred_element_type=jnp.float32
        )
        out = (numer / denom[:, :, None]).astype(jnp.bfloat16)
        return ((state + kv_blk, total + tot_blk), out)

    _, outs = lax.scan(
        advance, (state_in, total_in), (query_blks, key_blks, value_blks, block_kv, block_tot)
    )
    attended = outs.reshape(rows, heads * head_dim)
    result = lax.psum_scatter(
        jnp.dot(attended, out_weight, preferred_element_type=jnp.float32),
        "rep",
        scatter_dimension=0,
        tiled=True,
    )
    return result.astype(jnp.bfloat16)


def solution(mesh):
    in_specs = (
        P(("groups", "tm"), None),
        P("rep", None),
        P(),
        P(None, None, "rep"),
        P(None, None, "rep"),
        P("rep", None, None),
        P("rep", None),
    )
    out_specs = P(("groups", "tm", "rep"), None)
    return jax.shard_map(shards, mesh=mesh, in_specs=in_specs, out_specs=out_specs, check_vma=False)
```

profile of v0, /device:TPU:0, one launch (start us, length us, event | category | flops | bytes accessed | tf_op | source)
XLA Modules:
  0.0 160.5 jit_solution(5655309657368336891)
XLA Ops:
  7.3 2.3 %copy.30 = bf16[512,3,256]{0,2,1:T(8,128)(2,1)} copy(bf16[512,3,256]{2,0,1:T(8,128)(2,1)} %param.14) | data formatting | bytes 1572864 | tf_op args[3]
  9.6 11.1 %all-gather.5.cloned.1.call-done = bf16[1024,512]{1,0:T(8,128)(2,1)} async-done(((bf16[512,512]{1,0:T(8,128)(2,1)}), bf16[1024,512]{1,0:T(8,128)(2,1)}) %all-gather.5.cloned.1.call-update) | async-done | bytes 1048592 | tf_op jit(solution)/shard_map/all_gather | solution.py:51
  20.7 5.1 %multiply_reduce_fusion = (f32[2048]{0:T(1024)S(1)}, f32[2048,512]{0,1:T(8,128)S(1)}) fusion(bf16[2048,1024]{1,0:T(8,128)(2,1)} %param.11, bf16[1024,512]{1,0:T(8,128)(2,1)} %all-gather.5.cloned.1.call-done), kind=kOutput, calls=%fused_computation.39 | convolution fusion | flops 2149578752 | bytes 9445376 | tf_op jit(solution)/shard_map/dot_general | solution.py:49
  25.8 2.1 %convolution_convert_fusion = bf16[2048,768]{1,0:T(8,128)(2,1)S(1)} fusion(bf16[512,768]{0,1:T(8,128)(2,1)S(1)} %bitcast.132, f32[2048,512]{0,1:T(8,128)S(1)} %get-tuple-element.162, f32[512]{0:T(512)S(1)} %copy-done.6, f32[2048]{0:T(1024)S(1)} %add_rsqrt_fusion.2), kind=kOutput, calls=%fused_computation.40 | convolution fusion | flops 1615331328 | bytes 8136704 | tf_op jit(solution)/shard_map/dot_general | solution.py:81
  27.9 3.6 %collective-permute-start = (bf16[3,768]{1,0:T(4,128)(2,1)S(1)}, bf16[3,768]{1,0:T(4,128)(2,1)S(1)}, u32[]{:S(2)}, u32[]{:S(2)}) collective-permute-start(bf16[3,768]{1,0:T(4,128)(2,1)S(1)} %slice.51), channel_id=1, source_target_pairs={{0,2},{2,4},{4,6},{6,8},{8,10},{10,12},{12,14},{1,3},{3,5},{5,7},{... | collective-permute-start | bytes 13832 | tf_op jit(solution)/shard_map/ppermute | solution.py:12
  31.7 1.2 collective-permute-done
  32.9 3.2 %add_convert_fusion = bf16[2048,768]{1,0:T(8,128)(2,1)S(1)} fusion(bf16[2048,768]{1,0:T(8,128)(2,1)S(1)} %convolution_convert_fusion, bf16[3,768]{1,0:T(4,128)(2,1)S(1)} %collective-permute-done, f32[768]{0:T(1024)S(1)} %mul.95, f32[768]{0:T(1024)S(1)} %mul.92, f32[768]{0:T(1024)S(1)} %mul.89, f32[768]{0:T(1024)S(1)} %mul.81), kind=kLoop, calls=%fused_computation.32 | loop fusion | flops 33030144 | bytes 6308352 | tf_op jit(solution)/shard_map/convert.7
  36.1 2.4 %slice_convert_fusion = (f32[2048,256]{1,0:T(8,128)}, bf16[2048,256]{1,0:T(8,128)(2,1)S(1)}, f32[2048,256]{1,0:T(8,128)}) fusion(bf16[2048,768]{1,0:T(8,128)(2,1)S(1)} %add_convert_fusion), kind=kLoop, calls=%fused_computation.53 | loop fusion | flops 1048576 | bytes 8388608 | tf_op jit(solution)/shard_map/convert_element_type | solution.py:61
  38.5 1.9 %copy.31 = f32[2048,256]{0,1:T(8,128)S(1)} copy(f32[2048,256]{1,0:T(8,128)} %get-tuple-element.160) | data formatting | bytes 4194304 | tf_op jit(solution)/shard_map/convert_element_type | solution.py:61
  41.3 1.9 %reshape.92 = bf16[4,512,4,64]{3,2,1,0:T(4,128)(2,1)} reshape(bf16[2048,256]{1,0:T(8,128)(2,1)S(1)} %get-tuple-element.159) | data formatting | bytes 2097152 | tf_op jit(solution)/shard_map/reshape;reshape | solution.py:104
  43.1 2.9 %copy.34 = bf16[4,512,4,64]{1,3,2,0:T(8,128)(2,1)S(1)} copy(bf16[4,512,4,64]{3,2,1,0:T(4,128)(2,1)} %reshape.92) | data formatting | bytes 2097152 | tf_op jit(solution)/shard_map/reshape;reshape | solution.py:104
  46.1 3.8 %bitcast_reduce_fusion = (bf16[4,128]{1,0:T(4,128)(2,1)S(1)}, bf16[4,2048,128]{2,1,0:T(8,128)(2,1)S(1)}) fusion(bf16[4,64,128]{2,1,0:T(8,128)(2,1)S(1)} %copy-done.3, f32[2048,4,64]{0,2,1:T(8,128)S(1)} %bitcast.127, f32[2048,4]{0,1:T(4,128)S(1)} %copy-done.4), kind=kOutput, calls=%fused_computation.44 | convolution fusion | flops 808451584 | bytes 4293632 | tf_op jit(solution)/shard_map/thd,hdf->thf/dot_general | solution.py:67
  50.2 1.5 copy.33
  51.7 1.3 fusion.37
  53.0 33.1 %all-gather = bf16[32,128,64]{1,2,0:T(8,128)(2,1)S(1)} all-gather(bf16[4,128,64]{1,2,0:T(8,128)(2,1)S(1)} %get-tuple-element.163), channel_id=2, replica_groups=mesh['groups'=2,'tm'=8,'rep'=2] {'tm'}, dimensions={0}, use_global_device_ids=true | all-gather | bytes 589824 | tf_op jit(solution)/shard_map/all_gather | solution.py:18
  86.1 19.4 %all-gather.2 = bf16[8,4,128]{2,1,0:T(4,128)(2,1)S(1)} all-gather(bf16[1,4,128]{2,1,0:T(4,128)(2,1)S(1)} %bitcast.135), channel_id=3, replica_groups=mesh['groups'=2,'tm'=8,'rep'=2] {'tm'}, dimensions={0}, use_global_device_ids=true | all-gather | bytes 9216 | tf_op jit(solution)/shard_map/all_gather | solution.py:18
  105.9 1.9 %copy.36 = f32[2048,256]{0,1:T(8,128)S(1)} copy(f32[2048,256]{1,0:T(8,128)} %get-tuple-element.158) | data formatting | bytes 4194304 | tf_op jit(solution)/shard_map/convert_element_type | solution.py:61
  108.1 1.0 copy-done.1
  109.1 5.1 %exponential_convert_fusion = bf16[4,2048,128]{2,1,0:T(8,128)(2,1)S(1)} fusion(bf16[4,64,128]{2,1,0:T(8,128)(2,1)} %param.16, f32[2048,4,64]{0,2,1:T(8,128)} %bitcast.128, f32[2048,4]{0,1:T(4,128)S(1)} %add_rsqrt_fusion), kind=kOutput, calls=%fused_computation.35 | convolution fusion | flops 807403520 | bytes 4292608 | tf_op jit(solution)/shard_map/thd,hdf->thf/dot_general | solution.py:67
  114.2 21.3 %while.27 = (s32[]{:T(128)}, f32[4,128,64]{1,2,0:T(8,128)S(1)}, f32[4,128]{1,0:T(4,128)S(1)}, bf16[4,512,4,64]{1,3,2,0:T(8,128)(2,1)}, f32[4,4,128,64]{2,3,1,0:T...) while((s32[]{:T(128)}, f32[4,128,64]{1,2,0:T(8,128)S(1)}, ...), condition=%wide.region_10.11_spmd, body=%wide.region_8.10_spmd.sunk | while | flops 612008448 | bytes 8976501 | solution.py:128
  114.3 1.9 %convert_reduce_fusion.3 = (f32[4,512]{1,0:T(4,128)S(1)}, bf16[4,512,512]{1,2,0:T(8,128)(2,1)S(1)}) fusion(bf16[4,512,4,128]{3,1,2,0:T(8,128)(2,1)} %get-tuple-element.319, s32[]{:T(128)} %get-tuple-element.301, bf16[4,512,4,128]{3,1,0,2:T(8,128)(2,1)S(1)} %get-tuple-element.318, pred[512,512]{0,1:T(8,128)(4,1)S(1)} %iota_compare_fusion.2), kind=kOutput, calls=%fused_computation.3.clone.1 | convolution fusion | flops 272627712 | bytes 3417088 | tf_op jit(solution)/shard_map/while/body/eval_jaxpr/thf,shf->hts/dot_general | solution.py:36
  117.4 1.2 fusion.67
  119.6 1.9 %convert_reduce_fusion.3 = (f32[4,512]{1,0:T(4,128)S(1)}, bf16[4,512,512]{1,2,0:T(8,128)(2,1)S(1)}) fusion(bf16[4,512,4,128]{3,1,2,0:T(8,128)(2,1)} %get-tuple-element.319, s32[]{:T(128)} %get-tuple-element.301, bf16[4,512,4,128]{3,1,0,2:T(8,128)(2,1)S(1)} %get-tuple-element.318, pred[512,512]{0,1:T(8,128)(4,1)S(1)} %iota_compare_fusion.2), kind=kOutput, calls=%fused_computation.3.clone.1 | convolution fusion | flops 272627712 | bytes 3417088 | tf_op jit(solution)/shard_map/while/body/eval_jaxpr/thf,shf->hts/dot_general | solution.py:36
  122.7 1.2 fusion.67
  125.0 1.9 %convert_reduce_fusion.3 = (f32[4,512]{1,0:T(4,128)S(1)}, bf16[4,512,512]{1,2,0:T(8,128)(2,1)S(1)}) fusion(bf16[4,512,4,128]{3,1,2,0:T(8,128)(2,1)} %get-tuple-element.319, s32[]{:T(128)} %get-tuple-element.301, bf16[4,512,4,128]{3,1,0,2:T(8,128)(2,1)S(1)} %get-tuple-element.318, pred[512,512]{0,1:T(8,128)(4,1)S(1)} %iota_compare_fusion.2), kind=kOutput, calls=%fused_computation.3.clone.1 | convolution fusion | flops 272627712 | bytes 3417088 | tf_op jit(solution)/shard_map/while/body/eval_jaxpr/thf,shf->hts/dot_general | solution.py:36
  128.1 1.2 fusion.67
  130.3 1.9 %convert_reduce_fusion.3 = (f32[4,512]{1,0:T(4,128)S(1)}, bf16[4,512,512]{1,2,0:T(8,128)(2,1)S(1)}) fusion(bf16[4,512,4,128]{3,1,2,0:T(8,128)(2,1)} %get-tuple-element.319, s32[]{:T(128)} %get-tuple-element.301, bf16[4,512,4,128]{3,1,0,2:T(8,128)(2,1)S(1)} %get-tuple-element.318, pred[512,512]{0,1:T(8,128)(4,1)S(1)} %iota_compare_fusion.2), kind=kOutput, calls=%fused_computation.3.clone.1 | convolution fusion | flops 272627712 | bytes 3417088 | tf_op jit(solution)/shard_map/while/body/eval_jaxpr/thf,shf->hts/dot_general | solution.py:36
  133.4 1.2 fusion.67
  135.5 2.0 %copy.42 = bf16[4,512,4,64]{1,0,3,2:T(4,128)(2,1)S(1)} copy(bf16[4,512,4,64]{1,3,2,0:T(8,128)(2,1)} %get-tuple-element.88) | data formatting | bytes 2097152 | tf_op jit(solution)/shard_map/while | solution.py:128
  137.9 2.7 %fusion.38 = f32[2048,512]{1,0:T(8,128)} fusion(bf16[2048,256]{0,1:T(8,128)(2,1)S(1)} %bitcast.129, bf16[256,512]{1,0:T(8,128)(2,1)S(1)} %copy-done), kind=kOutput, calls=%fused_computation.71 | convolution fusion | flops 536870912 | bytes 5505024 | tf_op jit(solution)/shard_map/dot_general | solution.py:133
  140.6 10.4 %reduce-scatter.2.cloned.1.call-done = f32[1024,512]{1,0:T(8,128)} async-done(((f32[2048,512]{1,0:T(8,128)}), f32[1024,512]{1,0:T(8,128)}) %reduce-scatter.2.cloned.1.call-update) | async-done | bytes 2097168 | tf_op jit(solution)/shard_map/reduce_scatter | solution.py:132
  151.0 2.7 %convert_element_type.104 = bf16[1024,512]{1,0:T(8,128)(2,1)} convert(f32[1024,512]{1,0:T(8,128)} %reduce-scatter.2.cloned.1.call-done) | non-fusion elementwise | flops 524288 | bytes 3145728 | tf_op jit(solution)/shard_map/convert_element_type | solution.py:138
  (63 shorter events, 11.8 us)
Async XLA Ops:
  6.5 131.3 %copy-start = (bf16[256,512]{1,0:T(8,128)(2,1)S(1)}, bf16[256,512]{1,0:T(8,128)(2,1)}, u32[]{:S(2)}) copy-start(bf16[256,512]{1,0:T(8,128)(2,1)} %param.17) | copy-start | bytes 786436
  6.5 14.1 %all-gather.5.cloned.1.call-start = ((), (), s32[]{:S(2)}) async-start(), calls=%async_computation.1 | async-start | bytes 1572864 | tf_op jit(solution)/shard_map/all_gather | solution.py:51
  7.3 143.7 %reduce-scatter.2.cloned.1.call-start = ((), (), s32[]{:S(2)}) async-start(), calls=%async_computation.2 | async-start | bytes 6291456 | tf_op jit(solution)/shard_map/reduce_scatter | solution.py:132
  9.6 16.2 %copy-start.6 = (f32[512]{0:T(512)S(1)}, f32[512]{0:T(512)}, u32[]{:S(2)}) copy-start(f32[512]{0:T(512)} %param.13) | copy-start | bytes 6148
  20.7 5.1 %copy-start.2 = (bf16[512,3,256]{0,2,1:T(8,128)(2,1)S(1)}, bf16[512,3,256]{0,2,1:T(8,128)(2,1)}, u32[]{:S(2)}) copy-start(bf16[512,3,256]{0,2,1:T(8,128)(2,1)} %copy.30) | copy-start | bytes 2359300
  25.8 5.8 %copy-start.5 = (f32[4,3,256]{2,0,1:T(4,128)S(1)}, f32[4,3,256]{2,0,1:T(4,128)}, u32[]{:S(2)}) copy-start(f32[4,3,256]{2,0,1:T(4,128)} %param.15) | copy-start | bytes 36868
  27.9 5.0 %collective-permute-start = (bf16[3,768]{1,0:T(4,128)(2,1)S(1)}, bf16[3,768]{1,0:T(4,128)(2,1)S(1)}, u32[]{:S(2)}, u32[]{:S(2)}) collective-permute-start(bf16[3,768]{1,0:T(4,128)(2,1)S(1)} %slice.51), channel_id=1, source_target_pairs={{0,2},{2,4},{4,6},{6,8},{8,10},{10,12},{12,14},{1,3},{3,5},{5,7},{... | collective-permute-start | bytes 13832 | tf_op jit(solution)/shard_map/ppermute | solution.py:12
  43.1 3.0 %copy-start.3 = (bf16[4,64,128]{2,1,0:T(8,128)(2,1)S(1)}, bf16[4,64,128]{2,1,0:T(8,128)(2,1)}, u32[]{:S(2)}) copy-start(bf16[4,64,128]{2,1,0:T(8,128)(2,1)} %param.16) | copy-start | bytes 196612
  43.1 3.0 %copy-start.4 = (f32[2048,4]{0,1:T(4,128)S(1)}, f32[2048,4]{0,1:T(4,128)}, u32[]{:S(2)}) copy-start(f32[2048,4]{0,1:T(4,128)} %add_rsqrt_fusion.1) | copy-start | bytes 98308
  107.8 1.3 copy-start.1
Sparse Core Ops, SparseCore 0:
  8.9 11.7 all-gather.4
  140.7 10.2 reduce-scatter.1
where the time goes:
time: 161 us
  blocking collectives  52.6 us (33%)
  matrix products  37 us (23%)
  waiting for transfers between devices  23.4 us (15%)
  local copies, waits for them, and re-layouts  16 us (10%)
  other arithmetic  13.8 us (9%)
  between operations  13.7 us (9%)
  starting transfers between devices  3.68 us (2%)
    all_gather x2, blocking collectives, prefix(): lax.all_gather(a.astype(kind), axis)  52.6 us
    all_gather x1, waiting for transfers between devices, embed_norm(): lax.all_gather(embed_weight, 'rep', axis=0, tiled=True)  11.1 us
    reduce_scatter x1, waiting for transfers between devices, shards(): lax.psum_scatter(jnp.dot(attended, out_weight, preferred_element_type=jnp...  10.4 us
    dot_general x2, matrix products, feature_map(): jnp.einsum('thd,hdf->thf', unit, feat_weights, precision=high)  8.83 us
    dot_general x4, matrix products, local_block(): jnp.einsum('thf,shf->hts', query_blk, key_blk, preferred_element_type=jnp...  7.51 us
    dot_general x1, matrix products, embed_norm(): jnp.dot(sig_rows, lax.all_gather(embed_weight, 'rep', axis=0, tiled=True)...  5.11 us
    another operation x2, local copies, waits for them, and re-layouts, shards(): value_blks = value.reshape(nblocks, BLOCK, heads, head_dim)  4.8 us
    dot_general x4, matrix products, local_block(): jnp.einsum('hts,shd->thd', weights, value_blk, preferred_element_type=jnp...  4.7 us
  transfers between devices with their start and end apart: 3, of which 3 were waited for; matrix products, arithmetic and copies ran while one was open for 1% of the time, Pallas kernels for 0%

commit v1 on v0

v1 whole, which is shorter than its diff:
```python
import functools
import math

import jax
import jax.numpy as jnp
from jax import lax
from jax.experimental import pallas as pl
from jax.experimental.pallas import tpu as pltpu
from jax.sharding import PartitionSpec as P

EPS = 1e-05
LOG2E = math.log2(math.e)
SUB = 256
STEP = 512
RIM = 16
PAD = 8
LANES = 128
F32 = jnp.float32
BF16 = jnp.bfloat16
NT = (((1,), (1,)), ((), ()))
TN = (((0,), (0,)), ((), ()))


def dot(a, b, dims=(((1,), (0,)), ((), ()))):
    return lax.dot_general(a, b, dims, preferred_element_type=F32)


def params(mib=40):
    return pltpu.CompilerParams(dimension_semantics=("arbitrary",), vmem_limit_bytes=mib << 20)


def whole(shape):
    zeros = (0,) * len(shape)
    return pl.BlockSpec(shape, lambda *_: zeros)


def normalize(sig_a, sig_b, ew_a, ew_b, gain):
    emb = dot(sig_a, ew_a) + dot(sig_b, ew_b)
    mean = jnp.mean(emb * emb, -1, keepdims=True)
    return (emb * lax.rsqrt(mean + EPS) * gain).astype(BF16)


def convolve(pad_ref, proj, taps_ref, parts):
    rows = proj.shape[0]
    taps = taps_ref.shape[0]
    tiles = proj.shape[1] // LANES
    per = tiles // len(parts)
    out = []
    for c in range(tiles):
        pad_ref[c, PAD : PAD + rows, :] = proj[:, c * LANES : (c + 1) * LANES]
    for c in range(tiles):
        at = (c % per) * LANES
        total = None
        for tap in range(taps):
            weight = taps_ref[tap, parts[c // per] : parts[c // per] + 1, at : at + LANES]
            term = weight * pad_ref[c, PAD - taps + 1 + tap : PAD - taps + 1 + tap + rows, :]
            total = term if total is None else total + term
        out.append(total.astype(BF16))
    for c in range(tiles):
        pad_ref[c, 0:PAD, :] = pad_ref[c, rows : rows + PAD, :]
    return out


def start_rim(pad_ref, proj, keep):
    rows = proj.shape[0]
    for c in range(pad_ref.shape[0]):
        pad_ref[c, 0:PAD, :] = proj[rows - PAD :, c * LANES : (c + 1) * LANES] * keep


def spread_features(feat_ref, diag_ref, ones_ref):
    heads, head_dim, feat = feat_ref.shape
    diag_ref[...] = jnp.zeros_like(diag_ref)
    ones_ref[...] = jnp.zeros_like(ones_ref)
    for h in range(heads):
        at = (slice(h * head_dim, (h + 1) * head_dim), slice(h * feat, (h + 1) * feat))
        diag_ref[at] = feat_ref[h]
        ones_ref[at] = jnp.ones((head_dim, feat), BF16)


def features(part, diag_ref, ones_ref, head_dim):
    part_f = part.astype(F32)
    logits = dot(part, diag_ref[...])
    squares = dot((part_f * part_f).astype(BF16), ones_ref[...])
    scale = lax.rsqrt(squares * (1.0 / head_dim) + EPS) * (LOG2E / math.sqrt(head_dim))
    return jnp.exp2(logits * scale).astype(BF16)


def key_kernel(
    sc, sig_a, sig_b, rim_a, rim_b, ew_a, ew_b, gain, weight, taps, feat_w,
    normed_ref, nrim_ref, kf_ref, v_ref, before_ref, total_ref,
    pad, diag, ones, acc,
):
    step = pl.program_id(0)
    cols = v_ref.shape[1]
    heads, head_dim, feat = feat_w.shape

    @pl.when(step == 0)
    def _():
        spread_features(feat_w, diag, ones)
        nrim = normalize(rim_a[...], rim_b[...], ew_a[...], ew_b[...], gain[...])
        nrim_ref[...] = nrim
        keep = (sc[1] > 0).astype(F32)
        proj = dot(nrim, weight[:, cols:]).astype(BF16).astype(F32)
        start_rim(pad, proj, keep)
        acc[...] = jnp.zeros_like(acc)

    normed = normalize(sig_a[...], sig_b[...], ew_a[...], ew_b[...], gain[...])
    normed_ref[...] = normed
    proj = dot(normed, weight[:, cols:]).astype(BF16).astype(F32)
    tiles = convolve(pad, proj, taps, (1, 2))
    half = len(tiles) // 2
    key = jnp.concatenate(tiles[:half], 1)
    value = jnp.concatenate(tiles[half:], 1)
    v_ref[...] = value
    key_feat = features(key, diag, ones, head_dim)
    kf_ref[...] = key_feat
    for b in range(key.shape[0] // SUB):
        rows = slice(b * SUB, (b + 1) * SUB)
        before_ref[b] = acc[...]
        for pair in range(heads // 2):
            vp = value[rows, pair * 2 * head_dim : (pair + 1) * 2 * head_dim]
            kp = key_feat[rows, pair * 2 * feat : (pair + 1) * 2 * feat]
            both = dot(vp, kp, TN)
            for side in range(2):
                h = pair * 2 + side
                acc[h * head_dim : (h + 1) * head_dim, :] += both[
                    side * head_dim : (side + 1) * head_dim, side * feat : (side + 1) * feat
                ]
        sums = jnp.sum(key_feat[rows].astype(F32), 0, keepdims=True)
        for h in range(heads):
            at = heads * head_dim + h
            acc[at : at + 1, :] += sums[:, h * feat : (h + 1) * feat]

    @pl.when(step == pl.num_programs(0) - 1)
    def _():
        total_ref[...] = acc[...].astype(BF16)


def query_kernel(sc, normed, nrim, weight, taps, feat_w, qf_ref, pad, diag, ones):
    cols = weight.shape[1] // 3

    @pl.when(pl.program_id(0) == 0)
    def _():
        spread_features(feat_w, diag, ones)
        keep = (sc[1] > 0).astype(F32)
        start_rim(pad, dot(nrim[...], weight[:, :cols]).astype(BF16).astype(F32), keep)

    proj = dot(normed[...], weight[:, :cols]).astype(BF16).astype(F32)
    query = jnp.concatenate(convolve(pad, proj, taps, (0,)), 1)
    qf_ref[...] = features(query, diag, ones, feat_w.shape[1])


def local_kernel(qf, kf, v, out_ref, *, heads):
    feat = qf.shape[1] // heads
    width = v.shape[1] // heads
    row = lax.broadcasted_iota(jnp.int32, (SUB, SUB), 0)
    col = lax.broadcasted_iota(jnp.int32, (SUB, SUB), 1)
    causal = row >= col
    left = lax.broadcasted_iota(jnp.int32, (SUB, 2 * width), 1) < width
    one, zero = jnp.ones((SUB, 2 * width), BF16), jnp.zeros((SUB, 2 * width), BF16)
    for b in range(qf.shape[0] // SUB):
        rows = slice(b * SUB, (b + 1) * SUB)
        for pair in range(heads // 2):
            vp = v[rows, pair * 2 * width : (pair + 1) * 2 * width]
            total = None
            for side in range(2):
                at = slice((pair * 2 + side) * feat, (pair * 2 + side + 1) * feat)
                mine = left if side == 0 else ~left
                scores = dot(qf[rows, at], kf[rows, at], NT)
                weights = jnp.where(causal, scores, 0.0).astype(BF16)
                rhs = jnp.concatenate([jnp.where(mine, vp, zero), jnp.where(mine, one, zero)], 1)
                term = dot(weights, rhs)
                total = term if total is None else total + term
            out_ref[rows, pair * 4 * width : (pair + 1) * 4 * width] = total


def combine_kernel(sc, qf, local, before, near, far, out_ref, *, heads):
    feat = qf.shape[1] // heads
    width = out_ref.shape[1] // heads
    state_in = near[...] + far[...].astype(F32) * (sc[2] > 0).astype(F32)
    zero = jnp.zeros((width, feat), BF16)
    for b in range(qf.shape[0] // SUB):
        rows = slice(b * SUB, (b + 1) * SUB)
        state = (before[b] + state_in).astype(BF16)
        for pair in range(heads // 2):
            h = pair * 2
            s0, s1 = (state[(h + k) * width : (h + k + 1) * width] for k in range(2))
            t0, t1 = (
                jnp.broadcast_to(
                    state[heads * width + h + k : heads * width + h + k + 1], (width, feat)
                )
                for k in range(2)
            )
            rhs = jnp.concatenate(
                [
                    jnp.concatenate([s0, zero], 1),
                    jnp.concatenate([zero, s1], 1),
                    jnp.concatenate([t0, zero], 1),
                    jnp.concatenate([zero, t1], 1),
                ],
                0,
            )
            both = local[rows, pair * 4 * width : (pair + 1) * 4 * width] + dot(
                qf[rows, pair * 2 * feat : (pair + 1) * 2 * feat], rhs, NT
            )
            out_ref[rows, pair * 2 * width : (pair + 1) * 2 * width] = (
                both[:, : 2 * width] / both[:, 2 * width :]
            ).astype(BF16)


def output_kernel(mine, other, w_mine, w_other, out_ref):
    out_ref[...] = (dot(mine[...], w_mine[...]) + dot(other[...], w_other[...])).astype(BF16)


def swap(array, axis, by):
    devices = lax.axis_size(axis)
    return lax.ppermute(array, axis, [(i, i ^ by) for i in range(devices)])


def prefix(total, axis):
    devices = lax.axis_size(axis)
    place = lax.axis_index(axis)
    near = jnp.zeros(total.shape, F32)
    group = total.astype(F32)
    span = 1
    while True:
        radix = min(4, devices // span)
        sent = group.astype(BF16)
        got = [swap(sent, axis, k * span) for k in range(1, radix)]
        if span * radix >= devices and radix == 2:
            return near, got[0], (place & span) > 0
        digit = (place // span) % radix
        for k, g in enumerate(got, 1):
            g = g.astype(F32)
            group = group + g
            near = near + jnp.where((digit ^ k) < digit, g, 0.0)
        span *= radix
        if span >= devices:
            return near, jnp.zeros_like(total), place < 0


def shards(signal, embed_weight, norm_gain, qkv_weight, conv_weight, feature_weight, out_weight):
    rows, depth = signal.shape
    half_depth, width = embed_weight.shape
    cols = qkv_weight.shape[2]
    heads, head_dim, feat = feature_weight.shape
    feats = heads * feat
    states = heads * head_dim + 16
    taps = conv_weight.shape[0]
    place, rep = lax.axis_index("tm"), lax.axis_index("rep")
    devices = lax.axis_size("tm")

    ew_other = swap(embed_weight, "rep", 1)
    rim = lax.ppermute(signal[rows - RIM :], "tm", [(i, (i + 1) % devices) for i in range(devices)])
    ow_other = swap(out_weight, "rep", 1)
    weight = qkv_weight.reshape(width, 3 * cols)
    sc = jnp.stack([rep, place]).astype(jnp.int32)
    gain = norm_gain.reshape(1, width)
    steps = rows // STEP
    scratch = [
        pltpu.VMEM((2 * cols // LANES, PAD + STEP, LANES), F32),
        pltpu.VMEM((cols, feats), BF16),
        pltpu.VMEM((cols, feats), BF16),
        pltpu.VMEM((states, feat), F32),
    ]
    normed, nrim, kf, value, before, total = pl.pallas_call(
        key_kernel,
        grid_spec=pltpu.PrefetchScalarGridSpec(
            num_scalar_prefetch=1,
            grid=(steps,),
            in_specs=[
                pl.BlockSpec((STEP, half_depth), lambda i, s: (i, s[0])),
                pl.BlockSpec((STEP, half_depth), lambda i, s: (i, 1 - s[0])),
                pl.BlockSpec((RIM, half_depth), lambda i, s: (0, s[0])),
                pl.BlockSpec((RIM, half_depth), lambda i, s: (0, 1 - s[0])),
                whole((half_depth, width)),
                whole((half_depth, width)),
                whole((1, width)),
                whole((width, 3 * cols)),
                whole(conv_weight.shape),
                whole(feature_weight.shape),
            ],
            out_specs=[
                pl.BlockSpec((STEP, width), lambda i, s: (i, 0)),
                whole((RIM, width)),
                pl.BlockSpec((STEP, feats), lambda i, s: (i, 0)),
                pl.BlockSpec((STEP, cols), lambda i, s: (i, 0)),
                pl.BlockSpec((STEP // SUB, states, feat), lambda i, s: (i, 0, 0)),
                whole((states, feat)),
            ],
            scratch_shapes=scratch,
        ),
        out_shape=[
            jax.ShapeDtypeStruct((rows, width), BF16),
            jax.ShapeDtypeStruct((RIM, width), BF16),
            jax.ShapeDtypeStruct((rows, feats), BF16),
            jax.ShapeDtypeStruct((rows, cols), BF16),
            jax.ShapeDtypeStruct((rows // SUB, states, feat), F32),
            jax.ShapeDtypeStruct((states, feat), BF16),
        ],
        compiler_params=params(),
        name="keys",
    )(sc, signal, signal, rim, rim, embed_weight, ew_other, gain, weight, conv_weight, feature_weight)

    near, far, flag = prefix(total, "tm")

    query_feat = pl.pallas_call(
        query_kernel,
        grid_spec=pltpu.PrefetchScalarGridSpec(
            num_scalar_prefetch=1,
            grid=(steps,),
            in_specs=[
                pl.BlockSpec((STEP, width), lambda i, s: (i, 0)),
                whole((RIM, width)),
                whole((width, 3 * cols)),
                whole(conv_weight.shape),
                whole(feature_weight.shape),
            ],
            out_specs=pl.BlockSpec((STEP, feats), lambda i, s: (i, 0)),
            scratch_shapes=[
                pltpu.VMEM((cols // LANES, PAD + STEP, LANES), F32),
                pltpu.VMEM((cols, feats), BF16),
                pltpu.VMEM((cols, feats), BF16),
            ],
        ),
        out_shape=jax.ShapeDtypeStruct((rows, feats), BF16),
        compiler_params=params(),
        cost_estimate=pl.CostEstimate(flops=2 * rows * width * cols * 4, bytes_accessed=8 << 20, transcendentals=0),
        name="queries",
    )(sc, normed, nrim, weight, conv_weight, feature_weight)

    local = pl.pallas_call(
        functools.partial(local_kernel, heads=heads),
        grid=(steps,),
        in_specs=[
            pl.BlockSpec((STEP, feats), lambda i: (i, 0)),
            pl.BlockSpec((STEP, feats), lambda i: (i, 0)),
            pl.BlockSpec((STEP, cols), lambda i: (i, 0)),
        ],
        out_specs=pl.BlockSpec((STEP, 2 * cols), lambda i: (i, 0)),
        out_shape=jax.ShapeDtypeStruct((rows, 2 * cols), F32),
        compiler_params=params(),
        cost_estimate=pl.CostEstimate(flops=2 * rows * SUB * 1024 * 4, bytes_accessed=9 << 20, transcendentals=0),
        name="local",
    )(query_feat, kf, value)

    half = rows // 2
    half_steps = half // STEP

    def combine(which):
        scal = jnp.stack([which * half_steps, which, flag]).astype(jnp.int32)
        return pl.pallas_call(
            functools.partial(combine_kernel, heads=heads),
            grid_spec=pltpu.PrefetchScalarGridSpec(
                num_scalar_prefetch=1,
                grid=(half_steps,),
                in_specs=[
                    pl.BlockSpec((STEP, feats), lambda i, s: (i + s[0], 0)),
                    pl.BlockSpec((STEP, 2 * cols), lambda i, s: (i + s[0], 0)),
                    pl.BlockSpec((STEP // SUB, states, feat), lambda i, s: (i + s[0], 0, 0)),
                    whole((states, feat)),
                    whole((states, feat)),
                ],
                out_specs=pl.BlockSpec((STEP, cols), lambda i, s: (i, 0)),
            ),
            out_shape=jax.ShapeDtypeStruct((half, cols), BF16),
            compiler_params=params(),
            cost_estimate=pl.CostEstimate(flops=2 * half * 256 * 512, bytes_accessed=4 << 20, transcendentals=0),
            name="combine",
        )(scal, query_feat, local, before, near, far)

    for_other = swap(combine(1 - rep), "rep", 1)
    mine = combine(rep)
    return pl.pallas_call(
        output_kernel,
        grid=(half_steps,),
        in_specs=[
            pl.BlockSpec((STEP, cols), lambda i: (i, 0)),
            pl.BlockSpec((STEP, cols), lambda i: (i, 0)),
            whole(out_weight.shape),
            whole(out_weight.shape),
        ],
        out_specs=pl.BlockSpec((STEP, width), lambda i: (i, 0)),
        out_shape=jax.ShapeDtypeStruct((half, width), BF16),
        compiler_params=params(),
        name="output",
    )(mine, for_other, out_weight, ow_other)


def solution(mesh):
    in_specs = (
        P(("groups", "tm"), None),
        P("rep", None),
        P(),
        P(None, None, "rep"),
        P(None, None, "rep"),
        P("rep", None, None),
        P("rep", None),
    )
    out_specs = P(("groups", "tm", "rep"), None)
    return jax.shard_map(shards, mesh=mesh, in_specs=in_specs, out_specs=out_specs, check_vma=False)
```

time: 161 us -> 44.5 us (0.28)
  blocking collectives: 52.6 us -> 0 us
  matrix products: 37 us -> 0 us
  Pallas kernels: 0 us -> 23.5 us
  waiting for transfers between devices: 23.4 us -> 4.07 us
  between operations: 13.7 us -> 0.18 us
  other arithmetic: 13.8 us -> 0.3 us
  local copies, waits for them, and re-layouts: 16 us -> 7.98 us
  starting transfers between devices: 3.68 us -> 8.12 us
    all_gather x2 -> x0, blocking collectives: 52.6 us -> none  [prefix(): lax.all_gather(a.astype(kind), axis)]
    dot_general x22 -> x0, matrix products: 37 us -> none  [the longest x2 8.83 us: feature_map(): jnp.einsum('thd,hdf->thf', unit, feat_weights, precision=high)]
    pallas_call x0 -> x6, Pallas kernels: none -> 23.5 us  [the longest x1 9.35 us: shards(): pl.pallas_call(key_kernel, grid_spec=pltpu.PrefetchScalarGridSpec(num_sca...]
    all_gather x1 -> x0, waiting for transfers between devices: 11.1 us -> none  [embed_norm(): lax.all_gather(embed_weight, 'rep', axis=0, tiled=True)]
    reduce_scatter x1 -> x0, waiting for transfers between devices: 10.4 us -> none  [shards(): lax.psum_scatter(jnp.dot(attended, out_weight, preferred_element_type=jnp...]
    convert_element_type x2 -> x1, other arithmetic: 5.06 us -> 0.07 us  [prefix(): sent = group.astype(BF16)]
    another operation x2 -> x0, local copies, waits for them, and re-layouts: 4.8 us -> none  [shards(): value_blks = value.reshape(nblocks, BLOCK, heads, head_dim)]
    ppermute x1 -> x8, starting transfers between devices: 3.64 us -> 8.12 us  [the longest x7 5.53 us: swap(): return lax.ppermute(array, axis, [(i, i ^ by) for i in range(devices)])]
  transfers between devices with their start and end apart: 3 -> 8, of which waited for: 3 -> 2; matrix products, arithmetic and copies ran while one was open for 1% -> 6% of each run, Pallas kernels for 0% -> 21%
where the time goes in v1:
time: 44.5 us; the launch traced here: 44.1 us
  Pallas kernels  23.5 us (53%)
  starting transfers between devices  8.12 us (18%)
  local copies, waits for them, and re-layouts  7.98 us (18%)
  waiting for transfers between devices  4.07 us (9%)
    pallas_call x1, Pallas kernels, shards(): pl.pallas_call(key_kernel, grid_spec=pltpu.PrefetchScalarGridSpec(num_sca...  9.35 us
    unnamed x20, local copies, waits for them, and re-layouts  6.95 us
    ppermute x7, starting transfers between devices, swap(): return lax.ppermute(array, axis, [(i, i ^ by) for i in range(devices)])  5.53 us
    pallas_call x1, Pallas kernels, shards(): pl.pallas_call(query_kernel, grid_spec=pltpu.PrefetchScalarGridSpec(num_s...  4.5 us
    pallas_call x1, Pallas kernels, shards(): pl.pallas_call(functools.partial(local_kernel, heads=heads), grid=(steps,...  3.57 us
    pallas_call x2, Pallas kernels, combine(): pl.pallas_call(functools.partial(combine_kernel, heads=heads), grid_spec=...  3.26 us
    ppermute x1, waiting for transfers between devices, shards(): lax.ppermute(signal[rows - RIM:], 'tm', [(i, (i + 1) % devices) for i in...  3.13 us
    pallas_call x1, Pallas kernels, shards(): pl.pallas_call(output_kernel, grid=(half_steps,), in_specs=[pl.BlockSpec(...  2.82 us
  transfers between devices with their start and end apart: 8, of which 2 were waited for; matrix products, arithmetic and copies ran while one was open for 6% of the time, Pallas kernels for 21%

profile of v1, /device:TPU:0, one launch (start us, length us, event | category | flops | bytes accessed | tf_op | source)
XLA Modules:
  0.0 44.1 jit_solution(10872516742871716912)
XLA Ops:
  0.0 0.5 %collective-permute-start.1 = (bf16[512,512]{1,0:T(8,128)(2,1)}, bf16[512,512]{1,0:T(8,128)(2,1)S(1)}, u32[]{:S(2)}, u32[]{:S(2)}) collective-permute-start(bf16[512,512]{1,0:T(8,128)(2,1)} %ew_a.1), channel_id=1, source_target_pairs={{0,1},{1,0},{2,3},{3,2},{4,5},{5,4},{6,7},{7,6},{8,9},{9,8},{10,11... | collective-permute-start | bytes 1572872 | tf_op jit(solution)/shard_map/ppermute | solution.py:217
  0.5 0.8 %slice.3 = bf16[16,1024]{1,0:T(8,128)(2,1)S(1)} slice(bf16[2048,1024]{1,0:T(8,128)(2,1)} %sig_b.1), slice={[2032:2048], [0:1024]} | slice | bytes 65536 | tf_op jit(solution)/shard_map/slice | solution.py:254
  1.3 2.6 %collective-permute-start = (bf16[16,1024]{1,0:T(8,128)(2,1)S(1)}, bf16[16,1024]{1,0:T(8,128)(2,1)S(1)}, u32[]{:S(2)}, u32[]{:S(2)}) collective-permute-start(bf16[16,1024]{1,0:T(8,128)(2,1)S(1)} %slice.3), channel_id=1, source_target_pairs={{0,2},{2,4},{4,6},{6,8},{8,10},{10,12},{12,14},{14,0},{1,3},{3,5},... | collective-permute-start | bytes 98312 | tf_op jit(solution)/shard_map/ppermute | solution.py:254
  3.9 0.1 pad_add_fusion.sc
  4.0 0.1 add_add_fusion.1.sc
  4.0 1.4 %copy.11 = bf16[512,3,256]{0,2,1:T(8,128)(2,1)S(1)} copy(bf16[512,3,256]{2,0,1:T(8,128)(2,1)} %param.10) | data formatting | bytes 1572864 | tf_op args[3]
  5.5 0.3 copy.12.weight
  5.7 0.0 copy-start.3
  5.8 3.1 %collective-permute-done.rim_a.rim_b = bf16[16,1024]{1,0:T(8,128)(2,1)S(1)} collective-permute-done((bf16[16,1024]{1,0:T(8,128)(2,1)S(1)}, bf16[16,1024]{1,0:T(8,128)(2,1)S(1)}, u32[]{:S(2)}, u32[]{:S(2)}) %collective-permute-start) | collective-permute-done | bytes 32800 | tf_op jit(solution)/shard_map/ppermute | solution.py:254
  8.9 0.0 collective-permute-done.1.ew_b
  8.9 0.0 copy-start
  8.9 2.2 %copy-done = bf16[2048,1024]{1,0:T(8,128)(2,1)S(1)} copy-done((bf16[2048,1024]{1,0:T(8,128)(2,1)S(1)}, bf16[2048,1024]{1,0:T(8,128)(2,1)}, u32[]{:S(2)}) %copy-start) | copy-done | bytes 4194328
  11.1 9.3 %keys.1 = (bf16[2048,512]{1,0:T(8,128)(2,1)S(1)}, bf16[16,512]{1,0:T(8,128)(2,1)S(1)}, bf16[2048,512]{1,0:T(8,128)(2,1)S(1)}, bf16[2048,256]{1,0:T(8,128)(2,1)S(...) custom-call(s32[2]{0:T(128)S(1)} %pad_add_fusion.sc, bf16[2048,1024]{1,0:T(8,128)(2,1)S(1)} %copy-done, ...), custom_call_target="tpu_custom_call" | custom-call | tf_op jit(solution)/shard_map/keys/pallas_call | solution.py:266
  20.5 0.1 collective-permute-start.4
  20.6 0.4 collective-permute-start.3
  20.9 3.1 %collective-permute-start.2 = (bf16[272,128]{1,0:T(8,128)(2,1)S(1)}, bf16[272,128]{1,0:T(8,128)(2,1)S(1)}, u32[]{:S(2)}, u32[]{:S(2)}) collective-permute-start(bf16[272,128]{1,0:T(8,128)(2,1)S(1)} %get-tuple-element.16), channel_id=1, source_target_pairs={{0,2},{2,0},{4,6},{6,4},{8,10},{10,8},{12,14},{14,12},{1,3},{3,1},... | collective-permute-start | bytes 208904 | tf_op jit(solution)/shard_map/ppermute | solution.py:217
  24.0 1.1 %copy-done.4 = bf16[512,768]{1,0:T(8,128)(2,1)S(1)} copy-done((bf16[512,768]{1,0:T(8,128)(2,1)S(1)}, bf16[512,768]{1,0:T(8,128)(2,1)}, u32[]{:S(2)}) %copy-start.4) | copy-done | bytes 786456
  25.2 4.5 %queries.1.qf = bf16[2048,512]{1,0:T(8,128)(2,1)S(1)} custom-call(s32[2]{0:T(128)S(1)} %pad_add_fusion.sc, bf16[2048,512]{1,0:T(8,128)(2,1)S(1)} %get-tuple-element.11.normed, bf16[16,512]{1,0:T(8,128)(2,1)S(1)} %get-tuple-element.12.nrim, bf16[512,768]{1,0:T(8,128)(2,1)S(1)} %copy-done.4, f32[4,3,256]{2,1,0:T(4,128)S(1)} %copy.13.taps, ...), custom_call_target="tpu_custom_call" | custom-call | flops 2147483648 | bytes 8388608 | tf_op jit(solution)/shard_map/queries/pallas_call | solution.py:307
  29.7 0.0 collective-permute-done.3
  29.7 0.0 collective-permute-done.2
  29.7 0.1 fusion.2
  29.8 0.9 %collective-permute-start.5 = (bf16[272,128]{1,0:T(8,128)(2,1)S(1)}, bf16[272,128]{1,0:T(8,128)(2,1)S(1)}, u32[]{:S(2)}, u32[]{:S(2)}) collective-permute-start(bf16[272,128]{1,0:T(8,128)(2,1)S(1)} %get-tuple-element.17), channel_id=1, source_target_pairs={{0,8},{2,10},{4,12},{6,14},{8,0},{10,2},{12,4},{14,6},{1,9},{3,11}... | collective-permute-start | bytes 208904 | tf_op jit(solution)/shard_map/ppermute | solution.py:217
  30.7 3.6 %local.1 = f32[2048,512]{1,0:T(8,128)S(1)} custom-call(bf16[2048,512]{1,0:T(8,128)(2,1)S(1)} %queries.1.qf, bf16[2048,512]{1,0:T(8,128)(2,1)S(1)} %get-tuple-element.13.kf, bf16[2048,256]{1,0:T(8,128)(2,1)S(1)} %get-tuple-element.14.v), custom_call_target="tpu_custom_call" | custom-call | flops 4294967296 | bytes 9437184 | tf_op jit(solution)/shard_map/local/pallas_call | solution.py:332
  34.3 0.9 %collective-permute-done.5.far = bf16[272,128]{1,0:T(8,128)(2,1)S(1)} collective-permute-done((bf16[272,128]{1,0:T(8,128)(2,1)S(1)}, bf16[272,128]{1,0:T(8,128)(2,1)S(1)}, u32[]{:S(2)}, u32[]{:S(2)}) %collective-permute-start.5) | collective-permute-done | bytes 69664 | tf_op jit(solution)/shard_map/ppermute | solution.py:217
  35.3 2.0 %combine.3 = bf16[1024,256]{1,0:T(8,128)(2,1)} custom-call(s32[3]{0:T(128)S(1)} %add_add_fusion.1.sc, bf16[2048,512]{1,0:T(8,128)(2,1)S(1)} %queries.1.qf, f32[2048,512]{1,0:T(8,128)S(1)} %local.1, f32[8,272,128]{2,1,0:T(8,128)S(1)} %get-tuple-element.15.before, f32[272,128]{1,0:T(8,128)S(1)} %get-tuple-element.18.near, ...), custom_call_target="tpu_custom_call" | custom-call | flops 268435456 | bytes 4194304 | tf_op jit(solution)/shard_map/combine/pallas_call | solution.py:352
  37.2 0.0 collective-permute-start.6
  37.2 0.5 %collective-permute-start.7 = (bf16[256,512]{1,0:T(8,128)(2,1)}, bf16[256,512]{1,0:T(8,128)(2,1)}, u32[]{:S(2)}, u32[]{:S(2)}) collective-permute-start(bf16[256,512]{1,0:T(8,128)(2,1)} %w_mine.1), channel_id=1, source_target_pairs={{0,1},{1,0},{2,3},{3,2},{4,5},{5,4},{6,7},{7,6},{8,9},{9,8},{10,11... | collective-permute-start | bytes 786440 | tf_op jit(solution)/shard_map/ppermute | solution.py:217
  37.7 0.1 add_add_fusion.sc
  37.8 2.2 %copy-done.2 = f32[2048,512]{1,0:T(8,128)S(1)} copy-done((f32[2048,512]{1,0:T(8,128)S(1)}, f32[2048,512]{1,0:T(8,128)}, u32[]{:S(2)}) %copy-start.2) | copy-done | bytes 4194328
  40.0 1.3 %combine.2.mine = bf16[1024,256]{1,0:T(8,128)(2,1)S(1)} custom-call(s32[3]{0:T(128)S(1)} %add_add_fusion.sc, bf16[2048,512]{1,0:T(8,128)(2,1)S(1)} %queries.1.qf, f32[2048,512]{1,0:T(8,128)S(1)} %copy-done.2, f32[8,272,128]{2,1,0:T(8,128)S(1)} %get-tuple-element.15.before, f32[272,128]{1,0:T(8,128)S(1)} %get-tuple-element.18.near, ...), custom_call_target="tpu_custom_call" | custom-call | flops 268435456 | bytes 4194304 | tf_op jit(solution)/shard_map/combine/pallas_call | solution.py:352
  41.3 0.0 collective-permute-done.6.other
  41.3 2.8 %output.1 = bf16[1024,512]{1,0:T(8,128)(2,1)} custom-call(bf16[1024,256]{1,0:T(8,128)(2,1)S(1)} %combine.2.mine, bf16[1024,256]{1,0:T(8,128)(2,1)} %collective-permute-done.6.other, bf16[256,512]{1,0:T(8,128)(2,1)} %w_mine.1, bf16[256,512]{1,0:T(8,128)(2,1)} %collective-permute-done.7.w_other), custom_call_target="tpu_custom_call" | custom-call | tf_op jit(solution)/shard_map/output/pallas_call | solution.py:374
  (16 shorter events, 0.0 us)
Async XLA Ops:
  0.0 8.9 %copy-start.5 = (bf16[512,512]{1,0:T(8,128)(2,1)S(1)}, bf16[512,512]{1,0:T(8,128)(2,1)}, u32[]{:S(2)}) copy-start(bf16[512,512]{1,0:T(8,128)(2,1)} %ew_a.1) | copy-start | bytes 1572868
  0.0 5.7 %copy-start.8 = (f32[4,3,256]{2,0,1:T(4,128)S(1)}, f32[4,3,256]{2,0,1:T(4,128)}, u32[]{:S(2)}) copy-start(f32[4,3,256]{2,0,1:T(4,128)} %param.11) | copy-start | bytes 36868
  0.0 8.9 %copy-start.7 = (f32[512]{0:T(512)S(1)}, f32[512]{0:T(512)}, u32[]{:S(2)}) copy-start(f32[512]{0:T(512)} %param.9) | copy-start | bytes 6148
  0.0 8.9 %copy-start.6 = (bf16[4,64,128]{2,1,0:T(8,128)(2,1)S(1)}, bf16[4,64,128]{2,1,0:T(8,128)(2,1)}, u32[]{:S(2)}) copy-start(bf16[4,64,128]{2,1,0:T(8,128)(2,1)} %feat_w.3) | copy-start | bytes 196612
  0.0 8.9 %collective-permute-start.1 = (bf16[512,512]{1,0:T(8,128)(2,1)}, bf16[512,512]{1,0:T(8,128)(2,1)S(1)}, u32[]{:S(2)}, u32[]{:S(2)}) collective-permute-start(bf16[512,512]{1,0:T(8,128)(2,1)} %ew_a.1), channel_id=1, source_target_pairs={{0,1},{1,0},{2,3},{3,2},{4,5},{5,4},{6,7},{7,6},{8,9},{9,8},{10,11... | collective-permute-start | bytes 1572872 | tf_op jit(solution)/shard_map/ppermute | solution.py:217
  1.3 7.6 %collective-permute-start = (bf16[16,1024]{1,0:T(8,128)(2,1)S(1)}, bf16[16,1024]{1,0:T(8,128)(2,1)S(1)}, u32[]{:S(2)}, u32[]{:S(2)}) collective-permute-start(bf16[16,1024]{1,0:T(8,128)(2,1)S(1)} %slice.3), channel_id=1, source_target_pairs={{0,2},{2,4},{4,6},{6,8},{8,10},{10,12},{12,14},{14,0},{1,3},{3,5},... | collective-permute-start | bytes 98312 | tf_op jit(solution)/shard_map/ppermute | solution.py:254
  5.7 14.7 %copy-start.3 = (bf16[512,768]{1,0:T(8,128)(2,1)}, bf16[512,768]{1,0:T(8,128)(2,1)S(1)}, u32[]{:S(2)}) copy-start(bf16[512,768]{1,0:T(8,128)(2,1)S(1)} %copy.12.weight) | copy-start | bytes 2359300
  8.9 2.2 %copy-start = (bf16[2048,1024]{1,0:T(8,128)(2,1)S(1)}, bf16[2048,1024]{1,0:T(8,128)(2,1)}, u32[]{:S(2)}) copy-start(bf16[2048,1024]{1,0:T(8,128)(2,1)} %sig_b.1) | copy-start | bytes 12582916
  20.5 9.2 %collective-permute-start.4 = (bf16[272,128]{1,0:T(8,128)(2,1)S(1)}, bf16[272,128]{1,0:T(8,128)(2,1)S(1)}, u32[]{:S(2)}, u32[]{:S(2)}) collective-permute-start(bf16[272,128]{1,0:T(8,128)(2,1)S(1)} %get-tuple-element.16), channel_id=1, source_target_pairs={{0,6},{2,4},{4,2},{6,0},{8,14},{10,12},{12,10},{14,8},{1,7},{3,5},... | collective-permute-start | bytes 208904 | tf_op jit(solution)/shard_map/ppermute | solution.py:217
  20.6 9.1 %collective-permute-start.3 = (bf16[272,128]{1,0:T(8,128)(2,1)S(1)}, bf16[272,128]{1,0:T(8,128)(2,1)S(1)}, u32[]{:S(2)}, u32[]{:S(2)}) collective-permute-start(bf16[272,128]{1,0:T(8,128)(2,1)S(1)} %get-tuple-element.16), channel_id=1, source_target_pairs={{0,4},{2,6},{4,0},{6,2},{8,12},{10,14},{12,8},{14,10},{1,5},{3,7},... | collective-permute-start | bytes 208904 | tf_op jit(solution)/shard_map/ppermute | solution.py:217
  20.9 8.8 %collective-permute-start.2 = (bf16[272,128]{1,0:T(8,128)(2,1)S(1)}, bf16[272,128]{1,0:T(8,128)(2,1)S(1)}, u32[]{:S(2)}, u32[]{:S(2)}) collective-permute-start(bf16[272,128]{1,0:T(8,128)(2,1)S(1)} %get-tuple-element.16), channel_id=1, source_target_pairs={{0,2},{2,0},{4,6},{6,4},{8,10},{10,8},{12,14},{14,12},{1,3},{3,1},... | collective-permute-start | bytes 208904 | tf_op jit(solution)/shard_map/ppermute | solution.py:217
  24.0 1.1 %copy-start.4 = (bf16[512,768]{1,0:T(8,128)(2,1)S(1)}, bf16[512,768]{1,0:T(8,128)(2,1)}, u32[]{:S(2)}) copy-start(bf16[512,768]{1,0:T(8,128)(2,1)} %copy-done.3) | copy-start | bytes 2359300
  29.8 5.5 %collective-permute-start.5 = (bf16[272,128]{1,0:T(8,128)(2,1)S(1)}, bf16[272,128]{1,0:T(8,128)(2,1)S(1)}, u32[]{:S(2)}, u32[]{:S(2)}) collective-permute-start(bf16[272,128]{1,0:T(8,128)(2,1)S(1)} %get-tuple-element.17), channel_id=1, source_target_pairs={{0,8},{2,10},{4,12},{6,14},{8,0},{10,2},{12,4},{14,6},{1,9},{3,11}... | collective-permute-start | bytes 208904 | tf_op jit(solution)/shard_map/ppermute | solution.py:217
  34.3 2.9 %copy-start.1 = (f32[2048,512]{1,0:T(8,128)}, f32[2048,512]{1,0:T(8,128)S(1)}, u32[]{:S(2)}) copy-start(f32[2048,512]{1,0:T(8,128)S(1)} %local.1) | copy-start | bytes 12582916
  37.2 4.1 %collective-permute-start.6 = (bf16[1024,256]{1,0:T(8,128)(2,1)}, bf16[1024,256]{1,0:T(8,128)(2,1)}, u32[]{:S(2)}, u32[]{:S(2)}) collective-permute-start(bf16[1024,256]{1,0:T(8,128)(2,1)} %combine.3), channel_id=1, source_target_pairs={{0,1},{1,0},{2,3},{3,2},{4,5},{5,4},{6,7},{7,6},{8,9},{9,8},{10,11... | collective-permute-start | bytes 1572872 | tf_op jit(solution)/shard_map/ppermute | solution.py:217
  37.2 4.1 %collective-permute-start.7 = (bf16[256,512]{1,0:T(8,128)(2,1)}, bf16[256,512]{1,0:T(8,128)(2,1)}, u32[]{:S(2)}, u32[]{:S(2)}) collective-permute-start(bf16[256,512]{1,0:T(8,128)(2,1)} %w_mine.1), channel_id=1, source_target_pairs={{0,1},{1,0},{2,3},{3,2},{4,5},{5,4},{6,7},{7,6},{8,9},{9,8},{10,11... | collective-permute-start | bytes 786440 | tf_op jit(solution)/shard_map/ppermute | solution.py:217
  37.8 2.2 %copy-start.2 = (f32[2048,512]{1,0:T(8,128)S(1)}, f32[2048,512]{1,0:T(8,128)}, u32[]{:S(2)}) copy-start(f32[2048,512]{1,0:T(8,128)} %copy-done.1) | copy-start | bytes 12582916

commit v2 on v0

v2 whole, which is shorter than its diff:
```python
import functools
import math

import jax
import jax.numpy as jnp
from jax import lax
from jax.experimental import pallas as pl
from jax.experimental.pallas import tpu as pltpu
from jax.sharding import PartitionSpec as P

EPS = 1e-05
LOG2E = math.log2(math.e)
SUB = 256
RIM = 16
PAD = 8
LANES = 128
F32 = jnp.float32
BF16 = jnp.bfloat16
NN = (((1,), (0,)), ((), ()))
NT = (((1,), (1,)), ((), ()))
TN = (((0,), (0,)), ((), ()))


def dot(a, b, dims=NN):
    return lax.dot_general(a, b, dims, preferred_element_type=F32)


def call(kernel, ins, outs, name, scratch=(), work=(1, 1), mib=16):
    def spec(place):
        return pl.BlockSpec(memory_space=pltpu.VMEM if place is None else place)

    def pinned(array, place):
        return pltpu.with_memory_space_constraint(array, place) if place is pltpu.HBM else array

    return pl.pallas_call(
        kernel,
        in_specs=[spec(p) for _, p in ins],
        out_specs=[spec(p) for _, _, p in outs],
        out_shape=[jax.ShapeDtypeStruct(s, t) for s, t, _ in outs],
        scratch_shapes=list(scratch),
        compiler_params=pltpu.CompilerParams(vmem_limit_bytes=mib << 20),
        cost_estimate=pl.CostEstimate(flops=work[0] << 3, bytes_accessed=work[1], transcendentals=0),
        name=name,
    )(*[pinned(*i) for i in ins])


def vmem(*arrays):
    return [(a, None) for a in arrays]


def normalize(emb, gain):
    mean = jnp.mean(emb * emb, -1, keepdims=True)
    return (emb * lax.rsqrt(mean + EPS) * gain).astype(BF16)


def embed_own_kernel(
    sc, sig, ew_hbm, gain_hbm,
    partial, sig_other, near_rim, far_rim, ew, gain,
    buf, sem, late_sem,
):
    rep = sc[0]
    rows, half = sig_other.shape
    blocks = rows // SUB
    own = pl.ds(pl.multiple_of(rep * half, half), half)
    other = pl.ds(pl.multiple_of((1 - rep) * half, half), half)
    weight = pltpu.make_async_copy(ew_hbm, ew, late_sem.at[0])
    weight.start()
    copies = []
    for b in range(blocks):
        at = pl.ds(pl.multiple_of(rep * rows + b * SUB, SUB), SUB)
        copies.append(pltpu.make_async_copy(sig.at[at, own], buf.at[b], sem.at[b]))
        copies[-1].start()
    all_rows = pl.ds(pl.multiple_of(rep * rows, SUB), rows)
    late = [
        pltpu.make_async_copy(sig.at[pl.ds(2 * rows - RIM, RIM), :], far_rim, late_sem.at[1]),
        pltpu.make_async_copy(sig.at[pl.ds(rows - RIM, RIM), :], near_rim, late_sem.at[2]),
        pltpu.make_async_copy(gain_hbm, gain, late_sem.at[3]),
        pltpu.make_async_copy(sig.at[all_rows, other], sig_other, late_sem.at[4]),
    ]
    for copy in late:
        copy.start()
    weight.wait()
    for b in range(blocks):
        copies[b].wait()
        partial[b * SUB : (b + 1) * SUB, :] = dot(buf[b], ew[...])
    for copy in late:
        copy.wait()


def embed_other_kernel(partial, sig_other, ew_own, ew, gain, normed, ew_on):
    ew_on[...] = ew_own[...]
    for b in range(normed.shape[0] // SUB):
        rows = slice(b * SUB, (b + 1) * SUB)
        normed[rows, :] = normalize(partial[rows, :] + dot(sig_other[rows, :], ew[...]), gain[...])


def store_proj(pad, normed, weights, start):
    rows = normed.shape[0]
    c = 0
    for w in weights:
        proj = dot(normed, w).astype(BF16).astype(F32)
        for j in range(w.shape[1] // LANES):
            pad[c, start : start + rows, :] = proj[:, j * LANES : (j + 1) * LANES]
            c += 1


def convolve(pad, taps, part, first, count, start, rows):
    out = []
    for j in range(count):
        total = None
        for tap in range(taps.shape[1]):
            at = start - taps.shape[1] + 1 + tap
            weight = taps[part, tap : tap + 1, j * LANES : (j + 1) * LANES]
            term = weight * pad[first + j, at : at + rows, :]
            total = term if total is None else total + term
        out.append(total.astype(BF16))
    return jnp.concatenate(out, 1)


def features(part, diag, ones, head_dim):
    part_f = part.astype(F32)
    logits = dot(part, diag[...])
    squares = dot((part_f * part_f).astype(BF16), ones[...])
    scale = lax.rsqrt(squares * (1.0 / head_dim) + EPS) * (LOG2E / math.sqrt(head_dim))
    return jnp.exp2(logits * scale).astype(BF16)


def rim_rows(pad, nrim, weights, keep):
    c = 0
    for w in weights:
        proj = dot(nrim, w).astype(BF16).astype(F32) * keep
        for j in range(w.shape[1] // LANES):
            pad[c, 0:PAD, :] = proj[RIM - PAD :, j * LANES : (j + 1) * LANES]
            c += 1


def key_body(sc, normed, nrim, weight, taps, feat_w, kf, val, before, total, diag, ones, pad):
    heads, head_dim, feat = feat_w.shape
    cols = val.shape[1]
    tiles = cols // LANES
    diag[...] = jnp.zeros_like(diag)
    ones[...] = jnp.zeros_like(ones)
    for h in range(heads):
        at = (slice(h * head_dim, (h + 1) * head_dim), slice(h * feat, (h + 1) * feat))
        diag[at] = feat_w[h]
        ones[at] = jnp.ones((head_dim, feat), BF16)
    weights = (weight[1], weight[2])
    rim_rows(pad, nrim, weights, (sc[1] > 0).astype(F32))
    total[...] = jnp.zeros_like(total)
    for b in range(normed.shape[0] // SUB):
        rows = slice(b * SUB, (b + 1) * SUB)
        start = PAD + b * SUB
        store_proj(pad, normed[rows, :], weights, start)
        key = convolve(pad, taps, 1, 0, tiles, start, SUB)
        value = convolve(pad, taps, 2, tiles, tiles, start, SUB)
        val[rows, :] = value
        key_feat = features(key, diag, ones, head_dim)
        kf[rows, :] = key_feat
        before[b] = total[...]
        for pair in range(heads // 2):
            vp = value[:, pair * 2 * head_dim : (pair + 1) * 2 * head_dim]
            kp = key_feat[:, pair * 2 * feat : (pair + 1) * 2 * feat]
            both = dot(vp, kp, TN)
            for side in range(2):
                h = pair * 2 + side
                total[h * head_dim : (h + 1) * head_dim, :] += both[
                    side * head_dim : (side + 1) * head_dim, side * feat : (side + 1) * feat
                ]
        sums = jnp.sum(key_feat.astype(F32), 0, keepdims=True)
        for h in range(heads):
            at = heads * head_dim + h
            total[at : at + 1, :] += sums[:, h * feat : (h + 1) * feat]


def first_key_kernel(
    sc, far_rim, near_rim, ew_a, ew_b, gain, normed, weight, taps, feat_w,
    nrim, kf, val, before, total, diag, ones, pad,
):
    half = ew_a.shape[0]
    own = sc[0] == 0
    rim = jnp.where(own, far_rim[...].astype(F32), near_rim[...].astype(F32))
    lo, hi = rim[:, :half], rim[:, half:]
    mine = jnp.where(own, lo, hi).astype(BF16)
    other = jnp.where(own, hi, lo).astype(BF16)
    rows_n = normalize(dot(mine, ew_a[...]) + dot(other, ew_b[...]), gain[...])
    nrim[...] = rows_n
    key_body(sc, normed, rows_n, weight, taps, feat_w, kf, val, before, total, diag, ones, pad)


def key_kernel(
    sc, normed, nrim, weight, taps, feat_w, ow_hbm,
    kf, val, before, total, diag, ones, ow, pad, sem,
):
    copy = pltpu.make_async_copy(ow_hbm, ow, sem)
    copy.start()
    key_body(sc, normed, nrim[...], weight, taps, feat_w, kf, val, before, total, diag, ones, pad)
    copy.wait()


def query_kernel(
    sc, after, normed, nrim, weight, taps, diag, ones, kf, val, qf, out, pad, *, heads
):
    del after
    tiles = weight.shape[2] // LANES
    feat = qf.shape[1] // heads
    width = val.shape[1] // heads
    row = lax.broadcasted_iota(jnp.int32, (SUB, SUB), 0)
    col = lax.broadcasted_iota(jnp.int32, (SUB, SUB), 1)
    causal = row >= col
    left = lax.broadcasted_iota(jnp.int32, (SUB, 2 * width), 1) < width
    one, zero = jnp.ones((SUB, 2 * width), BF16), jnp.zeros((SUB, 2 * width), BF16)
    rim_rows(pad, nrim[...], (weight[0],), (sc[1] > 0).astype(F32))
    for b in range(normed.shape[0] // SUB):
        rows = slice(b * SUB, (b + 1) * SUB)
        start = PAD + b * SUB
        store_proj(pad, normed[rows, :], (weight[0],), start)
        query = convolve(pad, taps, 0, 0, tiles, start, SUB)
        query_feat = features(query, diag, ones, width)
        qf[rows, :] = query_feat
        for pair in range(heads // 2):
            vp = val[rows, pair * 2 * width : (pair + 1) * 2 * width]
            total = None
            for side in range(2):
                at = slice((pair * 2 + side) * feat, (pair * 2 + side + 1) * feat)
                mine = left if side == 0 else ~left
                scores = dot(query_feat[:, at], kf[rows, at], NT)
                weights = jnp.where(causal, scores, 0.0).astype(BF16)
                rhs = jnp.concatenate([jnp.where(mine, vp, zero), jnp.where(mine, one, zero)], 1)
                term = dot(weights, rhs)
                total = term if total is None else total + term
            out[rows, pair * 4 * width : (pair + 1) * 4 * width] = total


def attend(qf, local, before, state_in, b, heads):
    feat = qf.shape[1] // heads
    width = local.shape[1] // heads // 2
    zero = jnp.zeros((width, feat), BF16)
    rows = slice(b * SUB, (b + 1) * SUB)
    state = (before[b] + state_in).astype(BF16)
    out = []
    for pair in range(heads // 2):
        h = pair * 2
        s0, s1 = (state[(h + k) * width : (h + k + 1) * width] for k in range(2))
        t0, t1 = (
            jnp.broadcast_to(
                state[heads * width + h + k : heads * width + h + k + 1], (width, feat)
            )
            for k in range(2)
        )
        rhs = jnp.concatenate(
            [
                jnp.concatenate([s0, zero], 1),
                jnp.concatenate([zero, s1], 1),
                jnp.concatenate([t0, zero], 1),
                jnp.concatenate([zero, t1], 1),
            ],
            0,
        )
        both = local[rows, pair * 4 * width : (pair + 1) * 4 * width] + dot(
            qf[rows, pair * 2 * feat : (pair + 1) * 2 * feat], rhs, NT
        )
        out.append((both[:, : 2 * width] / both[:, 2 * width :]).astype(BF16))
    return jnp.concatenate(out, 1)


def own_kernel(qf, local, before, state, weight, out, *, heads):
    for b in range(qf.shape[0] // SUB):
        out[b * SUB : (b + 1) * SUB, :] = dot(
            attend(qf, local, before, state[...], b, heads), weight[...]
        )


def last_kernel(qf, local, before, state, weight, partial, out, buf, sem, *, heads):
    copies = []
    for b in range(qf.shape[0] // SUB):
        rows = slice(b * SUB, (b + 1) * SUB)
        attended = attend(qf, local, before, state[...].astype(F32), b, heads)
        buf[b] = (partial[rows, :] + dot(attended, weight[...])).astype(BF16)
        copies.append(pltpu.make_async_copy(buf.at[b], out.at[pl.ds(b * SUB, SUB), :], sem.at[b]))
        copies[-1].start()
    for copy in copies:
        copy.wait()


def swap(array, axis, by):
    devices = lax.axis_size(axis)
    return lax.ppermute(array, axis, [(i, i ^ by) for i in range(devices)])


def rounds(axis):
    devices, span, out = lax.axis_size(axis), 1, []
    while span < devices:
        radix = min(4, devices // span)
        out.append((span, radix))
        span *= radix
    return out


def earlier(axis):
    place = lax.axis_index(axis)
    flags = []
    for span, radix in rounds(axis):
        digit = (place >> (span.bit_length() - 1)) & (radix - 1)
        flags += [(digit ^ k) < digit for k in range(1, radix)]
    return flags


def prefix(group, axis, masks, covers):
    near = jnp.zeros(group.shape, F32)
    row = 0
    for span, radix in rounds(axis):
        sent = group.astype(BF16)
        if covers:
            covers.pop(0)(sent)
        for k in range(1, radix):
            got = swap(sent, axis, k * span).astype(F32)
            group = group + got
            near = near + jnp.where(masks[row : row + 1] > 0, got, 0.0)
            row += 1
    while covers:
        covers.pop(0)(group)
    return near


def shards(signal, embed_weight, norm_gain, qkv_weight, conv_weight, feature_weight, out_weight):
    rows, depth = signal.shape
    rows //= 2
    half, width = embed_weight.shape
    cols = qkv_weight.shape[2]
    heads, head_dim, feat = feature_weight.shape
    feats = heads * feat
    states = heads * head_dim + 16
    blocks = rows // SUB
    place, rep = lax.axis_index("tm"), lax.axis_index("rep")
    devices = lax.axis_size("tm")
    smem, hbm = pltpu.SMEM, pltpu.HBM

    ew_other = swap(embed_weight, "rep", 1)
    wqkv = [qkv_weight.transpose(1, 0, 2), swap(qkv_weight.transpose(1, 0, 2), "rep", 1)]
    taps = [conv_weight.transpose(1, 0, 2), swap(conv_weight.transpose(1, 0, 2), "rep", 1)]
    feat_w = [feature_weight, swap(feature_weight, "rep", 1)]
    sc = jnp.stack([rep, 2 * place + rep]).astype(jnp.int32)
    flags = jnp.stack([rep > 0, *earlier("tm")]).astype(F32)
    sc, masks = lax.optimization_barrier((sc, jnp.broadcast_to(flags[:, None], (flags.size, feat))))
    second, masks = masks[:1] > 0, masks[1:]
    gain = norm_gain.reshape(1, width)

    partial, sig_other, near_rim, _, ew_own, gain = call(
        embed_own_kernel,
        [(sc, smem), (signal, hbm), (embed_weight, hbm), (gain, hbm)],
        [
            ((rows, width), F32, None),
            ((rows, half), BF16, None),
            ((RIM, depth), BF16, None),
            ((RIM, depth), BF16, None),
            ((half, width), BF16, None),
            ((1, width), F32, None),
        ],
        "embed_own",
        [
            pltpu.VMEM((blocks, SUB, half), BF16),
            pltpu.SemaphoreType.DMA((blocks,)),
            pltpu.SemaphoreType.DMA((5,)),
        ],
        (2 * rows * half * width, 4 << 20),
    )
    far_rim = lax.ppermute(signal[2 * rows - RIM :], "tm", [(i, (i + 1) % devices) for i in range(devices)])
    normed, ew_own = call(
        embed_other_kernel,
        vmem(partial, sig_other, ew_own, ew_other, gain),
        [((rows, width), BF16, None), ((half, width), BF16, None)],
        "embed_other",
        (),
        (8, 8),
    )

    key_outs = [
        ((rows, feats), BF16, None),
        ((rows, cols), BF16, None),
        ((blocks, states, feat), F32, None),
        ((states, feat), F32, None),
        ((cols, feats), BF16, None),
        ((cols, feats), BF16, None),
    ]
    pads = pltpu.VMEM((2 * cols // LANES, PAD + rows, LANES), F32)
    key_work = (6 * rows * width * 2 * cols, 4 << 20)
    nrim, *other = call(
        first_key_kernel,
        [
            (sc, smem),
            *vmem(far_rim, near_rim, ew_own, ew_other, gain, normed),
            *vmem(wqkv[1], taps[1], feat_w[1]),
        ],
        [((RIM, width), BF16, None), *key_outs],
        "keys_other",
        [pads],
        key_work,
    )
    back = swap(other[3].astype(BF16), "rep", 1).astype(F32)
    own = call(
        key_kernel,
        [(sc, smem), *vmem(normed, nrim, wqkv[0], taps[0], feat_w[0]), (out_weight, hbm)],
        [*key_outs, (out_weight.shape, BF16, None)],
        "keys_own",
        [pads, pltpu.SemaphoreType.DMA],
        key_work,
    )
    ow = [own[6], swap(own[6], "rep", 1)]
    qf, local = [None] * 2, [None] * 2

    def query(k, keys, after):
        qf[k], local[k] = call(
            functools.partial(query_kernel, heads=heads),
            [(sc, smem), *vmem(after, normed, nrim, wqkv[k], taps[k], *keys[4:6], *keys[:2])],
            [((rows, feats), BF16, None), ((rows, 2 * cols), F32, None)],
            "queries",
            [pltpu.VMEM((cols // LANES, PAD + rows, LANES), F32)],
            (6 * rows * width * cols, 4 << 20),
        )

    covers = [functools.partial(query, 0, own), functools.partial(query, 1, other)]
    before = prefix(own[3] + back, "tm", masks, covers)
    state_own = before + jnp.where(second, back, 0.0)
    state_other = swap((before + jnp.where(second, 0.0, own[3])).astype(BF16), "rep", 1)

    (partial,) = call(
        functools.partial(own_kernel, heads=heads),
        vmem(qf[0], local[0], own[2], state_own, ow[0]),
        [((rows, width), F32, None)],
        "attend_own",
        (),
        (4 * rows * width * cols, 4 << 20),
    )
    return call(
        functools.partial(last_kernel, heads=heads),
        vmem(qf[1], local[1], other[2], state_other, ow[1], partial),
        [((rows, width), BF16, hbm)],
        "attend_other",
        [pltpu.VMEM((blocks, SUB, width), BF16), pltpu.SemaphoreType.DMA((blocks,))],
        (4 * rows * width * cols, 4 << 20),
    )[0]


def solution(mesh):
    in_specs = (
        P(("groups", "tm"), None),
        P("rep", None),
        P(),
        P(None, None, "rep"),
        P(None, None, "rep"),
        P("rep", None, None),
        P("rep", None),
    )
    out_specs = P(("groups", "tm", "rep"), None)
    return jax.shard_map(shards, mesh=mesh, in_specs=in_specs, out_specs=out_specs, check_vma=False)
```

time: 161 us -> 35.4 us (0.22)
  blocking collectives: 52.6 us -> 0 us
  matrix products: 37 us -> 0 us
  Pallas kernels: 0 us -> 22.3 us
  waiting for transfers between devices: 23.4 us -> 1.93 us
  local copies, waits for them, and re-layouts: 16 us -> 0.95 us
  between operations: 13.7 us -> 0.15 us
  other arithmetic: 13.8 us -> 0.27 us
  starting transfers between devices: 3.68 us -> 9.58 us
    all_gather x2 -> x0, blocking collectives: 52.6 us -> none  [prefix(): lax.all_gather(a.astype(kind), axis)]
    dot_general x22 -> x0, matrix products: 37 us -> none  [the longest x2 8.83 us: feature_map(): jnp.einsum('thd,hdf->thf', unit, feat_weights, precision=high)]
    pallas_call x0 -> x8, Pallas kernels: none -> 22.3 us  [call(): pl.pallas_call(kernel, in_specs=[spec(p) for _, p in ins], out_specs=[spe...]
    all_gather x1 -> x0, waiting for transfers between devices: 11.1 us -> none  [embed_norm(): lax.all_gather(embed_weight, 'rep', axis=0, tiled=True)]
    reduce_scatter x1 -> x0, waiting for transfers between devices: 10.4 us -> none  [shards(): lax.psum_scatter(jnp.dot(attended, out_weight, preferred_element_type=jnp...]
    ppermute x1 -> x12, starting transfers between devices: 3.64 us -> 9.58 us  [the longest x11 7.06 us: swap(): return lax.ppermute(array, axis, [(i, i ^ by) for i in range(devices)])]
    convert_element_type x2 -> x4, other arithmetic: 5.06 us -> 0.09 us  [the longest x2 0.08 us: prefix(): sent = group.astype(BF16)]
    another operation x2 -> x1, local copies, waits for them, and re-layouts: 4.8 us -> 0.1 us  [shards(): flags = jnp.stack([rep > 0, *earlier('tm')]).astype(F32)]
  transfers between devices with their start and end apart: 3 -> 12, of which waited for: 3 -> 4; matrix products, arithmetic and copies ran while one was open for 1% -> 3% of each run, Pallas kernels for 0% -> 47%
where the time goes in v2:
time: 35.4 us; the launch traced here: 35.2 us
  Pallas kernels  22.3 us (63%)
  starting transfers between devices  9.58 us (27%)
  waiting for transfers between devices  1.93 us (5%)
  local copies, waits for them, and re-layouts  0.95 us (3%)
    pallas_call x8, Pallas kernels, call(): pl.pallas_call(kernel, in_specs=[spec(p) for _, p in ins], out_specs=[spe...  22.3 us
    ppermute x11, starting transfers between devices, swap(): return lax.ppermute(array, axis, [(i, i ^ by) for i in range(devices)])  7.06 us
    ppermute x1, starting transfers between devices, shards(): lax.ppermute(signal[2 * rows - RIM:], 'tm', [(i, (i + 1) % devices) for i...  2.52 us
    ppermute x11, waiting for transfers between devices, swap(): return lax.ppermute(array, axis, [(i, i ^ by) for i in range(devices)])  1.84 us
    slice x1, local copies, waits for them, and re-layouts, shards(): signal[2 * rows - RIM:]  0.76 us
  transfers between devices with their start and end apart: 12, of which 4 were waited for; matrix products, arithmetic and copies ran while one was open for 3% of the time, Pallas kernels for 47%

profile of v2, /device:TPU:0, one launch (start us, length us, event | category | flops | bytes accessed | tf_op | source)
XLA Modules:
  0.0 35.2 jit_solution(8120782810972097121)
XLA Ops:
  0.0 0.5 %collective-permute-start.2 = (bf16[3,512,256]{2,1,0:T(8,128)(2,1)}, bf16[3,512,256]{2,1,0:T(8,128)(2,1)S(1)}, u32[]{:S(2)}, u32[]{:S(2)}) collective-permute-start(bf16[3,512,256]{2,1,0:T(8,128)(2,1)} %bitcast.20), channel_id=1, source_target_pairs={{0,1},{1,0},{2,3},{3,2},{4,5},{5,4},{6,7},{7,6},{8,9},{9,8},{10,11... | collective-permute-start | bytes 2359304 | tf_op jit(solution)/shard_map/ppermute | solution.py:287
  0.5 0.1 collective-permute-start
  0.5 0.5 %collective-permute-start.3 = (f32[3,4,256]{2,1,0:T(4,128)}, f32[3,4,256]{2,1,0:T(4,128)S(1)}, u32[]{:S(2)}, u32[]{:S(2)}) collective-permute-start(f32[3,4,256]{2,1,0:T(4,128)} %bitcast.23), channel_id=1, source_target_pairs={{0,1},{1,0},{2,3},{3,2},{4,5},{5,4},{6,7},{7,6},{8,9},{9,8},{10,11... | collective-permute-start | bytes 36872 | tf_op jit(solution)/shard_map/ppermute | solution.py:287
  1.0 0.8 %slice.23 = bf16[16,1024]{1,0:T(8,128)(2,1)S(1)} slice(bf16[2048,1024]{1,0:T(8,128)(2,1)} %sig.1), slice={[2032:2048], [0:1024]} | slice | bytes 65536 | tf_op jit(solution)/shard_map/slice | solution.py:367
  1.7 2.5 %collective-permute-start.1 = (bf16[16,1024]{1,0:T(8,128)(2,1)S(1)}, bf16[16,1024]{1,0:T(8,128)(2,1)S(1)}, u32[]{:S(2)}, u32[]{:S(2)}) collective-permute-start(bf16[16,1024]{1,0:T(8,128)(2,1)S(1)} %slice.23), channel_id=1, source_target_pairs={{0,2},{2,4},{4,6},{6,8},{8,10},{10,12},{12,14},{14,0},{1,3},{3,5},... | collective-permute-start | bytes 98312 | tf_op jit(solution)/shard_map/ppermute | solution.py:367
  4.2 0.2 collective-permute-start.4
  4.5 0.1 stack.35
  4.6 0.1 pad_add_fusion.sc
  4.7 0.1 broadcast_in_dim.60
  4.7 3.6 %embed_own.1 = (f32[1024,512]{1,0:T(8,128)S(1)}, bf16[1024,512]{1,0:T(8,128)(2,1)S(1)}, bf16[16,1024]{1,0:T(8,128)(2,1)S(1)}, bf16[16,1024]{1,0:T(8,128)(2,1)}, ...) custom-call(s32[2]{0:T(128)S(1)} %pad_add_fusion.sc, bf16[2048,1024]{1,0:T(8,128)(2,1)} %sig.1, ...), custom_call_target="tpu_custom_call" | custom-call | flops 4294967296 | bytes 4194304 | tf_op jit(solution)/shard_map/embed_own/pallas_call | solution.py:35
  8.3 0.9 %embed_other.1 = (bf16[1024,512]{1,0:T(8,128)(2,1)S(1)}, bf16[512,512]{1,0:T(8,128)(2,1)S(1)}) custom-call(f32[1024,512]{1,0:T(8,128)S(1)} %get-tuple-element.33.partial, bf16[1024,512]{1,0:T(8,128)(2,1)S(1)} %get-tuple-element.34.sig_other, bf16[512,512]{1,0:T(8,128)(2,1)S(1)} %get-tuple-element.35.ew_own, ...), custom_call_target="tpu_custom_call" | custom-call | flops 64 | bytes 8 | tf_op jit(solution)/shard_map/embed_other/pallas_call | solution.py:35
  9.2 0.1 collective-permute-done.1.far_rim
  9.4 0.0 copy-start.1
  9.4 0.0 copy-start.2
  9.4 3.9 %keys_other.1 = (bf16[16,512]{1,0:T(8,128)(2,1)S(1)}, bf16[1024,512]{1,0:T(8,128)(2,1)S(1)}, bf16[1024,256]{1,0:T(8,128)(2,1)S(1)}, f32[4,272,128]{2,1,0:T(8,128...) custom-call(s32[2]{0:T(128)S(1)} %pad_add_fusion.sc, ...), custom_call_target="tpu_custom_call" | custom-call | flops 12884901888 | bytes 4194304 | tf_op jit(solution)/shard_map/keys_other/pallas_call | solution.py:35
  13.3 0.3 collective-permute-start.5
  13.6 3.6 %keys_own.1 = (bf16[1024,512]{1,0:T(8,128)(2,1)S(1)}, bf16[1024,256]{1,0:T(8,128)(2,1)S(1)}, f32[4,272,128]{2,1,0:T(8,128)S(1)}, f32[272,128]{1,0:T(8,128)S(1)},...) custom-call(s32[2]{0:T(128)S(1)} %pad_add_fusion.sc, ...), custom_call_target="tpu_custom_call" | custom-call | flops 12884901888 | bytes 4194304 | tf_op jit(solution)/shard_map/keys_own/pallas_call | solution.py:35
  17.2 0.3 collective-permute-start.11
  17.5 1.5 %collective-permute-start.6 = (bf16[272,128]{1,0:T(8,128)(2,1)S(1)}, bf16[272,128]{1,0:T(8,128)(2,1)S(1)}, u32[]{:S(2)}, u32[]{:S(2)}) collective-permute-start(bf16[272,128]{1,0:T(8,128)(2,1)S(1)} %fusion.5.after), channel_id=1, source_target_pairs={{0,2},{2,0},{4,6},{6,4},{8,10},{10,8},{12,14},{14,12},{1,3},{3,1},... | collective-permute-start | bytes 208904 | tf_op jit(solution)/shard_map/ppermute | solution.py:287
  19.1 1.6 %collective-permute-start.7 = (bf16[272,128]{1,0:T(8,128)(2,1)S(1)}, bf16[272,128]{1,0:T(8,128)(2,1)S(1)}, u32[]{:S(2)}, u32[]{:S(2)}) collective-permute-start(bf16[272,128]{1,0:T(8,128)(2,1)S(1)} %fusion.5.after), channel_id=1, source_target_pairs={{0,4},{2,6},{4,0},{6,2},{8,12},{10,14},{12,8},{14,10},{1,5},{3,7},... | collective-permute-start | bytes 208904 | tf_op jit(solution)/shard_map/ppermute | solution.py:287
  20.6 0.5 %collective-permute-start.8 = (bf16[272,128]{1,0:T(8,128)(2,1)S(1)}, bf16[272,128]{1,0:T(8,128)(2,1)S(1)}, u32[]{:S(2)}, u32[]{:S(2)}) collective-permute-start(bf16[272,128]{1,0:T(8,128)(2,1)S(1)} %fusion.5.after), channel_id=1, source_target_pairs={{0,6},{2,4},{4,2},{6,0},{8,14},{10,12},{12,10},{14,8},{1,7},{3,5},... | collective-permute-start | bytes 208904 | tf_op jit(solution)/shard_map/ppermute | solution.py:287
  21.1 3.7 %queries.3 = (bf16[1024,512]{1,0:T(8,128)(2,1)S(1)}, f32[1024,512]{1,0:T(8,128)S(1)}) custom-call(s32[2]{0:T(128)S(1)} %pad_add_fusion.sc, bf16[272,128]{1,0:T(8,128)(2,1)S(1)} %fusion.5.after, bf16[1024,512]{1,0:T(8,128)(2,1)S(1)} %get-tuple-element.37.normed, bf16[16,512]{1,0:T(8,128)(2,1)S(1)} %get-tuple-element.40.nrim, ...), custom_call_target="tpu_custom_call" | custom-call | flops 6442450944 | bytes 4194304 | tf_op jit(solution)/shard_map/queries/pallas_call | solution.py:35
  24.8 1.0 %collective-permute-done.8 = bf16[272,128]{1,0:T(8,128)(2,1)S(1)} collective-permute-done((bf16[272,128]{1,0:T(8,128)(2,1)S(1)}, bf16[272,128]{1,0:T(8,128)(2,1)S(1)}, u32[]{:S(2)}, u32[]{:S(2)}) %collective-permute-start.8) | collective-permute-done | bytes 69664 | tf_op jit(solution)/shard_map/ppermute | solution.py:287
  25.8 0.1 fusion.4.after
  25.9 1.6 %collective-permute-start.9 = (bf16[272,128]{1,0:T(8,128)(2,1)S(1)}, bf16[272,128]{1,0:T(8,128)(2,1)S(1)}, u32[]{:S(2)}, u32[]{:S(2)}) collective-permute-start(bf16[272,128]{1,0:T(8,128)(2,1)S(1)} %fusion.4.after), channel_id=1, source_target_pairs={{0,8},{2,10},{4,12},{6,14},{8,0},{10,2},{12,4},{14,6},{1,9},{3,11}... | collective-permute-start | bytes 208904 | tf_op jit(solution)/shard_map/ppermute | solution.py:287
  27.5 3.7 %queries.2 = (bf16[1024,512]{1,0:T(8,128)(2,1)S(1)}, f32[1024,512]{1,0:T(8,128)S(1)}) custom-call(s32[2]{0:T(128)S(1)} %pad_add_fusion.sc, bf16[272,128]{1,0:T(8,128)(2,1)S(1)} %fusion.4.after, bf16[1024,512]{1,0:T(8,128)(2,1)S(1)} %get-tuple-element.37.normed, bf16[16,512]{1,0:T(8,128)(2,1)S(1)} %get-tuple-element.40.nrim, ...), custom_call_target="tpu_custom_call" | custom-call | flops 6442450944 | bytes 4194304 | tf_op jit(solution)/shard_map/queries/pallas_call | solution.py:35
  31.2 0.7 %collective-permute-done.9 = bf16[272,128]{1,0:T(8,128)(2,1)S(1)} collective-permute-done((bf16[272,128]{1,0:T(8,128)(2,1)S(1)}, bf16[272,128]{1,0:T(8,128)(2,1)S(1)}, u32[]{:S(2)}, u32[]{:S(2)}) %collective-permute-start.9) | collective-permute-done | bytes 69664 | tf_op jit(solution)/shard_map/ppermute | solution.py:287
  31.9 0.1 fusion
  32.0 0.1 collective-permute-start.10
  32.1 1.1 %attend_own.1.partial = f32[1024,512]{1,0:T(8,128)S(1)} custom-call(bf16[1024,512]{1,0:T(8,128)(2,1)S(1)} %get-tuple-element.56.qf, f32[1024,512]{1,0:T(8,128)S(1)} %get-tuple-element.57.local, f32[4,272,128]{2,1,0:T(8,128)S(1)} %get-tuple-element.58.before, f32[272,128]{1,0:T(8,128)S(1)} %get-tuple-element.59.state, ...), custom_call_target="tpu_custom_call" | custom-call | flops 4294967296 | bytes 4194304 | tf_op jit(solution)/shard_map/attend_own/pallas_call | solution.py:35
  33.2 0.2 collective-permute-done.10.state
  33.3 1.9 %attend_other.1 = bf16[1024,512]{1,0:T(8,128)(2,1)} custom-call(bf16[1024,512]{1,0:T(8,128)(2,1)S(1)} %get-tuple-element.47.qf, f32[1024,512]{1,0:T(8,128)S(1)} %get-tuple-element.48.local, f32[4,272,128]{2,1,0:T(8,128)S(1)} %get-tuple-element.49.before, bf16[272,128]{1,0:T(8,128)(2,1)S(1)} %collective-permute-done.10.state, ...), custom_call_target="tpu_custom_call" | custom-call | flops 4294967296 | bytes 4194304 | tf_op jit(solution)/shard_map/attend_other/pallas_call | solution.py:35
  (16 shorter events, 0.1 us)
Async XLA Ops:
  0.0 9.3 %collective-permute-start.2 = (bf16[3,512,256]{2,1,0:T(8,128)(2,1)}, bf16[3,512,256]{2,1,0:T(8,128)(2,1)S(1)}, u32[]{:S(2)}, u32[]{:S(2)}) collective-permute-start(bf16[3,512,256]{2,1,0:T(8,128)(2,1)} %bitcast.20), channel_id=1, source_target_pairs={{0,1},{1,0},{2,3},{3,2},{4,5},{5,4},{6,7},{7,6},{8,9},{9,8},{10,11... | collective-permute-start | bytes 2359304 | tf_op jit(solution)/shard_map/ppermute | solution.py:287
  0.5 7.9 %collective-permute-start = (bf16[512,512]{1,0:T(8,128)(2,1)}, bf16[512,512]{1,0:T(8,128)(2,1)S(1)}, u32[]{:S(2)}, u32[]{:S(2)}) collective-permute-start(bf16[512,512]{1,0:T(8,128)(2,1)} %ew_hbm.1), channel_id=1, source_target_pairs={{0,1},{1,0},{2,3},{3,2},{4,5},{5,4},{6,7},{7,6},{8,9},{9,8},{10,11... | collective-permute-start | bytes 1572872 | tf_op jit(solution)/shard_map/ppermute | solution.py:287
  0.5 8.7 %collective-permute-start.3 = (f32[3,4,256]{2,1,0:T(4,128)}, f32[3,4,256]{2,1,0:T(4,128)S(1)}, u32[]{:S(2)}, u32[]{:S(2)}) collective-permute-start(f32[3,4,256]{2,1,0:T(4,128)} %bitcast.23), channel_id=1, source_target_pairs={{0,1},{1,0},{2,3},{3,2},{4,5},{5,4},{6,7},{7,6},{8,9},{9,8},{10,11... | collective-permute-start | bytes 36872 | tf_op jit(solution)/shard_map/ppermute | solution.py:287
  1.7 7.6 %collective-permute-start.1 = (bf16[16,1024]{1,0:T(8,128)(2,1)S(1)}, bf16[16,1024]{1,0:T(8,128)(2,1)S(1)}, u32[]{:S(2)}, u32[]{:S(2)}) collective-permute-start(bf16[16,1024]{1,0:T(8,128)(2,1)S(1)} %slice.23), channel_id=1, source_target_pairs={{0,2},{2,4},{4,6},{6,8},{8,10},{10,12},{12,14},{14,0},{1,3},{3,5},... | collective-permute-start | bytes 98312 | tf_op jit(solution)/shard_map/ppermute | solution.py:367
  4.2 5.1 %collective-permute-start.4 = (bf16[4,64,128]{2,1,0:T(8,128)(2,1)}, bf16[4,64,128]{2,1,0:T(8,128)(2,1)S(1)}, u32[]{:S(2)}, u32[]{:S(2)}) collective-permute-start(bf16[4,64,128]{2,1,0:T(8,128)(2,1)} %feat_w.1), channel_id=1, source_target_pairs={{0,1},{1,0},{2,3},{3,2},{4,5},{5,4},{6,7},{7,6},{8,9},{9,8},{10,11... | collective-permute-start | bytes 196616 | tf_op jit(solution)/shard_map/ppermute | solution.py:287
  9.3 4.2 %copy-start = (bf16[512,3,256]{2,0,1:T(8,128)(2,1)S(1)}, bf16[512,3,256]{2,0,1:T(8,128)(2,1)}, u32[]{:S(2)}) copy-start(bf16[512,3,256]{2,0,1:T(8,128)(2,1)} %param.10) | copy-start | bytes 2359300
  9.4 4.2 %copy-start.1 = (bf16[4,64,128]{2,1,0:T(8,128)(2,1)S(1)}, bf16[4,64,128]{2,1,0:T(8,128)(2,1)}, u32[]{:S(2)}) copy-start(bf16[4,64,128]{2,1,0:T(8,128)(2,1)} %feat_w.1) | copy-start | bytes 196612
  9.4 4.2 %copy-start.2 = (f32[4,3,256]{2,0,1:T(4,128)S(1)}, f32[4,3,256]{2,0,1:T(4,128)}, u32[]{:S(2)}) copy-start(f32[4,3,256]{2,0,1:T(4,128)} %param.11) | copy-start | bytes 36868
  13.3 4.2 %collective-permute-start.5 = (bf16[272,128]{1,0:T(8,128)(2,1)S(1)}, bf16[272,128]{1,0:T(8,128)(2,1)S(1)}, u32[]{:S(2)}, u32[]{:S(2)}) collective-permute-start(bf16[272,128]{1,0:T(8,128)(2,1)S(1)} %convert_element_type.35), channel_id=1, source_target_pairs={{0,1},{1,0},{2,3},{3,2},{4,5},{5,4},{6,7},{7,6},{8,9},{9,8},{10,11... | collective-permute-start | bytes 208904 | tf_op jit(solution)/shard_map/ppermute | solution.py:287
  17.2 16.0 %collective-permute-start.11 = (bf16[256,512]{1,0:T(8,128)(2,1)S(1)}, bf16[256,512]{1,0:T(8,128)(2,1)S(1)}, u32[]{:S(2)}, u32[]{:S(2)}) collective-permute-start(bf16[256,512]{1,0:T(8,128)(2,1)S(1)} %get-tuple-element.51.weight), channel_id=1, source_target_pairs={{0,1},{1,0},{2,3},{3,2},{4,5},{5,4},{6,7},{7,6},{8,9},{9,8},{10,11... | collective-permute-start | bytes 786440 | tf_op jit(solution)/shard_map/ppermute | solution.py:287
  17.5 7.3 %collective-permute-start.6 = (bf16[272,128]{1,0:T(8,128)(2,1)S(1)}, bf16[272,128]{1,0:T(8,128)(2,1)S(1)}, u32[]{:S(2)}, u32[]{:S(2)}) collective-permute-start(bf16[272,128]{1,0:T(8,128)(2,1)S(1)} %fusion.5.after), channel_id=1, source_target_pairs={{0,2},{2,0},{4,6},{6,4},{8,10},{10,8},{12,14},{14,12},{1,3},{3,1},... | collective-permute-start | bytes 208904 | tf_op jit(solution)/shard_map/ppermute | solution.py:287
  19.1 5.8 %collective-permute-start.7 = (bf16[272,128]{1,0:T(8,128)(2,1)S(1)}, bf16[272,128]{1,0:T(8,128)(2,1)S(1)}, u32[]{:S(2)}, u32[]{:S(2)}) collective-permute-start(bf16[272,128]{1,0:T(8,128)(2,1)S(1)} %fusion.5.after), channel_id=1, source_target_pairs={{0,4},{2,6},{4,0},{6,2},{8,12},{10,14},{12,8},{14,10},{1,5},{3,7},... | collective-permute-start | bytes 208904 | tf_op jit(solution)/shard_map/ppermute | solution.py:287
  20.6 5.2 %collective-permute-start.8 = (bf16[272,128]{1,0:T(8,128)(2,1)S(1)}, bf16[272,128]{1,0:T(8,128)(2,1)S(1)}, u32[]{:S(2)}, u32[]{:S(2)}) collective-permute-start(bf16[272,128]{1,0:T(8,128)(2,1)S(1)} %fusion.5.after), channel_id=1, source_target_pairs={{0,6},{2,4},{4,2},{6,0},{8,14},{10,12},{12,10},{14,8},{1,7},{3,5},... | collective-permute-start | bytes 208904 | tf_op jit(solution)/shard_map/ppermute | solution.py:287
  25.9 6.0 %collective-permute-start.9 = (bf16[272,128]{1,0:T(8,128)(2,1)S(1)}, bf16[272,128]{1,0:T(8,128)(2,1)S(1)}, u32[]{:S(2)}, u32[]{:S(2)}) collective-permute-start(bf16[272,128]{1,0:T(8,128)(2,1)S(1)} %fusion.4.after), channel_id=1, source_target_pairs={{0,8},{2,10},{4,12},{6,14},{8,0},{10,2},{12,4},{14,6},{1,9},{3,11}... | collective-permute-start | bytes 208904 | tf_op jit(solution)/shard_map/ppermute | solution.py:287
  32.0 1.3 %collective-permute-start.10 = (bf16[272,128]{1,0:T(8,128)(2,1)S(1)}, bf16[272,128]{1,0:T(8,128)(2,1)S(1)}, u32[]{:S(2)}, u32[]{:S(2)}) collective-permute-start(bf16[272,128]{1,0:T(8,128)(2,1)S(1)} %get-tuple-element.60), channel_id=1, source_target_pairs={{0,1},{1,0},{2,3},{3,2},{4,5},{5,4},{6,7},{7,6},{8,9},{9,8},{10,11... | collective-permute-start | bytes 208904 | tf_op jit(solution)/shard_map/ppermute | solution.py:287

commit v3 on v2

--- a/solution.py
+++ b/solution.py
@@ -11,6 +11,7 @@
 EPS = 1e-05
 LOG2E = math.log2(math.e)
 SUB = 256
+STEP = 512
 RIM = 16
 PAD = 8
 LANES = 128
@@ -53,45 +54,25 @@
     return (emb * lax.rsqrt(mean + EPS) * gain).astype(BF16)
 
 
-def embed_own_kernel(
-    sc, sig, ew_hbm, gain_hbm,
-    partial, sig_other, near_rim, far_rim, ew, gain,
-    buf, sem, late_sem,
-):
+def rim_kernel(sc, sig, rim, sem):
+    del sc
+    copy = pltpu.make_async_copy(sig.at[pl.ds(sig.shape[0] - RIM, RIM), :], rim, sem)
+    copy.start()
+    copy.wait()
+
+
+def embed_kernel(sc, sig, ew_a, ew_b, gain, normed, near_rim):
     rep = sc[0]
-    rows, half = sig_other.shape
-    blocks = rows // SUB
+    rows = normed.shape[0]
+    half = ew_a.shape[0]
     own = pl.ds(pl.multiple_of(rep * half, half), half)
     other = pl.ds(pl.multiple_of((1 - rep) * half, half), half)
-    weight = pltpu.make_async_copy(ew_hbm, ew, late_sem.at[0])
-    weight.start()
-    copies = []
-    for b in range(blocks):
-        at = pl.ds(pl.multiple_of(rep * rows + b * SUB, SUB), SUB)
-        copies.append(pltpu.make_async_copy(sig.at[at, own], buf.at[b], sem.at[b]))
-        copies[-1].start()
-    all_rows = pl.ds(pl.multiple_of(rep * rows, SUB), rows)
-    late = [
-        pltpu.make_async_copy(sig.at[pl.ds(2 * rows - RIM, RIM), :], far_rim, late_sem.at[1]),
-        pltpu.make_async_copy(sig.at[pl.ds(rows - RIM, RIM), :], near_rim, late_sem.at[2]),
-        pltpu.make_async_copy(gain_hbm, gain, late_sem.at[3]),
-        pltpu.make_async_copy(sig.at[all_rows, other], sig_other, late_sem.at[4]),
-    ]
-    for copy in late:
-        copy.start()
-    weight.wait()
-    for b in range(blocks):
-        copies[b].wait()
-        partial[b * SUB : (b + 1) * SUB, :] = dot(buf[b], ew[...])
-    for copy in late:
-        copy.wait()
-
-
-def embed_other_kernel(partial, sig_other, ew_own, ew, gain, normed, ew_on):
-    ew_on[...] = ew_own[...]
-    for b in range(normed.shape[0] // SUB):
-        rows = slice(b * SUB, (b + 1) * SUB)
-        normed[rows, :] = normalize(partial[rows, :] + dot(sig_other[rows, :], ew[...]), gain[...])
+    near_rim[...] = sig[rows - RIM : rows, :]
+    for b in range(rows // STEP):
+        at = pl.ds(pl.multiple_of(rep * rows + b * STEP, STEP), STEP)
+        normed[b * STEP : (b + 1) * STEP, :] = normalize(
+            dot(sig[at, own], ew_a[...]) + dot(sig[at, other], ew_b[...]), gain[...]
+        )
 
 
 def store_proj(pad, normed, weights, start):
@@ -117,12 +98,19 @@
     return jnp.concatenate(out, 1)
 
 
-def features(part, diag, ones, head_dim):
+def features(part, diag, ones, heads):
+    rows, width = part.shape[0], part.shape[1] // heads
+    feat = diag.shape[1] // heads
     part_f = part.astype(F32)
     logits = dot(part, diag[...])
     squares = dot((part_f * part_f).astype(BF16), ones[...])
-    scale = lax.rsqrt(squares * (1.0 / head_dim) + EPS) * (LOG2E / math.sqrt(head_dim))
-    return jnp.exp2(logits * scale).astype(BF16)
+    scale = lax.rsqrt(squares * (1.0 / width) + EPS) * (LOG2E / math.sqrt(width))
+    share = scale.shape[1] // heads
+    out = []
+    for h in range(heads):
+        mine = jnp.broadcast_to(scale[:, h * share : h * share + 1], (rows, feat))
+        out.append(jnp.exp2(logits[:, h * feat : (h + 1) * feat] * mine).astype(BF16))
+    return jnp.concatenate(out, 1)
 
 
 def rim_rows(pad, nrim, weights, keep):
@@ -139,34 +127,35 @@
     cols = val.shape[1]
     tiles = cols // LANES
     diag[...] = jnp.zeros_like(diag)
-    ones[...] = jnp.zeros_like(ones)
+    share = LANES // heads
+    of_row = lax.broadcasted_iota(jnp.int32, ones.shape, 0) // head_dim
+    of_col = lax.broadcasted_iota(jnp.int32, ones.shape, 1) // share
+    ones[...] = jnp.where(of_row == of_col, 1.0, 0.0).astype(BF16)
     for h in range(heads):
-        at = (slice(h * head_dim, (h + 1) * head_dim), slice(h * feat, (h + 1) * feat))
-        diag[at] = feat_w[h]
-        ones[at] = jnp.ones((head_dim, feat), BF16)
+        diag[h * head_dim : (h + 1) * head_dim, h * feat : (h + 1) * feat] = feat_w[h]
     weights = (weight[1], weight[2])
     rim_rows(pad, nrim, weights, (sc[1] > 0).astype(F32))
     total[...] = jnp.zeros_like(total)
-    for b in range(normed.shape[0] // SUB):
-        rows = slice(b * SUB, (b + 1) * SUB)
-        start = PAD + b * SUB
-        store_proj(pad, normed[rows, :], weights, start)
-        key = convolve(pad, taps, 1, 0, tiles, start, SUB)
-        value = convolve(pad, taps, 2, tiles, tiles, start, SUB)
-        val[rows, :] = value
-        key_feat = features(key, diag, ones, head_dim)
-        kf[rows, :] = key_feat
+    rows = normed.shape[0]
+    store_proj(pad, normed[...], weights, PAD)
+    key = convolve(pad, taps, 1, 0, tiles, PAD, rows)
+    value = convolve(pad, taps, 2, tiles, tiles, PAD, rows)
+    val[...] = value
+    key_feat = features(key, diag, ones, heads)
+    kf[...] = key_feat
+    for b in range(rows // SUB):
+        sub = slice(b * SUB, (b + 1) * SUB)
         before[b] = total[...]
         for pair in range(heads // 2):
-            vp = value[:, pair * 2 * head_dim : (pair + 1) * 2 * head_dim]
-            kp = key_feat[:, pair * 2 * feat : (pair + 1) * 2 * feat]
+            vp = value[sub, pair * 2 * head_dim : (pair + 1) * 2 * head_dim]
+            kp = key_feat[sub, pair * 2 * feat : (pair + 1) * 2 * feat]
             both = dot(vp, kp, TN)
             for side in range(2):
                 h = pair * 2 + side
                 total[h * head_dim : (h + 1) * head_dim, :] += both[
                     side * head_dim : (side + 1) * head_dim, side * feat : (side + 1) * feat
                 ]
-        sums = jnp.sum(key_feat.astype(F32), 0, keepdims=True)
+        sums = jnp.sum(key_feat[sub].astype(F32), 0, keepdims=True)
         for h in range(heads):
             at = heads * head_dim + h
             total[at : at + 1, :] += sums[:, h * feat : (h + 1) * feat]
@@ -201,34 +190,32 @@
     sc, after, normed, nrim, weight, taps, diag, ones, kf, val, qf, out, pad, *, heads
 ):
     del after
-    tiles = weight.shape[2] // LANES
+    rows = normed.shape[0]
     feat = qf.shape[1] // heads
     width = val.shape[1] // heads
     row = lax.broadcasted_iota(jnp.int32, (SUB, SUB), 0)
     col = lax.broadcasted_iota(jnp.int32, (SUB, SUB), 1)
     causal = row >= col
-    left = lax.broadcasted_iota(jnp.int32, (SUB, 2 * width), 1) < width
-    one, zero = jnp.ones((SUB, 2 * width), BF16), jnp.zeros((SUB, 2 * width), BF16)
+    left = (lax.broadcasted_iota(jnp.int32, (SUB, 4 * width), 1) & (2 * width - 1)) < width
+    one = jnp.ones((SUB, 2 * width), BF16)
     rim_rows(pad, nrim[...], (weight[0],), (sc[1] > 0).astype(F32))
-    for b in range(normed.shape[0] // SUB):
-        rows = slice(b * SUB, (b + 1) * SUB)
-        start = PAD + b * SUB
-        store_proj(pad, normed[rows, :], (weight[0],), start)
-        query = convolve(pad, taps, 0, 0, tiles, start, SUB)
-        query_feat = features(query, diag, ones, width)
-        qf[rows, :] = query_feat
+    store_proj(pad, normed[...], (weight[0],), PAD)
+    query = convolve(pad, taps, 0, 0, weight.shape[2] // LANES, PAD, rows)
+    query_feat = features(query, diag, ones, heads)
+    qf[...] = query_feat
+    for b in range(rows // SUB):
+        sub = slice(b * SUB, (b + 1) * SUB)
         for pair in range(heads // 2):
-            vp = val[rows, pair * 2 * width : (pair + 1) * 2 * width]
-            total = None
-            for side in range(2):
-                at = slice((pair * 2 + side) * feat, (pair * 2 + side + 1) * feat)
-                mine = left if side == 0 else ~left
-                scores = dot(query_feat[:, at], kf[rows, at], NT)
-                weights = jnp.where(causal, scores, 0.0).astype(BF16)
-                rhs = jnp.concatenate([jnp.where(mine, vp, zero), jnp.where(mine, one, zero)], 1)
-                term = dot(weights, rhs)
-                total = term if total is None else total + term
-            out[rows, pair * 4 * width : (pair + 1) * 4 * width] = total
+            weights = []
+            for h in (2 * pair, 2 * pair + 1):
+                at = slice(h * feat, (h + 1) * feat)
+                scores = dot(query_feat[sub, at], kf[sub, at], NT)
+                weights.append(jnp.where(causal, scores, 0.0).astype(BF16))
+            vp = val[sub, pair * 2 * width : (pair + 1) * 2 * width]
+            both = dot(jnp.concatenate(weights, 0), jnp.concatenate([vp, one], 1))
+            out[sub, pair * 4 * width : (pair + 1) * 4 * width] = jnp.where(
+                left, both[:SUB], both[SUB:]
+            )
 
 
 def attend(qf, local, before, state_in, b, heads):
@@ -264,19 +251,25 @@
 
 
 def own_kernel(qf, local, before, state, weight, out, *, heads):
-    for b in range(qf.shape[0] // SUB):
-        out[b * SUB : (b + 1) * SUB, :] = dot(
-            attend(qf, local, before, state[...], b, heads), weight[...]
-        )
+    attended = [
+        attend(qf, local, before, state[...], b, heads) for b in range(qf.shape[0] // SUB)
+    ]
+    out[...] = dot(jnp.concatenate(attended, 0), weight[...])
 
 
 def last_kernel(qf, local, before, state, weight, partial, out, buf, sem, *, heads):
     copies = []
-    for b in range(qf.shape[0] // SUB):
-        rows = slice(b * SUB, (b + 1) * SUB)
-        attended = attend(qf, local, before, state[...].astype(F32), b, heads)
-        buf[b] = (partial[rows, :] + dot(attended, weight[...])).astype(BF16)
-        copies.append(pltpu.make_async_copy(buf.at[b], out.at[pl.ds(b * SUB, SUB), :], sem.at[b]))
+    state_in = state[...].astype(F32)
+    per = buf.shape[1] // SUB
+    for s in range(buf.shape[0]):
+        attended = [
+            attend(qf, local, before, state_in, s * per + b, heads) for b in range(per)
+        ]
+        rows = slice(s * per * SUB, (s + 1) * per * SUB)
+        buf[s] = (partial[rows, :] + dot(jnp.concatenate(attended, 0), weight[...])).astype(BF16)
+        copies.append(
+            pltpu.make_async_copy(buf.at[s], out.at[pl.ds(s * per * SUB, per * SUB), :], sem.at[s])
+        )
         copies[-1].start()
     for copy in copies:
         copy.wait()
@@ -335,43 +328,37 @@
     devices = lax.axis_size("tm")
     smem, hbm = pltpu.SMEM, pltpu.HBM
 
+    sc = jnp.stack([rep, 2 * place + rep]).astype(jnp.int32)
+    flags = jnp.stack([rep > 0, *earlier("tm")]).astype(F32)
+    masks = jnp.broadcast_to(flags[:, None], (flags.size, feat))
+    sc, masks, signal, embed_weight, norm_gain, qkv_weight, conv_weight, feature_weight = (
+        lax.optimization_barrier(
+            (sc, masks, signal, embed_weight, norm_gain, qkv_weight, conv_weight, feature_weight)
+        )
+    )
+    second, masks = masks[:1] > 0, masks[1:]
     ew_other = swap(embed_weight, "rep", 1)
+    (far_rim,) = call(
+        rim_kernel,
+        [(sc, smem), (signal, hbm)],
+        [((RIM, depth), BF16, None)],
+        "rim",
+        [pltpu.SemaphoreType.DMA],
+        (1 << 30, 1 << 20),
+    )
+    far_rim = lax.ppermute(far_rim, "tm", [(i, (i + 1) % devices) for i in range(devices)])
     wqkv = [qkv_weight.transpose(1, 0, 2), swap(qkv_weight.transpose(1, 0, 2), "rep", 1)]
     taps = [conv_weight.transpose(1, 0, 2), swap(conv_weight.transpose(1, 0, 2), "rep", 1)]
     feat_w = [feature_weight, swap(feature_weight, "rep", 1)]
-    sc = jnp.stack([rep, 2 * place + rep]).astype(jnp.int32)
-    flags = jnp.stack([rep > 0, *earlier("tm")]).astype(F32)
-    sc, masks = lax.optimization_barrier((sc, jnp.broadcast_to(flags[:, None], (flags.size, feat))))
-    second, masks = masks[:1] > 0, masks[1:]
     gain = norm_gain.reshape(1, width)
 
-    partial, sig_other, near_rim, _, ew_own, gain = call(
-        embed_own_kernel,
-        [(sc, smem), (signal, hbm), (embed_weight, hbm), (gain, hbm)],
-        [
-            ((rows, width), F32, None),
-            ((rows, half), BF16, None),
-            ((RIM, depth), BF16, None),
-            ((RIM, depth), BF16, None),
-            ((half, width), BF16, None),
-            ((1, width), F32, None),
-        ],
-        "embed_own",
-        [
-            pltpu.VMEM((blocks, SUB, half), BF16),
-            pltpu.SemaphoreType.DMA((blocks,)),
-            pltpu.SemaphoreType.DMA((5,)),
-        ],
-        (2 * rows * half * width, 4 << 20),
-    )
-    far_rim = lax.ppermute(signal[2 * rows - RIM :], "tm", [(i, (i + 1) % devices) for i in range(devices)])
-    normed, ew_own = call(
-        embed_other_kernel,
-        vmem(partial, sig_other, ew_own, ew_other, gain),
-        [((rows, width), BF16, None), ((half, width), BF16, None)],
-        "embed_other",
+    normed, near_rim = call(
+        embed_kernel,
+        [(sc, smem), *vmem(signal, embed_weight, ew_other, gain)],
+        [((rows, width), BF16, None), ((RIM, depth), BF16, None)],
+        "embed",
         (),
-        (8, 8),
+        (2 * rows * depth * width, 4 << 20),
     )
 
     key_outs = [
@@ -380,7 +367,7 @@
         ((blocks, states, feat), F32, None),
         ((states, feat), F32, None),
         ((cols, feats), BF16, None),
-        ((cols, feats), BF16, None),
+        ((cols, LANES), BF16, None),
     ]
     pads = pltpu.VMEM((2 * cols // LANES, PAD + rows, LANES), F32)
     key_work = (6 * rows * width * 2 * cols, 4 << 20)
@@ -388,7 +375,7 @@
         first_key_kernel,
         [
             (sc, smem),
-            *vmem(far_rim, near_rim, ew_own, ew_other, gain, normed),
+            *vmem(far_rim, near_rim, embed_weight, ew_other, gain, normed),
             *vmem(wqkv[1], taps[1], feat_w[1]),
         ],
         [((RIM, width), BF16, None), *key_outs],
@@ -436,7 +423,7 @@
         vmem(qf[1], local[1], other[2], state_other, ow[1], partial),
         [((rows, width), BF16, hbm)],
         "attend_other",
-        [pltpu.VMEM((blocks, SUB, width), BF16), pltpu.SemaphoreType.DMA((blocks,))],
+        [pltpu.VMEM((2, rows // 2, width), BF16), pltpu.SemaphoreType.DMA((2,))],
         (4 * rows * width * cols, 4 << 20),
     )[0]
 

time: 35.4 us -> 33.2 us (0.938)
  Pallas kernels: 22.3 us -> 18.5 us
  waiting for transfers between devices: 1.93 us -> 4.47 us
  local copies, waits for them, and re-layouts: 0.95 us -> 0.2 us
    pallas_call x8, Pallas kernels: 22.3 us -> 18.5 us  [call(): pl.pallas_call(kernel, in_specs=[spec(p) for _, p in ins], out_specs=[spe...]
    ppermute x1, waiting for transfers between devices: 0.09 us -> 2.36 us  [shards(): lax.ppermute(far_rim, 'tm', [(i, (i + 1) % devices) for i in range(device...]
    slice x1 -> x0, local copies, waits for them, and re-layouts: 0.76 us -> none  [shards(): signal[2 * rows - RIM:]]
  transfers between devices with their start and end apart: 12 -> 12, of which waited for: 4 -> 4; matrix products, arithmetic and copies ran while one was open for 3% -> 1% of each run, Pallas kernels for 47% -> 42%
where the time goes in v3:
time: 33.2 us; the launch traced here: 33 us
  Pallas kernels  18.5 us (56%)
  starting transfers between devices  9.35 us (28%)
  waiting for transfers between devices  4.47 us (13%)
    pallas_call x8, Pallas kernels, call(): pl.pallas_call(kernel, in_specs=[spec(p) for _, p in ins], out_specs=[spe...  18.5 us
    ppermute x11, starting transfers between devices, swap(): return lax.ppermute(array, axis, [(i, i ^ by) for i in range(devices)])  6.97 us
    ppermute x1, starting transfers between devices, shards(): lax.ppermute(far_rim, 'tm', [(i, (i + 1) % devices) for i in range(device...  2.38 us
    ppermute x1, waiting for transfers between devices, shards(): lax.ppermute(far_rim, 'tm', [(i, (i + 1) % devices) for i in range(device...  2.36 us
    ppermute x11, waiting for transfers between devices, swap(): return lax.ppermute(array, axis, [(i, i ^ by) for i in range(devices)])  2.11 us
  transfers between devices with their start and end apart: 12, of which 4 were waited for; matrix products, arithmetic and copies ran while one was open for 1% of the time, Pallas kernels for 42%

profile of v3, /device:TPU:0, one launch (start us, length us, event | category | flops | bytes accessed | tf_op | source)
XLA Modules:
  0.0 33.0 jit_solution(3939211232942075048)
XLA Ops:
  0.0 0.1 stack.35
  0.1 0.1 pad_add_fusion.sc
  0.2 0.1 broadcast_in_dim.60
  0.3 0.0 copy-start.5
  0.3 0.5 %collective-permute-start = (bf16[512,512]{1,0:T(8,128)(2,1)}, bf16[512,512]{1,0:T(8,128)(2,1)S(1)}, u32[]{:S(2)}, u32[]{:S(2)}) collective-permute-start(bf16[512,512]{1,0:T(8,128)(2,1)} %ew_a.1), channel_id=1, source_target_pairs={{0,1},{1,0},{2,3},{3,2},{4,5},{5,4},{6,7},{7,6},{8,9},{9,8},{10,11... | collective-permute-start | bytes 1572872 | tf_op jit(solution)/shard_map/ppermute | solution.py:280
  0.8 1.8 %rim.1 = bf16[16,1024]{1,0:T(8,128)(2,1)S(1)} custom-call(s32[2]{0:T(128)S(1)} %pad_add_fusion.sc, bf16[2048,1024]{1,0:T(8,128)(2,1)} %sig.1), custom_call_target="tpu_custom_call" | custom-call | flops 8589934592 | bytes 1048576 | tf_op jit(solution)/shard_map/rim/pallas_call | solution.py:36
  2.6 2.4 %collective-permute-start.1 = (bf16[16,1024]{1,0:T(8,128)(2,1)S(1)}, bf16[16,1024]{1,0:T(8,128)(2,1)S(1)}, u32[]{:S(2)}, u32[]{:S(2)}) collective-permute-start(bf16[16,1024]{1,0:T(8,128)(2,1)S(1)} %rim.1), channel_id=1, source_target_pairs={{0,2},{2,4},{4,6},{6,8},{8,10},{10,12},{12,14},{14,0},{1,3},{3,5},... | collective-permute-start | bytes 98312 | tf_op jit(solution)/shard_map/ppermute | solution.py:349
  5.0 0.3 collective-permute-start.2
  5.3 0.2 collective-permute-start.3
  5.5 0.3 collective-permute-start.4
  5.9 1.9 %embed.1 = (bf16[1024,512]{1,0:T(8,128)(2,1)S(1)}, bf16[16,1024]{1,0:T(8,128)(2,1)S(1)}) custom-call(s32[2]{0:T(128)S(1)} %pad_add_fusion.sc, bf16[2048,1024]{1,0:T(8,128)(2,1)S(1)} %copy-done, bf16[512,512]{1,0:T(8,128)(2,1)S(1)} %copy-done.2, bf16[512,512]{1,0:T(8,128)(2,1)S(1)} %collective-permute-done.ew_b, f32[1,512]{1,0:T(1,128)S(1)} %bitcast.26), custom_call_target="tpu_custom_call" | custom-call | flops 8589934592 | bytes 4194304 | tf_op jit(solution)/shard_map/embed/pallas_call | solution.py:36
  7.8 2.4 %collective-permute-done.1.far_rim = bf16[16,1024]{1,0:T(8,128)(2,1)S(1)} collective-permute-done((bf16[16,1024]{1,0:T(8,128)(2,1)S(1)}, bf16[16,1024]{1,0:T(8,128)(2,1)S(1)}, u32[]{:S(2)}, u32[]{:S(2)}) %collective-permute-start.1) | collective-permute-done | bytes 32800 | tf_op jit(solution)/shard_map/ppermute | solution.py:349
  10.2 0.0 collective-permute-done.2.weight
  10.2 3.3 %keys_other.1 = (bf16[16,512]{1,0:T(8,128)(2,1)S(1)}, bf16[1024,512]{1,0:T(8,128)(2,1)S(1)}, bf16[1024,256]{1,0:T(8,128)(2,1)S(1)}, f32[4,272,128]{2,1,0:T(8,128...) custom-call(s32[2]{0:T(128)S(1)} %pad_add_fusion.sc, ...), custom_call_target="tpu_custom_call" | custom-call | flops 12884901888 | bytes 4194304 | tf_op jit(solution)/shard_map/keys_other/pallas_call | solution.py:36
  13.5 0.1 collective-permute-start.5
  13.5 3.0 %keys_own.1 = (bf16[1024,512]{1,0:T(8,128)(2,1)S(1)}, bf16[1024,256]{1,0:T(8,128)(2,1)S(1)}, f32[4,272,128]{2,1,0:T(8,128)S(1)}, f32[272,128]{1,0:T(8,128)S(1)},...) custom-call(s32[2]{0:T(128)S(1)} %pad_add_fusion.sc, ...), custom_call_target="tpu_custom_call" | custom-call | flops 12884901888 | bytes 4194304 | tf_op jit(solution)/shard_map/keys_own/pallas_call | solution.py:36
  16.5 0.6 %collective-permute-start.11 = (bf16[256,512]{1,0:T(8,128)(2,1)S(1)}, bf16[256,512]{1,0:T(8,128)(2,1)S(1)}, u32[]{:S(2)}, u32[]{:S(2)}) collective-permute-start(bf16[256,512]{1,0:T(8,128)(2,1)S(1)} %get-tuple-element.53.weight), channel_id=1, source_target_pairs={{0,1},{1,0},{2,3},{3,2},{4,5},{5,4},{6,7},{7,6},{8,9},{9,8},{10,11... | collective-permute-start | bytes 786440 | tf_op jit(solution)/shard_map/ppermute | solution.py:280
  17.1 0.0 collective-permute-done.5
  17.1 0.1 collective-permute-start.6
  17.2 0.8 %collective-permute-start.7 = (bf16[272,128]{1,0:T(8,128)(2,1)S(1)}, bf16[272,128]{1,0:T(8,128)(2,1)S(1)}, u32[]{:S(2)}, u32[]{:S(2)}) collective-permute-start(bf16[272,128]{1,0:T(8,128)(2,1)S(1)} %fusion.5.after), channel_id=1, source_target_pairs={{0,4},{2,6},{4,0},{6,2},{8,12},{10,14},{12,8},{14,10},{1,5},{3,7},... | collective-permute-start | bytes 208904 | tf_op jit(solution)/shard_map/ppermute | solution.py:280
  18.0 2.7 %collective-permute-start.8 = (bf16[272,128]{1,0:T(8,128)(2,1)S(1)}, bf16[272,128]{1,0:T(8,128)(2,1)S(1)}, u32[]{:S(2)}, u32[]{:S(2)}) collective-permute-start(bf16[272,128]{1,0:T(8,128)(2,1)S(1)} %fusion.5.after), channel_id=1, source_target_pairs={{0,6},{2,4},{4,2},{6,0},{8,14},{10,12},{12,10},{14,8},{1,7},{3,5},... | collective-permute-start | bytes 208904 | tf_op jit(solution)/shard_map/ppermute | solution.py:280
  20.7 3.1 %queries.3 = (bf16[1024,512]{1,0:T(8,128)(2,1)S(1)}, f32[1024,512]{1,0:T(8,128)S(1)}) custom-call(s32[2]{0:T(128)S(1)} %pad_add_fusion.sc, bf16[272,128]{1,0:T(8,128)(2,1)S(1)} %fusion.5.after, bf16[1024,512]{1,0:T(8,128)(2,1)S(1)} %get-tuple-element.37.normed, bf16[16,512]{1,0:T(8,128)(2,1)S(1)} %get-tuple-element.42.nrim, ...), custom_call_target="tpu_custom_call" | custom-call | flops 6442450944 | bytes 4194304 | tf_op jit(solution)/shard_map/queries/pallas_call | solution.py:36
  23.8 0.2 collective-permute-done.8
  24.0 0.1 fusion.4.after
  24.0 1.4 %collective-permute-start.9 = (bf16[272,128]{1,0:T(8,128)(2,1)S(1)}, bf16[272,128]{1,0:T(8,128)(2,1)S(1)}, u32[]{:S(2)}, u32[]{:S(2)}) collective-permute-start(bf16[272,128]{1,0:T(8,128)(2,1)S(1)} %fusion.4.after), channel_id=1, source_target_pairs={{0,8},{2,10},{4,12},{6,14},{8,0},{10,2},{12,4},{14,6},{1,9},{3,11}... | collective-permute-start | bytes 208904 | tf_op jit(solution)/shard_map/ppermute | solution.py:280
  25.5 3.1 %queries.2 = (bf16[1024,512]{1,0:T(8,128)(2,1)S(1)}, f32[1024,512]{1,0:T(8,128)S(1)}) custom-call(s32[2]{0:T(128)S(1)} %pad_add_fusion.sc, bf16[272,128]{1,0:T(8,128)(2,1)S(1)} %fusion.4.after, bf16[1024,512]{1,0:T(8,128)(2,1)S(1)} %get-tuple-element.37.normed, bf16[16,512]{1,0:T(8,128)(2,1)S(1)} %get-tuple-element.42.nrim, ...), custom_call_target="tpu_custom_call" | custom-call | flops 6442450944 | bytes 4194304 | tf_op jit(solution)/shard_map/queries/pallas_call | solution.py:36
  28.5 1.5 %collective-permute-done.9 = bf16[272,128]{1,0:T(8,128)(2,1)S(1)} collective-permute-done((bf16[272,128]{1,0:T(8,128)(2,1)S(1)}, bf16[272,128]{1,0:T(8,128)(2,1)S(1)}, u32[]{:S(2)}, u32[]{:S(2)}) %collective-permute-start.9) | collective-permute-done | bytes 69664 | tf_op jit(solution)/shard_map/ppermute | solution.py:280
  30.0 0.1 fusion
  30.1 0.1 collective-permute-start.10
  30.2 0.8 %attend_own.1.partial = f32[1024,512]{1,0:T(8,128)S(1)} custom-call(bf16[1024,512]{1,0:T(8,128)(2,1)S(1)} %get-tuple-element.58.qf, f32[1024,512]{1,0:T(8,128)S(1)} %get-tuple-element.59.local, f32[4,272,128]{2,1,0:T(8,128)S(1)} %get-tuple-element.60.before, f32[272,128]{1,0:T(8,128)S(1)} %get-tuple-element.61.state, ...), custom_call_target="tpu_custom_call" | custom-call | flops 4294967296 | bytes 4194304 | tf_op jit(solution)/shard_map/attend_own/pallas_call | solution.py:36
  31.0 0.5 %collective-permute-done.10.state = bf16[272,128]{1,0:T(8,128)(2,1)S(1)} collective-permute-done((bf16[272,128]{1,0:T(8,128)(2,1)S(1)}, bf16[272,128]{1,0:T(8,128)(2,1)S(1)}, u32[]{:S(2)}, u32[]{:S(2)}) %collective-permute-start.10) | collective-permute-done | bytes 69664 | tf_op jit(solution)/shard_map/ppermute | solution.py:280
  31.4 1.6 %attend_other.1 = bf16[1024,512]{1,0:T(8,128)(2,1)} custom-call(bf16[1024,512]{1,0:T(8,128)(2,1)S(1)} %get-tuple-element.49.qf, f32[1024,512]{1,0:T(8,128)S(1)} %get-tuple-element.50.local, f32[4,272,128]{2,1,0:T(8,128)S(1)} %get-tuple-element.51.before, bf16[272,128]{1,0:T(8,128)(2,1)S(1)} %collective-permute-done.10.state, ...), custom_call_target="tpu_custom_call" | custom-call | flops 4294967296 | bytes 4194304 | tf_op jit(solution)/shard_map/attend_other/pallas_call | solution.py:36
  (21 shorter events, 0.1 us)
Async XLA Ops:
  0.3 4.8 %copy-start.1 = (bf16[512,3,256]{2,0,1:T(8,128)(2,1)S(1)}, bf16[512,3,256]{2,0,1:T(8,128)(2,1)}, u32[]{:S(2)}) copy-start(bf16[512,3,256]{2,0,1:T(8,128)(2,1)} %param.10) | copy-start | bytes 2359300
  0.3 5.0 %copy-start.4 = (f32[4,3,256]{2,0,1:T(4,128)S(1)}, f32[4,3,256]{2,0,1:T(4,128)}, u32[]{:S(2)}) copy-start(f32[4,3,256]{2,0,1:T(4,128)} %param.11) | copy-start | bytes 36868
  0.3 5.3 %copy-start.3 = (bf16[4,64,128]{2,1,0:T(8,128)(2,1)S(1)}, bf16[4,64,128]{2,1,0:T(8,128)(2,1)}, u32[]{:S(2)}) copy-start(bf16[4,64,128]{2,1,0:T(8,128)(2,1)} %feat_w) | copy-start | bytes 196612
  0.3 5.6 %copy-start = (bf16[2048,1024]{1,0:T(8,128)(2,1)S(1)}, bf16[2048,1024]{1,0:T(8,128)(2,1)}, u32[]{:S(2)}) copy-start(bf16[2048,1024]{1,0:T(8,128)(2,1)} %sig.1) | copy-start | bytes 12582916
  0.3 5.6 %copy-start.2 = (bf16[512,512]{1,0:T(8,128)(2,1)S(1)}, bf16[512,512]{1,0:T(8,128)(2,1)}, u32[]{:S(2)}) copy-start(bf16[512,512]{1,0:T(8,128)(2,1)} %ew_a.1) | copy-start | bytes 1572868
  0.3 5.6 %copy-start.5 = (f32[512]{0:T(512)S(1)}, f32[512]{0:T(512)}, u32[]{:S(2)}) copy-start(f32[512]{0:T(512)} %param.9) | copy-start | bytes 6148
  0.3 5.5 %collective-permute-start = (bf16[512,512]{1,0:T(8,128)(2,1)}, bf16[512,512]{1,0:T(8,128)(2,1)S(1)}, u32[]{:S(2)}, u32[]{:S(2)}) collective-permute-start(bf16[512,512]{1,0:T(8,128)(2,1)} %ew_a.1), channel_id=1, source_target_pairs={{0,1},{1,0},{2,3},{3,2},{4,5},{5,4},{6,7},{7,6},{8,9},{9,8},{10,11... | collective-permute-start | bytes 1572872 | tf_op jit(solution)/shard_map/ppermute | solution.py:280
  2.6 7.5 %collective-permute-start.1 = (bf16[16,1024]{1,0:T(8,128)(2,1)S(1)}, bf16[16,1024]{1,0:T(8,128)(2,1)S(1)}, u32[]{:S(2)}, u32[]{:S(2)}) collective-permute-start(bf16[16,1024]{1,0:T(8,128)(2,1)S(1)} %rim.1), channel_id=1, source_target_pairs={{0,2},{2,4},{4,6},{6,8},{8,10},{10,12},{12,14},{14,0},{1,3},{3,5},... | collective-permute-start | bytes 98312 | tf_op jit(solution)/shard_map/ppermute | solution.py:349
  5.0 5.2 %collective-permute-start.2 = (bf16[3,512,256]{2,1,0:T(8,128)(2,1)S(1)}, bf16[3,512,256]{2,1,0:T(8,128)(2,1)S(1)}, u32[]{:S(2)}, u32[]{:S(2)}) collective-permute-start(bf16[3,512,256]{2,1,0:T(8,128)(2,1)S(1)} %bitcast.20), channel_id=1, source_target_pairs={{0,1},{1,0},{2,3},{3,2},{4,5},{5,4},{6,7},{7,6},{8,9},{9,8},{10,11... | collective-permute-start | bytes 2359304 | tf_op jit(solution)/shard_map/ppermute | solution.py:280
  5.3 2.5 %collective-permute-start.3 = (f32[3,4,256]{2,1,0:T(4,128)S(1)}, f32[3,4,256]{2,1,0:T(4,128)S(1)}, u32[]{:S(2)}, u32[]{:S(2)}) collective-permute-start(f32[3,4,256]{2,1,0:T(4,128)S(1)} %bitcast.23), channel_id=1, source_target_pairs={{0,1},{1,0},{2,3},{3,2},{4,5},{5,4},{6,7},{7,6},{8,9},{9,8},{10,11... | collective-permute-start | bytes 36872 | tf_op jit(solution)/shard_map/ppermute | solution.py:280
  5.5 4.6 %collective-permute-start.4 = (bf16[4,64,128]{2,1,0:T(8,128)(2,1)S(1)}, bf16[4,64,128]{2,1,0:T(8,128)(2,1)S(1)}, u32[]{:S(2)}, u32[]{:S(2)}) collective-permute-start(bf16[4,64,128]{2,1,0:T(8,128)(2,1)S(1)} %copy-done.3), channel_id=1, source_target_pairs={{0,1},{1,0},{2,3},{3,2},{4,5},{5,4},{6,7},{7,6},{8,9},{9,8},{10,11... | collective-permute-start | bytes 196616 | tf_op jit(solution)/shard_map/ppermute | solution.py:280
  13.5 3.6 %collective-permute-start.5 = (bf16[272,128]{1,0:T(8,128)(2,1)S(1)}, bf16[272,128]{1,0:T(8,128)(2,1)S(1)}, u32[]{:S(2)}, u32[]{:S(2)}) collective-permute-start(bf16[272,128]{1,0:T(8,128)(2,1)S(1)} %convert_element_type.35), channel_id=1, source_target_pairs={{0,1},{1,0},{2,3},{3,2},{4,5},{5,4},{6,7},{7,6},{8,9},{9,8},{10,11... | collective-permute-start | bytes 208904 | tf_op jit(solution)/shard_map/ppermute | solution.py:280
  16.5 14.4 %collective-permute-start.11 = (bf16[256,512]{1,0:T(8,128)(2,1)S(1)}, bf16[256,512]{1,0:T(8,128)(2,1)S(1)}, u32[]{:S(2)}, u32[]{:S(2)}) collective-permute-start(bf16[256,512]{1,0:T(8,128)(2,1)S(1)} %get-tuple-element.53.weight), channel_id=1, source_target_pairs={{0,1},{1,0},{2,3},{3,2},{4,5},{5,4},{6,7},{7,6},{8,9},{9,8},{10,11... | collective-permute-start | bytes 786440 | tf_op jit(solution)/shard_map/ppermute | solution.py:280
  17.1 6.7 %collective-permute-start.6 = (bf16[272,128]{1,0:T(8,128)(2,1)S(1)}, bf16[272,128]{1,0:T(8,128)(2,1)S(1)}, u32[]{:S(2)}, u32[]{:S(2)}) collective-permute-start(bf16[272,128]{1,0:T(8,128)(2,1)S(1)} %fusion.5.after), channel_id=1, source_target_pairs={{0,2},{2,0},{4,6},{6,4},{8,10},{10,8},{12,14},{14,12},{1,3},{3,1},... | collective-permute-start | bytes 208904 | tf_op jit(solution)/shard_map/ppermute | solution.py:280
  17.2 6.6 %collective-permute-start.7 = (bf16[272,128]{1,0:T(8,128)(2,1)S(1)}, bf16[272,128]{1,0:T(8,128)(2,1)S(1)}, u32[]{:S(2)}, u32[]{:S(2)}) collective-permute-start(bf16[272,128]{1,0:T(8,128)(2,1)S(1)} %fusion.5.after), channel_id=1, source_target_pairs={{0,4},{2,6},{4,0},{6,2},{8,12},{10,14},{12,8},{14,10},{1,5},{3,7},... | collective-permute-start | bytes 208904 | tf_op jit(solution)/shard_map/ppermute | solution.py:280
  18.0 6.0 %collective-permute-start.8 = (bf16[272,128]{1,0:T(8,128)(2,1)S(1)}, bf16[272,128]{1,0:T(8,128)(2,1)S(1)}, u32[]{:S(2)}, u32[]{:S(2)}) collective-permute-start(bf16[272,128]{1,0:T(8,128)(2,1)S(1)} %fusion.5.after), channel_id=1, source_target_pairs={{0,6},{2,4},{4,2},{6,0},{8,14},{10,12},{12,10},{14,8},{1,7},{3,5},... | collective-permute-start | bytes 208904 | tf_op jit(solution)/shard_map/ppermute | solution.py:280
  24.0 6.0 %collective-permute-start.9 = (bf16[272,128]{1,0:T(8,128)(2,1)S(1)}, bf16[272,128]{1,0:T(8,128)(2,1)S(1)}, u32[]{:S(2)}, u32[]{:S(2)}) collective-permute-start(bf16[272,128]{1,0:T(8,128)(2,1)S(1)} %fusion.4.after), channel_id=1, source_target_pairs={{0,8},{2,10},{4,12},{6,14},{8,0},{10,2},{12,4},{14,6},{1,9},{3,11}... | collective-permute-start | bytes 208904 | tf_op jit(solution)/shard_map/ppermute | solution.py:280
  30.1 1.3 %collective-permute-start.10 = (bf16[272,128]{1,0:T(8,128)(2,1)S(1)}, bf16[272,128]{1,0:T(8,128)(2,1)S(1)}, u32[]{:S(2)}, u32[]{:S(2)}) collective-permute-start(bf16[272,128]{1,0:T(8,128)(2,1)S(1)} %get-tuple-element.62), channel_id=1, source_target_pairs={{0,1},{1,0},{2,3},{3,2},{4,5},{5,4},{6,7},{7,6},{8,9},{9,8},{10,11... | collective-permute-start | bytes 208904 | tf_op jit(solution)/shard_map/ppermute | solution.py:280

commit v4 on v3

--- a/solution.py
+++ b/solution.py
@@ -54,15 +54,15 @@
     return (emb * lax.rsqrt(mean + EPS) * gain).astype(BF16)
 
 
-def rim_kernel(sc, sig, rim, sem):
-    del sc
+def rim_kernel(after, sig, rim, sem):
+    del after
     copy = pltpu.make_async_copy(sig.at[pl.ds(sig.shape[0] - RIM, RIM), :], rim, sem)
     copy.start()
     copy.wait()
 
 
-def embed_kernel(sc, sig, ew_a, ew_b, gain, normed, near_rim):
-    rep = sc[0]
+def embed_kernel(sig, ew_a, ew_b, gain, normed, near_rim):
+    rep = lax.axis_index("rep")
     rows = normed.shape[0]
     half = ew_a.shape[0]
     own = pl.ds(pl.multiple_of(rep * half, half), half)
@@ -113,7 +113,8 @@
     return jnp.concatenate(out, 1)
 
 
-def rim_rows(pad, nrim, weights, keep):
+def rim_rows(pad, nrim, weights, masks):
+    keep = masks[1:2, : weights[0].shape[1]]
     c = 0
     for w in weights:
         proj = dot(nrim, w).astype(BF16).astype(F32) * keep
@@ -122,7 +123,7 @@
             c += 1
 
 
-def key_body(sc, normed, nrim, weight, taps, feat_w, kf, val, before, total, diag, ones, pad):
+def key_body(masks, normed, nrim, weight, taps, feat_w, kf, val, before, total, diag, ones, pad):
     heads, head_dim, feat = feat_w.shape
     cols = val.shape[1]
     tiles = cols // LANES
@@ -134,7 +135,7 @@
     for h in range(heads):
         diag[h * head_dim : (h + 1) * head_dim, h * feat : (h + 1) * feat] = feat_w[h]
     weights = (weight[1], weight[2])
-    rim_rows(pad, nrim, weights, (sc[1] > 0).astype(F32))
+    rim_rows(pad, nrim, weights, masks)
     total[...] = jnp.zeros_like(total)
     rows = normed.shape[0]
     store_proj(pad, normed[...], weights, PAD)
@@ -162,32 +163,36 @@
 
 
 def first_key_kernel(
-    sc, far_rim, near_rim, ew_a, ew_b, gain, normed, weight, taps, feat_w,
+    masks, far_rim, near_rim, ew_a, ew_b, gain, normed, weight, taps, feat_w,
     nrim, kf, val, before, total, diag, ones, pad,
 ):
     half = ew_a.shape[0]
-    own = sc[0] == 0
-    rim = jnp.where(own, far_rim[...].astype(F32), near_rim[...].astype(F32))
+    own = jnp.broadcast_to(masks[0:1, :], (RIM, half)) == 0
+    far, near = far_rim[...].astype(F32), near_rim[...].astype(F32)
+    rim = jnp.concatenate(
+        [jnp.where(own, far[:, :half], near[:, :half]), jnp.where(own, far[:, half:], near[:, half:])],
+        1,
+    )
     lo, hi = rim[:, :half], rim[:, half:]
     mine = jnp.where(own, lo, hi).astype(BF16)
     other = jnp.where(own, hi, lo).astype(BF16)
     rows_n = normalize(dot(mine, ew_a[...]) + dot(other, ew_b[...]), gain[...])
     nrim[...] = rows_n
-    key_body(sc, normed, rows_n, weight, taps, feat_w, kf, val, before, total, diag, ones, pad)
+    key_body(masks, normed, rows_n, weight, taps, feat_w, kf, val, before, total, diag, ones, pad)
 
 
 def key_kernel(
-    sc, normed, nrim, weight, taps, feat_w, ow_hbm,
+    masks, normed, nrim, weight, taps, feat_w, ow_hbm,
     kf, val, before, total, diag, ones, ow, pad, sem,
 ):
     copy = pltpu.make_async_copy(ow_hbm, ow, sem)
     copy.start()
-    key_body(sc, normed, nrim[...], weight, taps, feat_w, kf, val, before, total, diag, ones, pad)
+    key_body(masks, normed, nrim[...], weight, taps, feat_w, kf, val, before, total, diag, ones, pad)
     copy.wait()
 
 
 def query_kernel(
-    sc, after, normed, nrim, weight, taps, diag, ones, kf, val, qf, out, pad, *, heads
+    masks, after, normed, nrim, weight, taps, diag, ones, kf, val, qf, out, pad, *, heads
 ):
     del after
     rows = normed.shape[0]
@@ -198,7 +203,7 @@
     causal = row >= col
     left = (lax.broadcasted_iota(jnp.int32, (SUB, 4 * width), 1) & (2 * width - 1)) < width
     one = jnp.ones((SUB, 2 * width), BF16)
-    rim_rows(pad, nrim[...], (weight[0],), (sc[1] > 0).astype(F32))
+    rim_rows(pad, nrim[...], (weight[0],), masks)
     store_proj(pad, normed[...], (weight[0],), PAD)
     query = convolve(pad, taps, 0, 0, weight.shape[2] // LANES, PAD, rows)
     query_feat = features(query, diag, ones, heads)
@@ -326,21 +331,20 @@
     blocks = rows // SUB
     place, rep = lax.axis_index("tm"), lax.axis_index("rep")
     devices = lax.axis_size("tm")
-    smem, hbm = pltpu.SMEM, pltpu.HBM
-
-    sc = jnp.stack([rep, 2 * place + rep]).astype(jnp.int32)
-    flags = jnp.stack([rep > 0, *earlier("tm")]).astype(F32)
-    masks = jnp.broadcast_to(flags[:, None], (flags.size, feat))
-    sc, masks, signal, embed_weight, norm_gain, qkv_weight, conv_weight, feature_weight = (
+    hbm = pltpu.HBM
+
+    flags = jnp.stack([rep > 0, 2 * place + rep > 0, *earlier("tm")]).astype(F32)
+    masks = jnp.broadcast_to(flags[:, None], (flags.size, half))
+    masks, signal, embed_weight, norm_gain, qkv_weight, conv_weight, feature_weight = (
         lax.optimization_barrier(
-            (sc, masks, signal, embed_weight, norm_gain, qkv_weight, conv_weight, feature_weight)
-        )
-    )
-    second, masks = masks[:1] > 0, masks[1:]
+            (masks, signal, embed_weight, norm_gain, qkv_weight, conv_weight, feature_weight)
+        )
+    )
+    second = masks[:1, :feat] > 0
     ew_other = swap(embed_weight, "rep", 1)
     (far_rim,) = call(
         rim_kernel,
-        [(sc, smem), (signal, hbm)],
+        [(masks, None), (signal, hbm)],
         [((RIM, depth), BF16, None)],
         "rim",
         [pltpu.SemaphoreType.DMA],
@@ -354,7 +358,7 @@
 
     normed, near_rim = call(
         embed_kernel,
-        [(sc, smem), *vmem(signal, embed_weight, ew_other, gain)],
+        vmem(signal, embed_weight, ew_other, gain),
         [((rows, width), BF16, None), ((RIM, depth), BF16, None)],
         "embed",
         (),
@@ -374,8 +378,7 @@
     nrim, *other = call(
         first_key_kernel,
         [
-            (sc, smem),
-            *vmem(far_rim, near_rim, embed_weight, ew_other, gain, normed),
+            *vmem(masks, far_rim, near_rim, embed_weight, ew_other, gain, normed),
             *vmem(wqkv[1], taps[1], feat_w[1]),
         ],
         [((RIM, width), BF16, None), *key_outs],
@@ -386,7 +389,7 @@
     back = swap(other[3].astype(BF16), "rep", 1).astype(F32)
     own = call(
         key_kernel,
-        [(sc, smem), *vmem(normed, nrim, wqkv[0], taps[0], feat_w[0]), (out_weight, hbm)],
+        [*vmem(masks, normed, nrim, wqkv[0], taps[0], feat_w[0]), (out_weight, hbm)],
         [*key_outs, (out_weight.shape, BF16, None)],
         "keys_own",
         [pads, pltpu.SemaphoreType.DMA],
@@ -398,7 +401,7 @@
     def query(k, keys, after):
         qf[k], local[k] = call(
             functools.partial(query_kernel, heads=heads),
-            [(sc, smem), *vmem(after, normed, nrim, wqkv[k], taps[k], *keys[4:6], *keys[:2])],
+            [*vmem(masks, after, normed, nrim, wqkv[k], taps[k], *keys[4:6], *keys[:2])],
             [((rows, feats), BF16, None), ((rows, 2 * cols), F32, None)],
             "queries",
             [pltpu.VMEM((cols // LANES, PAD + rows, LANES), F32)],
@@ -406,7 +409,7 @@
         )
 
     covers = [functools.partial(query, 0, own), functools.partial(query, 1, other)]
-    before = prefix(own[3] + back, "tm", masks, covers)
+    before = prefix(own[3] + back, "tm", masks[2:, :feat], covers)
     state_own = before + jnp.where(second, back, 0.0)
     state_other = swap((before + jnp.where(second, 0.0, own[3])).astype(BF16), "rep", 1)
 

time: 33.2 us -> 31.4 us (0.946)
  Pallas kernels: 18.5 us -> 15 us
  waiting for transfers between devices: 4.47 us -> 6.1 us
    pallas_call x8, Pallas kernels: 18.5 us -> 15 us  [call(): pl.pallas_call(kernel, in_specs=[spec(p) for _, p in ins], out_specs=[spe...]
    ppermute x11, waiting for transfers between devices: 2.11 us -> 3.3 us  [swap(): return lax.ppermute(array, axis, [(i, i ^ by) for i in range(devices)])]
    ppermute x1, waiting for transfers between devices: 2.36 us -> 2.81 us  [shards(): lax.ppermute(far_rim, 'tm', [(i, (i + 1) % devices) for i in range(device...]
  transfers between devices with their start and end apart: 12 -> 12, of which waited for: 4 -> 4; matrix products, arithmetic and copies ran while one was open for 1% -> 1% of each run, Pallas kernels for 42% -> 34%
where the time goes in v4:
time: 31.4 us; the launch traced here: 31.2 us
  Pallas kernels  15 us (48%)
  starting transfers between devices  9.52 us (30%)
  waiting for transfers between devices  6.1 us (19%)
    pallas_call x8, Pallas kernels, call(): pl.pallas_call(kernel, in_specs=[spec(p) for _, p in ins], out_specs=[spe...  15 us
    ppermute x11, starting transfers between devices, swap(): return lax.ppermute(array, axis, [(i, i ^ by) for i in range(devices)])  7.07 us
    ppermute x11, waiting for transfers between devices, swap(): return lax.ppermute(array, axis, [(i, i ^ by) for i in range(devices)])  3.3 us
    ppermute x1, waiting for transfers between devices, shards(): lax.ppermute(far_rim, 'tm', [(i, (i + 1) % devices) for i in range(device...  2.81 us
    ppermute x1, starting transfers between devices, shards(): lax.ppermute(far_rim, 'tm', [(i, (i + 1) % devices) for i in range(device...  2.46 us
  transfers between devices with their start and end apart: 12, of which 4 were waited for; matrix products, arithmetic and copies ran while one was open for 1% of the time, Pallas kernels for 34%

profile of v4, /device:TPU:0, one launch (start us, length us, event | category | flops | bytes accessed | tf_op | source)
XLA Modules:
  0.0 31.2 jit_solution(11618129628476096090)
XLA Ops:
  0.0 0.1 stack.27
  0.1 0.1 broadcast_in_dim.60.after.masks
  0.2 0.0 copy-start.2
  0.2 0.0 copy-start.5
  0.2 0.5 %collective-permute-start = (bf16[512,512]{1,0:T(8,128)(2,1)}, bf16[512,512]{1,0:T(8,128)(2,1)S(1)}, u32[]{:S(2)}, u32[]{:S(2)}) collective-permute-start(bf16[512,512]{1,0:T(8,128)(2,1)} %ew_a.1), channel_id=1, source_target_pairs={{0,1},{1,0},{2,3},{3,2},{4,5},{5,4},{6,7},{7,6},{8,9},{9,8},{10,11... | collective-permute-start | bytes 1572872 | tf_op jit(solution)/shard_map/ppermute | solution.py:285
  0.7 1.0 %rim.1 = bf16[16,1024]{1,0:T(8,128)(2,1)S(1)} custom-call(f32[6,512]{1,0:T(8,128)S(1)} %broadcast_in_dim.60.after.masks, bf16[2048,1024]{1,0:T(8,128)(2,1)} %sig.1), custom_call_target="tpu_custom_call" | custom-call | flops 8589934592 | bytes 1048576 | tf_op jit(solution)/shard_map/rim/pallas_call | solution.py:36
  1.8 2.5 %collective-permute-start.1 = (bf16[16,1024]{1,0:T(8,128)(2,1)S(1)}, bf16[16,1024]{1,0:T(8,128)(2,1)S(1)}, u32[]{:S(2)}, u32[]{:S(2)}) collective-permute-start(bf16[16,1024]{1,0:T(8,128)(2,1)S(1)} %rim.1), channel_id=1, source_target_pairs={{0,2},{2,4},{4,6},{6,8},{8,10},{10,12},{12,14},{14,0},{1,3},{3,5},... | collective-permute-start | bytes 98312 | tf_op jit(solution)/shard_map/ppermute | solution.py:353
  4.2 0.4 %collective-permute-start.2 = (bf16[3,512,256]{2,1,0:T(8,128)(2,1)S(1)}, bf16[3,512,256]{2,1,0:T(8,128)(2,1)S(1)}, u32[]{:S(2)}, u32[]{:S(2)}) collective-permute-start(bf16[3,512,256]{2,1,0:T(8,128)(2,1)S(1)} %bitcast.19), channel_id=1, source_target_pairs={{0,1},{1,0},{2,3},{3,2},{4,5},{5,4},{6,7},{7,6},{8,9},{9,8},{10,11... | collective-permute-start | bytes 2359304 | tf_op jit(solution)/shard_map/ppermute | solution.py:285
  4.7 0.1 collective-permute-start.3
  4.8 0.4 %collective-permute-start.4 = (bf16[4,64,128]{2,1,0:T(8,128)(2,1)S(1)}, bf16[4,64,128]{2,1,0:T(8,128)(2,1)S(1)}, u32[]{:S(2)}, u32[]{:S(2)}) collective-permute-start(bf16[4,64,128]{2,1,0:T(8,128)(2,1)S(1)} %copy-done.3), channel_id=1, source_target_pairs={{0,1},{1,0},{2,3},{3,2},{4,5},{5,4},{6,7},{7,6},{8,9},{9,8},{10,11... | collective-permute-start | bytes 196616 | tf_op jit(solution)/shard_map/ppermute | solution.py:285
  5.2 0.0 collective-permute-done.ew_b
  5.3 1.4 %embed.1 = (bf16[1024,512]{1,0:T(8,128)(2,1)S(1)}, bf16[16,1024]{1,0:T(8,128)(2,1)S(1)}) custom-call(bf16[2048,1024]{1,0:T(8,128)(2,1)S(1)} %copy-done, bf16[512,512]{1,0:T(8,128)(2,1)S(1)} %copy-done.2, bf16[512,512]{1,0:T(8,128)(2,1)S(1)} %collective-permute-done.ew_b, f32[1,512]{1,0:T(1,128)S(1)} %bitcast.25), custom_call_target="tpu_custom_call" | custom-call | flops 8589934592 | bytes 4194304 | tf_op jit(solution)/shard_map/embed/pallas_call | solution.py:36
  6.7 0.0 collective-permute-done.3.taps
  6.7 2.8 %collective-permute-done.1.far_rim = bf16[16,1024]{1,0:T(8,128)(2,1)S(1)} collective-permute-done((bf16[16,1024]{1,0:T(8,128)(2,1)S(1)}, bf16[16,1024]{1,0:T(8,128)(2,1)S(1)}, u32[]{:S(2)}, u32[]{:S(2)}) %collective-permute-start.1) | collective-permute-done | bytes 32800 | tf_op jit(solution)/shard_map/ppermute | solution.py:353
  9.5 0.0 collective-permute-done.4.feat_w
  9.5 2.7 %keys_other.1 = (bf16[16,512]{1,0:T(8,128)(2,1)S(1)}, bf16[1024,512]{1,0:T(8,128)(2,1)S(1)}, bf16[1024,256]{1,0:T(8,128)(2,1)S(1)}, f32[4,272,128]{2,1,0:T(8,128...) custom-call(f32[6,512]{1,0:T(8,128)S(1)} %broadcast_in_dim.60.after.masks, ...), custom_call_target="tpu_custom_call" | custom-call | flops 12884901888 | bytes 4194304 | tf_op jit(solution)/shard_map/keys_other/pallas_call | solution.py:36
  12.2 0.2 collective-permute-start.5
  12.4 2.4 %keys_own.1 = (bf16[1024,512]{1,0:T(8,128)(2,1)S(1)}, bf16[1024,256]{1,0:T(8,128)(2,1)S(1)}, f32[4,272,128]{2,1,0:T(8,128)S(1)}, f32[272,128]{1,0:T(8,128)S(1)},...) custom-call(f32[6,512]{1,0:T(8,128)S(1)} %broadcast_in_dim.60.after.masks, ...), custom_call_target="tpu_custom_call" | custom-call | flops 12884901888 | bytes 4194304 | tf_op jit(solution)/shard_map/keys_own/pallas_call | solution.py:36
  14.9 0.5 %collective-permute-start.11 = (bf16[256,512]{1,0:T(8,128)(2,1)S(1)}, bf16[256,512]{1,0:T(8,128)(2,1)S(1)}, u32[]{:S(2)}, u32[]{:S(2)}) collective-permute-start(bf16[256,512]{1,0:T(8,128)(2,1)S(1)} %get-tuple-element.51.weight), channel_id=1, source_target_pairs={{0,1},{1,0},{2,3},{3,2},{4,5},{5,4},{6,7},{7,6},{8,9},{9,8},{10,11... | collective-permute-start | bytes 786440 | tf_op jit(solution)/shard_map/ppermute | solution.py:285
  15.3 0.1 collective-permute-start.6
  15.4 0.3 %collective-permute-start.7 = (bf16[272,128]{1,0:T(8,128)(2,1)S(1)}, bf16[272,128]{1,0:T(8,128)(2,1)S(1)}, u32[]{:S(2)}, u32[]{:S(2)}) collective-permute-start(bf16[272,128]{1,0:T(8,128)(2,1)S(1)} %fusion.5.after), channel_id=1, source_target_pairs={{0,4},{2,6},{4,0},{6,2},{8,12},{10,14},{12,8},{14,10},{1,5},{3,7},... | collective-permute-start | bytes 208904 | tf_op jit(solution)/shard_map/ppermute | solution.py:285
  15.8 3.1 %collective-permute-start.8 = (bf16[272,128]{1,0:T(8,128)(2,1)S(1)}, bf16[272,128]{1,0:T(8,128)(2,1)S(1)}, u32[]{:S(2)}, u32[]{:S(2)}) collective-permute-start(bf16[272,128]{1,0:T(8,128)(2,1)S(1)} %fusion.5.after), channel_id=1, source_target_pairs={{0,6},{2,4},{4,2},{6,0},{8,14},{10,12},{12,10},{14,8},{1,7},{3,5},... | collective-permute-start | bytes 208904 | tf_op jit(solution)/shard_map/ppermute | solution.py:285
  18.9 2.6 %queries.3 = (bf16[1024,512]{1,0:T(8,128)(2,1)S(1)}, f32[1024,512]{1,0:T(8,128)S(1)}) custom-call(f32[6,512]{1,0:T(8,128)S(1)} %broadcast_in_dim.60.after.masks, bf16[272,128]{1,0:T(8,128)(2,1)S(1)} %fusion.5.after, bf16[1024,512]{1,0:T(8,128)(2,1)S(1)} %get-tuple-element.36.normed, bf16[16,512]{1,0:T(8,128)(2,1)S(1)} %get-tuple-element.41.nrim, ...), custom_call_target="tpu_custom_call" | custom-call | flops 6442450944 | bytes 4194304 | tf_op jit(solution)/shard_map/queries/pallas_call | solution.py:36
  21.5 0.8 %collective-permute-done.8 = bf16[272,128]{1,0:T(8,128)(2,1)S(1)} collective-permute-done((bf16[272,128]{1,0:T(8,128)(2,1)S(1)}, bf16[272,128]{1,0:T(8,128)(2,1)S(1)}, u32[]{:S(2)}, u32[]{:S(2)}) %collective-permute-start.8) | collective-permute-done | bytes 69664 | tf_op jit(solution)/shard_map/ppermute | solution.py:285
  22.3 1.3 %collective-permute-start.9 = (bf16[272,128]{1,0:T(8,128)(2,1)S(1)}, bf16[272,128]{1,0:T(8,128)(2,1)S(1)}, u32[]{:S(2)}, u32[]{:S(2)}) collective-permute-start(bf16[272,128]{1,0:T(8,128)(2,1)S(1)} %fusion.4.after), channel_id=1, source_target_pairs={{0,8},{2,10},{4,12},{6,14},{8,0},{10,2},{12,4},{14,6},{1,9},{3,11}... | collective-permute-start | bytes 208904 | tf_op jit(solution)/shard_map/ppermute | solution.py:285
  23.7 2.5 %queries.2 = (bf16[1024,512]{1,0:T(8,128)(2,1)S(1)}, f32[1024,512]{1,0:T(8,128)S(1)}) custom-call(f32[6,512]{1,0:T(8,128)S(1)} %broadcast_in_dim.60.after.masks, bf16[272,128]{1,0:T(8,128)(2,1)S(1)} %fusion.4.after, bf16[1024,512]{1,0:T(8,128)(2,1)S(1)} %get-tuple-element.36.normed, bf16[16,512]{1,0:T(8,128)(2,1)S(1)} %get-tuple-element.41.nrim, ...), custom_call_target="tpu_custom_call" | custom-call | flops 6442450944 | bytes 4194304 | tf_op jit(solution)/shard_map/queries/pallas_call | solution.py:36
  26.2 2.0 %collective-permute-done.9 = bf16[272,128]{1,0:T(8,128)(2,1)S(1)} collective-permute-done((bf16[272,128]{1,0:T(8,128)(2,1)S(1)}, bf16[272,128]{1,0:T(8,128)(2,1)S(1)}, u32[]{:S(2)}, u32[]{:S(2)}) %collective-permute-start.9) | collective-permute-done | bytes 69664 | tf_op jit(solution)/shard_map/ppermute | solution.py:285
  28.2 0.1 fusion
  28.3 0.1 collective-permute-start.10
  28.4 0.8 %attend_own.1.partial = f32[1024,512]{1,0:T(8,128)S(1)} custom-call(bf16[1024,512]{1,0:T(8,128)(2,1)S(1)} %get-tuple-element.56.qf, f32[1024,512]{1,0:T(8,128)S(1)} %get-tuple-element.57.local, f32[4,272,128]{2,1,0:T(8,128)S(1)} %get-tuple-element.58.before, f32[272,128]{1,0:T(8,128)S(1)} %get-tuple-element.59.state, ...), custom_call_target="tpu_custom_call" | custom-call | flops 4294967296 | bytes 4194304 | tf_op jit(solution)/shard_map/attend_own/pallas_call | solution.py:36
  29.2 0.5 %collective-permute-done.10.state = bf16[272,128]{1,0:T(8,128)(2,1)S(1)} collective-permute-done((bf16[272,128]{1,0:T(8,128)(2,1)S(1)}, bf16[272,128]{1,0:T(8,128)(2,1)S(1)}, u32[]{:S(2)}, u32[]{:S(2)}) %collective-permute-start.10) | collective-permute-done | bytes 69664 | tf_op jit(solution)/shard_map/ppermute | solution.py:285
  29.6 1.6 %attend_other.1 = bf16[1024,512]{1,0:T(8,128)(2,1)} custom-call(bf16[1024,512]{1,0:T(8,128)(2,1)S(1)} %get-tuple-element.48.qf, f32[1024,512]{1,0:T(8,128)S(1)} %get-tuple-element.49.local, f32[4,272,128]{2,1,0:T(8,128)S(1)} %get-tuple-element.50.before, bf16[272,128]{1,0:T(8,128)(2,1)S(1)} %collective-permute-done.10.state, ...), custom_call_target="tpu_custom_call" | custom-call | flops 4294967296 | bytes 4194304 | tf_op jit(solution)/shard_map/attend_other/pallas_call | solution.py:36
  (20 shorter events, 0.1 us)
Async XLA Ops:
  0.2 4.1 %copy-start.1 = (bf16[512,3,256]{2,0,1:T(8,128)(2,1)S(1)}, bf16[512,3,256]{2,0,1:T(8,128)(2,1)}, u32[]{:S(2)}) copy-start(bf16[512,3,256]{2,0,1:T(8,128)(2,1)} %param.10) | copy-start | bytes 2359300
  0.2 4.5 %copy-start.4 = (f32[4,3,256]{2,0,1:T(4,128)S(1)}, f32[4,3,256]{2,0,1:T(4,128)}, u32[]{:S(2)}) copy-start(f32[4,3,256]{2,0,1:T(4,128)} %param.11) | copy-start | bytes 36868
  0.2 4.6 %copy-start.3 = (bf16[4,64,128]{2,1,0:T(8,128)(2,1)S(1)}, bf16[4,64,128]{2,1,0:T(8,128)(2,1)}, u32[]{:S(2)}) copy-start(bf16[4,64,128]{2,1,0:T(8,128)(2,1)} %feat_w) | copy-start | bytes 196612
  0.2 5.0 %copy-start = (bf16[2048,1024]{1,0:T(8,128)(2,1)S(1)}, bf16[2048,1024]{1,0:T(8,128)(2,1)}, u32[]{:S(2)}) copy-start(bf16[2048,1024]{1,0:T(8,128)(2,1)} %sig.1) | copy-start | bytes 12582916
  0.2 5.0 %copy-start.2 = (bf16[512,512]{1,0:T(8,128)(2,1)S(1)}, bf16[512,512]{1,0:T(8,128)(2,1)}, u32[]{:S(2)}) copy-start(bf16[512,512]{1,0:T(8,128)(2,1)} %ew_a.1) | copy-start | bytes 1572868
  0.2 5.0 %copy-start.5 = (f32[512]{0:T(512)S(1)}, f32[512]{0:T(512)}, u32[]{:S(2)}) copy-start(f32[512]{0:T(512)} %param.9) | copy-start | bytes 6148
  0.2 5.0 %collective-permute-start = (bf16[512,512]{1,0:T(8,128)(2,1)}, bf16[512,512]{1,0:T(8,128)(2,1)S(1)}, u32[]{:S(2)}, u32[]{:S(2)}) collective-permute-start(bf16[512,512]{1,0:T(8,128)(2,1)} %ew_a.1), channel_id=1, source_target_pairs={{0,1},{1,0},{2,3},{3,2},{4,5},{5,4},{6,7},{7,6},{8,9},{9,8},{10,11... | collective-permute-start | bytes 1572872 | tf_op jit(solution)/shard_map/ppermute | solution.py:285
  1.8 7.7 %collective-permute-start.1 = (bf16[16,1024]{1,0:T(8,128)(2,1)S(1)}, bf16[16,1024]{1,0:T(8,128)(2,1)S(1)}, u32[]{:S(2)}, u32[]{:S(2)}) collective-permute-start(bf16[16,1024]{1,0:T(8,128)(2,1)S(1)} %rim.1), channel_id=1, source_target_pairs={{0,2},{2,4},{4,6},{6,8},{8,10},{10,12},{12,14},{14,0},{1,3},{3,5},... | collective-permute-start | bytes 98312 | tf_op jit(solution)/shard_map/ppermute | solution.py:353
  4.2 5.2 %collective-permute-start.2 = (bf16[3,512,256]{2,1,0:T(8,128)(2,1)S(1)}, bf16[3,512,256]{2,1,0:T(8,128)(2,1)S(1)}, u32[]{:S(2)}, u32[]{:S(2)}) collective-permute-start(bf16[3,512,256]{2,1,0:T(8,128)(2,1)S(1)} %bitcast.19), channel_id=1, source_target_pairs={{0,1},{1,0},{2,3},{3,2},{4,5},{5,4},{6,7},{7,6},{8,9},{9,8},{10,11... | collective-permute-start | bytes 2359304 | tf_op jit(solution)/shard_map/ppermute | solution.py:285
  4.7 2.0 %collective-permute-start.3 = (f32[3,4,256]{2,1,0:T(4,128)S(1)}, f32[3,4,256]{2,1,0:T(4,128)S(1)}, u32[]{:S(2)}, u32[]{:S(2)}) collective-permute-start(f32[3,4,256]{2,1,0:T(4,128)S(1)} %bitcast.22), channel_id=1, source_target_pairs={{0,1},{1,0},{2,3},{3,2},{4,5},{5,4},{6,7},{7,6},{8,9},{9,8},{10,11... | collective-permute-start | bytes 36872 | tf_op jit(solution)/shard_map/ppermute | solution.py:285
  4.8 4.7 %collective-permute-start.4 = (bf16[4,64,128]{2,1,0:T(8,128)(2,1)S(1)}, bf16[4,64,128]{2,1,0:T(8,128)(2,1)S(1)}, u32[]{:S(2)}, u32[]{:S(2)}) collective-permute-start(bf16[4,64,128]{2,1,0:T(8,128)(2,1)S(1)} %copy-done.3), channel_id=1, source_target_pairs={{0,1},{1,0},{2,3},{3,2},{4,5},{5,4},{6,7},{7,6},{8,9},{9,8},{10,11... | collective-permute-start | bytes 196616 | tf_op jit(solution)/shard_map/ppermute | solution.py:285
  12.2 3.1 %collective-permute-start.5 = (bf16[272,128]{1,0:T(8,128)(2,1)S(1)}, bf16[272,128]{1,0:T(8,128)(2,1)S(1)}, u32[]{:S(2)}, u32[]{:S(2)}) collective-permute-start(bf16[272,128]{1,0:T(8,128)(2,1)S(1)} %convert_element_type.35), channel_id=1, source_target_pairs={{0,1},{1,0},{2,3},{3,2},{4,5},{5,4},{6,7},{7,6},{8,9},{9,8},{10,11... | collective-permute-start | bytes 208904 | tf_op jit(solution)/shard_map/ppermute | solution.py:285
  14.9 14.3 %collective-permute-start.11 = (bf16[256,512]{1,0:T(8,128)(2,1)S(1)}, bf16[256,512]{1,0:T(8,128)(2,1)S(1)}, u32[]{:S(2)}, u32[]{:S(2)}) collective-permute-start(bf16[256,512]{1,0:T(8,128)(2,1)S(1)} %get-tuple-element.51.weight), channel_id=1, source_target_pairs={{0,1},{1,0},{2,3},{3,2},{4,5},{5,4},{6,7},{7,6},{8,9},{9,8},{10,11... | collective-permute-start | bytes 786440 | tf_op jit(solution)/shard_map/ppermute | solution.py:285
  15.3 6.1 %collective-permute-start.6 = (bf16[272,128]{1,0:T(8,128)(2,1)S(1)}, bf16[272,128]{1,0:T(8,128)(2,1)S(1)}, u32[]{:S(2)}, u32[]{:S(2)}) collective-permute-start(bf16[272,128]{1,0:T(8,128)(2,1)S(1)} %fusion.5.after), channel_id=1, source_target_pairs={{0,2},{2,0},{4,6},{6,4},{8,10},{10,8},{12,14},{14,12},{1,3},{3,1},... | collective-permute-start | bytes 208904 | tf_op jit(solution)/shard_map/ppermute | solution.py:285
  15.4 6.1 %collective-permute-start.7 = (bf16[272,128]{1,0:T(8,128)(2,1)S(1)}, bf16[272,128]{1,0:T(8,128)(2,1)S(1)}, u32[]{:S(2)}, u32[]{:S(2)}) collective-permute-start(bf16[272,128]{1,0:T(8,128)(2,1)S(1)} %fusion.5.after), channel_id=1, source_target_pairs={{0,4},{2,6},{4,0},{6,2},{8,12},{10,14},{12,8},{14,10},{1,5},{3,7},... | collective-permute-start | bytes 208904 | tf_op jit(solution)/shard_map/ppermute | solution.py:285
  15.8 6.5 %collective-permute-start.8 = (bf16[272,128]{1,0:T(8,128)(2,1)S(1)}, bf16[272,128]{1,0:T(8,128)(2,1)S(1)}, u32[]{:S(2)}, u32[]{:S(2)}) collective-permute-start(bf16[272,128]{1,0:T(8,128)(2,1)S(1)} %fusion.5.after), channel_id=1, source_target_pairs={{0,6},{2,4},{4,2},{6,0},{8,14},{10,12},{12,10},{14,8},{1,7},{3,5},... | collective-permute-start | bytes 208904 | tf_op jit(solution)/shard_map/ppermute | solution.py:285
  22.3 5.9 %collective-permute-start.9 = (bf16[272,128]{1,0:T(8,128)(2,1)S(1)}, bf16[272,128]{1,0:T(8,128)(2,1)S(1)}, u32[]{:S(2)}, u32[]{:S(2)}) collective-permute-start(bf16[272,128]{1,0:T(8,128)(2,1)S(1)} %fusion.4.after), channel_id=1, source_target_pairs={{0,8},{2,10},{4,12},{6,14},{8,0},{10,2},{12,4},{14,6},{1,9},{3,11}... | collective-permute-start | bytes 208904 | tf_op jit(solution)/shard_map/ppermute | solution.py:285
  28.3 1.3 %collective-permute-start.10 = (bf16[272,128]{1,0:T(8,128)(2,1)S(1)}, bf16[272,128]{1,0:T(8,128)(2,1)S(1)}, u32[]{:S(2)}, u32[]{:S(2)}) collective-permute-start(bf16[272,128]{1,0:T(8,128)(2,1)S(1)} %get-tuple-element.60), channel_id=1, source_target_pairs={{0,1},{1,0},{2,3},{3,2},{4,5},{5,4},{6,7},{7,6},{8,9},{9,8},{10,11... | collective-permute-start | bytes 208904 | tf_op jit(solution)/shard_map/ppermute | solution.py:285

commit v5 on v4

--- a/solution.py
+++ b/solution.py
@@ -98,18 +98,20 @@
     return jnp.concatenate(out, 1)
 
 
-def features(part, diag, ones, heads):
+def features(part, diag, ones, heads, together):
     rows, width = part.shape[0], part.shape[1] // heads
-    feat = diag.shape[1] // heads
+    feat, share = diag.shape[1] // heads, ones.shape[1] // heads
     part_f = part.astype(F32)
-    logits = dot(part, diag[...])
-    squares = dot((part_f * part_f).astype(BF16), ones[...])
-    scale = lax.rsqrt(squares * (1.0 / width) + EPS) * (LOG2E / math.sqrt(width))
-    share = scale.shape[1] // heads
     out = []
-    for h in range(heads):
-        mine = jnp.broadcast_to(scale[:, h * share : h * share + 1], (rows, feat))
-        out.append(jnp.exp2(logits[:, h * feat : (h + 1) * feat] * mine).astype(BF16))
+    for first in range(0, heads, together):
+        at = slice(first * width, (first + together) * width)
+        logits = dot(part[:, at], diag[at, first * feat : (first + together) * feat])
+        squares = dot((part_f[:, at] * part_f[:, at]).astype(BF16), ones[at, :])
+        scale = lax.rsqrt(squares * (1.0 / width) + EPS) * (LOG2E / math.sqrt(width))
+        for k in range(together):
+            lane = (first + k) * share
+            mine = jnp.broadcast_to(scale[:, lane : lane + 1], (rows, feat))
+            out.append(jnp.exp2(logits[:, k * feat : (k + 1) * feat] * mine).astype(BF16))
     return jnp.concatenate(out, 1)
 
 
@@ -142,7 +144,7 @@
     key = convolve(pad, taps, 1, 0, tiles, PAD, rows)
     value = convolve(pad, taps, 2, tiles, tiles, PAD, rows)
     val[...] = value
-    key_feat = features(key, diag, ones, heads)
+    key_feat = features(key, diag, ones, heads, 2)
     kf[...] = key_feat
     for b in range(rows // SUB):
         sub = slice(b * SUB, (b + 1) * SUB)
@@ -206,7 +208,7 @@
     rim_rows(pad, nrim[...], (weight[0],), masks)
     store_proj(pad, normed[...], (weight[0],), PAD)
     query = convolve(pad, taps, 0, 0, weight.shape[2] // LANES, PAD, rows)
-    query_feat = features(query, diag, ones, heads)
+    query_feat = features(query, diag, ones, heads, heads)
     qf[...] = query_feat
     for b in range(rows // SUB):
         sub = slice(b * SUB, (b + 1) * SUB)
@@ -350,7 +352,9 @@
         [pltpu.SemaphoreType.DMA],
         (1 << 30, 1 << 20),
     )
-    far_rim = lax.ppermute(far_rim, "tm", [(i, (i + 1) % devices) for i in range(devices)])
+    ring = [(2 * i, 2 * i + 2) for i in range(devices - 1)] + [(2 * devices - 2, 2 * devices - 1)]
+    ring += [(2 * i + 1, 2 * i - 1) for i in range(1, devices)] + [(1, 0)]
+    far_rim = lax.ppermute(far_rim, ("tm", "rep"), ring)
     wqkv = [qkv_weight.transpose(1, 0, 2), swap(qkv_weight.transpose(1, 0, 2), "rep", 1)]
     taps = [conv_weight.transpose(1, 0, 2), swap(conv_weight.transpose(1, 0, 2), "rep", 1)]
     feat_w = [feature_weight, swap(feature_weight, "rep", 1)]
@@ -395,18 +399,19 @@
         [pads, pltpu.SemaphoreType.DMA],
         key_work,
     )
-    ow = [own[6], swap(own[6], "rep", 1)]
-    qf, local = [None] * 2, [None] * 2
+    qf, local, ow = [None] * 2, [None] * 2, [own[6]]
 
     def query(k, keys, after):
         qf[k], local[k] = call(
             functools.partial(query_kernel, heads=heads),
-            [*vmem(masks, after, normed, nrim, wqkv[k], taps[k], *keys[4:6], *keys[:2])],
+            vmem(masks, after, normed, nrim, wqkv[k], taps[k], *keys[4:6], *keys[:2]),
             [((rows, feats), BF16, None), ((rows, 2 * cols), F32, None)],
             "queries",
             [pltpu.VMEM((cols // LANES, PAD + rows, LANES), F32)],
             (6 * rows * width * cols, 4 << 20),
         )
+        if k == 1:
+            ow.append(swap(lax.optimization_barrier((ow[0], after))[0], "rep", 1))
 
     covers = [functools.partial(query, 0, own), functools.partial(query, 1, other)]
     before = prefix(own[3] + back, "tm", masks[2:, :feat], covers)

time: 31.4 us -> 29.5 us (0.939)
  waiting for transfers between devices: 6.1 us -> 4.35 us
  Pallas kernels: 15 us -> 14.5 us
  starting transfers between devices: 9.52 us -> 9.91 us
    ppermute x1, waiting for transfers between devices: 2.81 us -> 0.01 us  [shards(): far_rim = lax.ppermute(far_rim, ('tm', 'rep'), ring)]
    ppermute x11, waiting for transfers between devices: 3.3 us -> 4.34 us  [swap(): return lax.ppermute(array, axis, [(i, i ^ by) for i in range(devices)])]
    pallas_call x8, Pallas kernels: 15 us -> 14.5 us  [call(): pl.pallas_call(kernel, in_specs=[spec(p) for _, p in ins], out_specs=[spe...]
    ppermute x11, starting transfers between devices: 7.07 us -> 7.45 us  [swap(): return lax.ppermute(array, axis, [(i, i ^ by) for i in range(devices)])]
  transfers between devices with their start and end apart: 12 -> 12, of which waited for: 4 -> 5; matrix products, arithmetic and copies ran while one was open for 1% -> 0% of each run, Pallas kernels for 34% -> 36%
where the time goes in v5:
time: 29.5 us; the launch traced here: 29.3 us
  Pallas kernels  14.5 us (49%)
  starting transfers between devices  9.91 us (34%)
  waiting for transfers between devices  4.35 us (15%)
    pallas_call x8, Pallas kernels, call(): pl.pallas_call(kernel, in_specs=[spec(p) for _, p in ins], out_specs=[spe...  14.5 us
    ppermute x11, starting transfers between devices, swap(): return lax.ppermute(array, axis, [(i, i ^ by) for i in range(devices)])  7.45 us
    ppermute x11, waiting for transfers between devices, swap(): return lax.ppermute(array, axis, [(i, i ^ by) for i in range(devices)])  4.34 us
    ppermute x1, starting transfers between devices, shards(): far_rim = lax.ppermute(far_rim, ('tm', 'rep'), ring)  2.46 us
  transfers between devices with their start and end apart: 12, of which 5 were waited for; matrix products, arithmetic and copies ran while one was open for 0% of the time, Pallas kernels for 36%

profile of v5, /device:TPU:0, one launch (start us, length us, event | category | flops | bytes accessed | tf_op | source)
XLA Modules:
  0.0 29.3 jit_solution(11945838136090000585)
XLA Ops:
  0.0 0.1 stack.27
  0.1 0.1 broadcast_in_dim.60.after.masks
  0.2 0.0 copy-start.2
  0.2 0.0 copy-start.5
  0.2 0.5 %collective-permute-start = (bf16[512,512]{1,0:T(8,128)(2,1)}, bf16[512,512]{1,0:T(8,128)(2,1)S(1)}, u32[]{:S(2)}, u32[]{:S(2)}) collective-permute-start(bf16[512,512]{1,0:T(8,128)(2,1)} %ew_a.1), channel_id=1, source_target_pairs={{0,1},{1,0},{2,3},{3,2},{4,5},{5,4},{6,7},{7,6},{8,9},{9,8},{10,11... | collective-permute-start | bytes 1572872 | tf_op jit(solution)/shard_map/ppermute | solution.py:287
  0.7 1.0 %rim.1 = bf16[16,1024]{1,0:T(8,128)(2,1)S(1)} custom-call(f32[6,512]{1,0:T(8,128)S(1)} %broadcast_in_dim.60.after.masks, bf16[2048,1024]{1,0:T(8,128)(2,1)} %sig.1), custom_call_target="tpu_custom_call" | custom-call | flops 8589934592 | bytes 1048576 | tf_op jit(solution)/shard_map/rim/pallas_call | solution.py:36
  1.8 2.5 %collective-permute-start.1 = (bf16[16,1024]{1,0:T(8,128)(2,1)S(1)}, bf16[16,1024]{1,0:T(8,128)(2,1)S(1)}, u32[]{:S(2)}, u32[]{:S(2)}) collective-permute-start(bf16[16,1024]{1,0:T(8,128)(2,1)S(1)} %rim.1), channel_id=1, source_target_pairs={{0,2},{2,4},{4,6},{6,8},{8,10},{10,12},{12,14},{14,15},{3,1},{5,3}... | collective-permute-start | bytes 98312 | tf_op jit(solution)/shard_map/ppermute | solution.py:357
  4.3 0.0 collective-permute-start.2
  4.3 0.5 %collective-permute-start.3 = (f32[3,4,256]{2,1,0:T(4,128)S(1)}, f32[3,4,256]{2,1,0:T(4,128)S(1)}, u32[]{:S(2)}, u32[]{:S(2)}) collective-permute-start(f32[3,4,256]{2,1,0:T(4,128)S(1)} %bitcast.22), channel_id=1, source_target_pairs={{0,1},{1,0},{2,3},{3,2},{4,5},{5,4},{6,7},{7,6},{8,9},{9,8},{10,11... | collective-permute-start | bytes 36872 | tf_op jit(solution)/shard_map/ppermute | solution.py:287
  4.8 0.1 collective-permute-start.4
  4.9 0.0 collective-permute-done.ew_b
  4.9 1.4 %embed.1 = (bf16[1024,512]{1,0:T(8,128)(2,1)S(1)}, bf16[16,1024]{1,0:T(8,128)(2,1)S(1)}) custom-call(bf16[2048,1024]{1,0:T(8,128)(2,1)S(1)} %copy-done, bf16[512,512]{1,0:T(8,128)(2,1)S(1)} %copy-done.2, bf16[512,512]{1,0:T(8,128)(2,1)S(1)} %collective-permute-done.ew_b, f32[1,512]{1,0:T(1,128)S(1)} %bitcast.25), custom_call_target="tpu_custom_call" | custom-call | flops 8589934592 | bytes 4194304 | tf_op jit(solution)/shard_map/embed/pallas_call | solution.py:36
  6.3 0.3 collective-permute-done.3.taps
  6.6 0.0 collective-permute-done.1.far_rim
  6.6 0.1 collective-permute-done.4.feat_w
  6.7 2.5 %keys_other.1 = (bf16[16,512]{1,0:T(8,128)(2,1)S(1)}, bf16[1024,512]{1,0:T(8,128)(2,1)S(1)}, bf16[1024,256]{1,0:T(8,128)(2,1)S(1)}, f32[4,272,128]{2,1,0:T(8,128...) custom-call(f32[6,512]{1,0:T(8,128)S(1)} %broadcast_in_dim.60.after.masks, ...), custom_call_target="tpu_custom_call" | custom-call | flops 12884901888 | bytes 4194304 | tf_op jit(solution)/shard_map/keys_other/pallas_call | solution.py:36
  9.1 0.2 collective-permute-start.5
  9.3 2.2 %keys_own.1 = (bf16[1024,512]{1,0:T(8,128)(2,1)S(1)}, bf16[1024,256]{1,0:T(8,128)(2,1)S(1)}, f32[4,272,128]{2,1,0:T(8,128)S(1)}, f32[272,128]{1,0:T(8,128)S(1)},...) custom-call(f32[6,512]{1,0:T(8,128)S(1)} %broadcast_in_dim.60.after.masks, ...), custom_call_target="tpu_custom_call" | custom-call | flops 12884901888 | bytes 4194304 | tf_op jit(solution)/shard_map/keys_own/pallas_call | solution.py:36
  11.5 0.0 collective-permute-done.5
  11.6 1.9 %collective-permute-start.6 = (bf16[272,128]{1,0:T(8,128)(2,1)S(1)}, bf16[272,128]{1,0:T(8,128)(2,1)S(1)}, u32[]{:S(2)}, u32[]{:S(2)}) collective-permute-start(bf16[272,128]{1,0:T(8,128)(2,1)S(1)} %fusion.5.after), channel_id=1, source_target_pairs={{0,2},{2,0},{4,6},{6,4},{8,10},{10,8},{12,14},{14,12},{1,3},{3,1},... | collective-permute-start | bytes 208904 | tf_op jit(solution)/shard_map/ppermute | solution.py:287
  13.5 1.6 %collective-permute-start.7 = (bf16[272,128]{1,0:T(8,128)(2,1)S(1)}, bf16[272,128]{1,0:T(8,128)(2,1)S(1)}, u32[]{:S(2)}, u32[]{:S(2)}) collective-permute-start(bf16[272,128]{1,0:T(8,128)(2,1)S(1)} %fusion.5.after), channel_id=1, source_target_pairs={{0,4},{2,6},{4,0},{6,2},{8,12},{10,14},{12,8},{14,10},{1,5},{3,7},... | collective-permute-start | bytes 208904 | tf_op jit(solution)/shard_map/ppermute | solution.py:287
  15.1 0.4 %collective-permute-start.8 = (bf16[272,128]{1,0:T(8,128)(2,1)S(1)}, bf16[272,128]{1,0:T(8,128)(2,1)S(1)}, u32[]{:S(2)}, u32[]{:S(2)}) collective-permute-start(bf16[272,128]{1,0:T(8,128)(2,1)S(1)} %fusion.5.after), channel_id=1, source_target_pairs={{0,6},{2,4},{4,2},{6,0},{8,14},{10,12},{12,10},{14,8},{1,7},{3,5},... | collective-permute-start | bytes 208904 | tf_op jit(solution)/shard_map/ppermute | solution.py:287
  15.4 2.6 %queries.3 = (bf16[1024,512]{1,0:T(8,128)(2,1)S(1)}, f32[1024,512]{1,0:T(8,128)S(1)}) custom-call(f32[6,512]{1,0:T(8,128)S(1)} %broadcast_in_dim.60.after.masks, bf16[272,128]{1,0:T(8,128)(2,1)S(1)} %fusion.5.after, bf16[1024,512]{1,0:T(8,128)(2,1)S(1)} %get-tuple-element.37.normed, bf16[16,512]{1,0:T(8,128)(2,1)S(1)} %get-tuple-element.42.nrim, ...), custom_call_target="tpu_custom_call" | custom-call | flops 6442450944 | bytes 4194304 | tf_op jit(solution)/shard_map/queries/pallas_call | solution.py:36
  18.0 2.2 %collective-permute-done.8 = bf16[272,128]{1,0:T(8,128)(2,1)S(1)} collective-permute-done((bf16[272,128]{1,0:T(8,128)(2,1)S(1)}, bf16[272,128]{1,0:T(8,128)(2,1)S(1)}, u32[]{:S(2)}, u32[]{:S(2)}) %collective-permute-start.8) | collective-permute-done | bytes 69664 | tf_op jit(solution)/shard_map/ppermute | solution.py:287
  20.3 2.2 %collective-permute-start.9 = (bf16[272,128]{1,0:T(8,128)(2,1)S(1)}, bf16[272,128]{1,0:T(8,128)(2,1)S(1)}, u32[]{:S(2)}, u32[]{:S(2)}) collective-permute-start(bf16[272,128]{1,0:T(8,128)(2,1)S(1)} %fusion.4.after), channel_id=1, source_target_pairs={{0,8},{2,10},{4,12},{6,14},{8,0},{10,2},{12,4},{14,6},{1,9},{3,11}... | collective-permute-start | bytes 208904 | tf_op jit(solution)/shard_map/ppermute | solution.py:287
  22.5 2.5 %queries.2 = (bf16[1024,512]{1,0:T(8,128)(2,1)S(1)}, f32[1024,512]{1,0:T(8,128)S(1)}) custom-call(f32[6,512]{1,0:T(8,128)S(1)} %broadcast_in_dim.60.after.masks, bf16[272,128]{1,0:T(8,128)(2,1)S(1)} %fusion.4.after, bf16[1024,512]{1,0:T(8,128)(2,1)S(1)} %get-tuple-element.37.normed, bf16[16,512]{1,0:T(8,128)(2,1)S(1)} %get-tuple-element.42.nrim, ...), custom_call_target="tpu_custom_call" | custom-call | flops 6442450944 | bytes 4194304 | tf_op jit(solution)/shard_map/queries/pallas_call | solution.py:36
  25.1 1.3 %collective-permute-done.9 = bf16[272,128]{1,0:T(8,128)(2,1)S(1)} collective-permute-done((bf16[272,128]{1,0:T(8,128)(2,1)S(1)}, bf16[272,128]{1,0:T(8,128)(2,1)S(1)}, u32[]{:S(2)}, u32[]{:S(2)}) %collective-permute-start.9) | collective-permute-done | bytes 69664 | tf_op jit(solution)/shard_map/ppermute | solution.py:287
  26.3 0.1 fusion
  26.4 0.1 collective-permute-start.10
  26.5 0.8 %attend_own.1.partial = f32[1024,512]{1,0:T(8,128)S(1)} custom-call(bf16[1024,512]{1,0:T(8,128)(2,1)S(1)} %get-tuple-element.58.qf, f32[1024,512]{1,0:T(8,128)S(1)} %get-tuple-element.59.local, f32[4,272,128]{2,1,0:T(8,128)S(1)} %get-tuple-element.60.before, f32[272,128]{1,0:T(8,128)S(1)} %get-tuple-element.61.state, ...), custom_call_target="tpu_custom_call" | custom-call | flops 4294967296 | bytes 4194304 | tf_op jit(solution)/shard_map/attend_own/pallas_call | solution.py:36
  27.3 0.5 %collective-permute-done.10.state = bf16[272,128]{1,0:T(8,128)(2,1)S(1)} collective-permute-done((bf16[272,128]{1,0:T(8,128)(2,1)S(1)}, bf16[272,128]{1,0:T(8,128)(2,1)S(1)}, u32[]{:S(2)}, u32[]{:S(2)}) %collective-permute-start.10) | collective-permute-done | bytes 69664 | tf_op jit(solution)/shard_map/ppermute | solution.py:287
  27.8 1.6 %attend_other.1 = bf16[1024,512]{1,0:T(8,128)(2,1)} custom-call(bf16[1024,512]{1,0:T(8,128)(2,1)S(1)} %get-tuple-element.49.qf, f32[1024,512]{1,0:T(8,128)S(1)} %get-tuple-element.50.local, f32[4,272,128]{2,1,0:T(8,128)S(1)} %get-tuple-element.51.before, bf16[272,128]{1,0:T(8,128)(2,1)S(1)} %collective-permute-done.10.state, ...), custom_call_target="tpu_custom_call" | custom-call | flops 4294967296 | bytes 4194304 | tf_op jit(solution)/shard_map/attend_other/pallas_call | solution.py:36
  (20 shorter events, 0.1 us)
Async XLA Ops:
  0.2 4.1 %copy-start.1 = (bf16[512,3,256]{2,0,1:T(8,128)(2,1)S(1)}, bf16[512,3,256]{2,0,1:T(8,128)(2,1)}, u32[]{:S(2)}) copy-start(bf16[512,3,256]{2,0,1:T(8,128)(2,1)} %param.10) | copy-start | bytes 2359300
  0.2 4.1 %copy-start.4 = (f32[4,3,256]{2,0,1:T(4,128)S(1)}, f32[4,3,256]{2,0,1:T(4,128)}, u32[]{:S(2)}) copy-start(f32[4,3,256]{2,0,1:T(4,128)} %param.11) | copy-start | bytes 36868
  0.2 4.6 %copy-start.3 = (bf16[4,64,128]{2,1,0:T(8,128)(2,1)S(1)}, bf16[4,64,128]{2,1,0:T(8,128)(2,1)}, u32[]{:S(2)}) copy-start(bf16[4,64,128]{2,1,0:T(8,128)(2,1)} %feat_w) | copy-start | bytes 196612
  0.2 4.7 %copy-start = (bf16[2048,1024]{1,0:T(8,128)(2,1)S(1)}, bf16[2048,1024]{1,0:T(8,128)(2,1)}, u32[]{:S(2)}) copy-start(bf16[2048,1024]{1,0:T(8,128)(2,1)} %sig.1) | copy-start | bytes 12582916
  0.2 4.7 %copy-start.2 = (bf16[512,512]{1,0:T(8,128)(2,1)S(1)}, bf16[512,512]{1,0:T(8,128)(2,1)}, u32[]{:S(2)}) copy-start(bf16[512,512]{1,0:T(8,128)(2,1)} %ew_a.1) | copy-start | bytes 1572868
  0.2 4.7 %copy-start.5 = (f32[512]{0:T(512)S(1)}, f32[512]{0:T(512)}, u32[]{:S(2)}) copy-start(f32[512]{0:T(512)} %param.9) | copy-start | bytes 6148
  0.2 4.6 %collective-permute-start = (bf16[512,512]{1,0:T(8,128)(2,1)}, bf16[512,512]{1,0:T(8,128)(2,1)S(1)}, u32[]{:S(2)}, u32[]{:S(2)}) collective-permute-start(bf16[512,512]{1,0:T(8,128)(2,1)} %ew_a.1), channel_id=1, source_target_pairs={{0,1},{1,0},{2,3},{3,2},{4,5},{5,4},{6,7},{7,6},{8,9},{9,8},{10,11... | collective-permute-start | bytes 1572872 | tf_op jit(solution)/shard_map/ppermute | solution.py:287
  1.8 4.8 %collective-permute-start.1 = (bf16[16,1024]{1,0:T(8,128)(2,1)S(1)}, bf16[16,1024]{1,0:T(8,128)(2,1)S(1)}, u32[]{:S(2)}, u32[]{:S(2)}) collective-permute-start(bf16[16,1024]{1,0:T(8,128)(2,1)S(1)} %rim.1), channel_id=1, source_target_pairs={{0,2},{2,4},{4,6},{6,8},{8,10},{10,12},{12,14},{14,15},{3,1},{5,3}... | collective-permute-start | bytes 98312 | tf_op jit(solution)/shard_map/ppermute | solution.py:357
  4.3 2.4 %collective-permute-start.2 = (bf16[3,512,256]{2,1,0:T(8,128)(2,1)S(1)}, bf16[3,512,256]{2,1,0:T(8,128)(2,1)S(1)}, u32[]{:S(2)}, u32[]{:S(2)}) collective-permute-start(bf16[3,512,256]{2,1,0:T(8,128)(2,1)S(1)} %bitcast.19), channel_id=1, source_target_pairs={{0,1},{1,0},{2,3},{3,2},{4,5},{5,4},{6,7},{7,6},{8,9},{9,8},{10,11... | collective-permute-start | bytes 2359304 | tf_op jit(solution)/shard_map/ppermute | solution.py:287
  4.3 2.3 %collective-permute-start.3 = (f32[3,4,256]{2,1,0:T(4,128)S(1)}, f32[3,4,256]{2,1,0:T(4,128)S(1)}, u32[]{:S(2)}, u32[]{:S(2)}) collective-permute-start(f32[3,4,256]{2,1,0:T(4,128)S(1)} %bitcast.22), channel_id=1, source_target_pairs={{0,1},{1,0},{2,3},{3,2},{4,5},{5,4},{6,7},{7,6},{8,9},{9,8},{10,11... | collective-permute-start | bytes 36872 | tf_op jit(solution)/shard_map/ppermute | solution.py:287
  4.8 1.9 %collective-permute-start.4 = (bf16[4,64,128]{2,1,0:T(8,128)(2,1)S(1)}, bf16[4,64,128]{2,1,0:T(8,128)(2,1)S(1)}, u32[]{:S(2)}, u32[]{:S(2)}) collective-permute-start(bf16[4,64,128]{2,1,0:T(8,128)(2,1)S(1)} %copy-done.3), channel_id=1, source_target_pairs={{0,1},{1,0},{2,3},{3,2},{4,5},{5,4},{6,7},{7,6},{8,9},{9,8},{10,11... | collective-permute-start | bytes 196616 | tf_op jit(solution)/shard_map/ppermute | solution.py:287
  9.1 2.4 %collective-permute-start.5 = (bf16[272,128]{1,0:T(8,128)(2,1)S(1)}, bf16[272,128]{1,0:T(8,128)(2,1)S(1)}, u32[]{:S(2)}, u32[]{:S(2)}) collective-permute-start(bf16[272,128]{1,0:T(8,128)(2,1)S(1)} %convert_element_type.35), channel_id=1, source_target_pairs={{0,1},{1,0},{2,3},{3,2},{4,5},{5,4},{6,7},{7,6},{8,9},{9,8},{10,11... | collective-permute-start | bytes 208904 | tf_op jit(solution)/shard_map/ppermute | solution.py:287
  11.6 6.5 %collective-permute-start.6 = (bf16[272,128]{1,0:T(8,128)(2,1)S(1)}, bf16[272,128]{1,0:T(8,128)(2,1)S(1)}, u32[]{:S(2)}, u32[]{:S(2)}) collective-permute-start(bf16[272,128]{1,0:T(8,128)(2,1)S(1)} %fusion.5.after), channel_id=1, source_target_pairs={{0,2},{2,0},{4,6},{6,4},{8,10},{10,8},{12,14},{14,12},{1,3},{3,1},... | collective-permute-start | bytes 208904 | tf_op jit(solution)/shard_map/ppermute | solution.py:287
  13.5 4.6 %collective-permute-start.7 = (bf16[272,128]{1,0:T(8,128)(2,1)S(1)}, bf16[272,128]{1,0:T(8,128)(2,1)S(1)}, u32[]{:S(2)}, u32[]{:S(2)}) collective-permute-start(bf16[272,128]{1,0:T(8,128)(2,1)S(1)} %fusion.5.after), channel_id=1, source_target_pairs={{0,4},{2,6},{4,0},{6,2},{8,12},{10,14},{12,8},{14,10},{1,5},{3,7},... | collective-permute-start | bytes 208904 | tf_op jit(solution)/shard_map/ppermute | solution.py:287
  15.1 5.2 %collective-permute-start.8 = (bf16[272,128]{1,0:T(8,128)(2,1)S(1)}, bf16[272,128]{1,0:T(8,128)(2,1)S(1)}, u32[]{:S(2)}, u32[]{:S(2)}) collective-permute-start(bf16[272,128]{1,0:T(8,128)(2,1)S(1)} %fusion.5.after), channel_id=1, source_target_pairs={{0,6},{2,4},{4,2},{6,0},{8,14},{10,12},{12,10},{14,8},{1,7},{3,5},... | collective-permute-start | bytes 208904 | tf_op jit(solution)/shard_map/ppermute | solution.py:287
  20.3 6.0 %collective-permute-start.9 = (bf16[272,128]{1,0:T(8,128)(2,1)S(1)}, bf16[272,128]{1,0:T(8,128)(2,1)S(1)}, u32[]{:S(2)}, u32[]{:S(2)}) collective-permute-start(bf16[272,128]{1,0:T(8,128)(2,1)S(1)} %fusion.4.after), channel_id=1, source_target_pairs={{0,8},{2,10},{4,12},{6,14},{8,0},{10,2},{12,4},{14,6},{1,9},{3,11}... | collective-permute-start | bytes 208904 | tf_op jit(solution)/shard_map/ppermute | solution.py:287
  22.5 5.2 %collective-permute-start.11 = (bf16[256,512]{1,0:T(8,128)(2,1)S(1)}, bf16[256,512]{1,0:T(8,128)(2,1)S(1)}, u32[]{:S(2)}, u32[]{:S(2)}) collective-permute-start(bf16[256,512]{1,0:T(8,128)(2,1)S(1)} %get-tuple-element.53.weight), channel_id=1, source_target_pairs={{0,1},{1,0},{2,3},{3,2},{4,5},{5,4},{6,7},{7,6},{8,9},{9,8},{10,11... | collective-permute-start | bytes 786440 | tf_op jit(solution)/shard_map/ppermute | solution.py:287
  26.4 1.3 %collective-permute-start.10 = (bf16[272,128]{1,0:T(8,128)(2,1)S(1)}, bf16[272,128]{1,0:T(8,128)(2,1)S(1)}, u32[]{:S(2)}, u32[]{:S(2)}) collective-permute-start(bf16[272,128]{1,0:T(8,128)(2,1)S(1)} %get-tuple-element.62), channel_id=1, source_target_pairs={{0,1},{1,0},{2,3},{3,2},{4,5},{5,4},{6,7},{7,6},{8,9},{9,8},{10,11... | collective-permute-start | bytes 208904 | tf_op jit(solution)/shard_map/ppermute | solution.py:287

commit v6 on v5

--- a/solution.py
+++ b/solution.py
@@ -137,10 +137,10 @@
     for h in range(heads):
         diag[h * head_dim : (h + 1) * head_dim, h * feat : (h + 1) * feat] = feat_w[h]
     weights = (weight[1], weight[2])
-    rim_rows(pad, nrim, weights, masks)
     total[...] = jnp.zeros_like(total)
     rows = normed.shape[0]
     store_proj(pad, normed[...], weights, PAD)
+    rim_rows(pad, nrim(), weights, masks)
     key = convolve(pad, taps, 1, 0, tiles, PAD, rows)
     value = convolve(pad, taps, 2, tiles, tiles, PAD, rows)
     val[...] = value
@@ -178,9 +178,12 @@
     lo, hi = rim[:, :half], rim[:, half:]
     mine = jnp.where(own, lo, hi).astype(BF16)
     other = jnp.where(own, hi, lo).astype(BF16)
-    rows_n = normalize(dot(mine, ew_a[...]) + dot(other, ew_b[...]), gain[...])
-    nrim[...] = rows_n
-    key_body(masks, normed, rows_n, weight, taps, feat_w, kf, val, before, total, diag, ones, pad)
+
+    def rows_ahead():
+        nrim[...] = normalize(dot(mine, ew_a[...]) + dot(other, ew_b[...]), gain[...])
+        return nrim[...]
+
+    key_body(masks, normed, rows_ahead, weight, taps, feat_w, kf, val, before, total, diag, ones, pad)
 
 
 def key_kernel(
@@ -189,7 +192,10 @@
 ):
     copy = pltpu.make_async_copy(ow_hbm, ow, sem)
     copy.start()
-    key_body(masks, normed, nrim[...], weight, taps, feat_w, kf, val, before, total, diag, ones, pad)
+    key_body(
+        masks, normed, lambda: nrim[...], weight, taps, feat_w,
+        kf, val, before, total, diag, ones, pad,
+    )
     copy.wait()
 
 
@@ -312,11 +318,11 @@
         sent = group.astype(BF16)
         if covers:
             covers.pop(0)(sent)
-        for k in range(1, radix):
+        for k in range(radix - 1, 0, -1):
             got = swap(sent, axis, k * span).astype(F32)
             group = group + got
-            near = near + jnp.where(masks[row : row + 1] > 0, got, 0.0)
-            row += 1
+            near = near + jnp.where(masks[row + k - 1 : row + k] > 0, got, 0.0)
+        row += radix - 1
     while covers:
         covers.pop(0)(group)
     return near

time: 29.5 us -> 29 us (0.983)
  waiting for transfers between devices: 4.35 us -> 3.44 us
  starting transfers between devices: 9.91 us -> 10.5 us
    ppermute x11, waiting for transfers between devices: 4.34 us -> 3.44 us  [swap(): return lax.ppermute(array, axis, [(i, i ^ by) for i in range(devices)])]
    ppermute x11, starting transfers between devices: 7.45 us -> 8.03 us  [swap(): return lax.ppermute(array, axis, [(i, i ^ by) for i in range(devices)])]
  transfers between devices with their start and end apart: 12 -> 12, of which waited for: 5 -> 6; matrix products, arithmetic and copies ran while one was open for 0% -> 0% of each run, Pallas kernels for 36% -> 36%
where the time goes in v6:
time: 29 us; the launch traced here: 28.9 us
  Pallas kernels  14.4 us (50%)
  starting transfers between devices  10.5 us (36%)
  waiting for transfers between devices  3.44 us (12%)
    pallas_call x8, Pallas kernels, call(): pl.pallas_call(kernel, in_specs=[spec(p) for _, p in ins], out_specs=[spe...  14.4 us
    ppermute x11, starting transfers between devices, swap(): return lax.ppermute(array, axis, [(i, i ^ by) for i in range(devices)])  8.03 us
    ppermute x11, waiting for transfers between devices, swap(): return lax.ppermute(array, axis, [(i, i ^ by) for i in range(devices)])  3.44 us
    ppermute x1, starting transfers between devices, shards(): far_rim = lax.ppermute(far_rim, ('tm', 'rep'), ring)  2.46 us
  transfers between devices with their start and end apart: 12, of which 6 were waited for; matrix products, arithmetic and copies ran while one was open for 0% of the time, Pallas kernels for 36%

profile of v6, /device:TPU:0, one launch (start us, length us, event | category | flops | bytes accessed | tf_op | source)
XLA Modules:
  0.0 28.9 jit_solution(17627535743659596555)
XLA Ops:
  0.0 0.1 stack.27
  0.1 0.1 broadcast_in_dim.60.after.masks
  0.2 0.0 copy-start.2
  0.2 0.0 copy-start.5
  0.2 0.5 %collective-permute-start = (bf16[512,512]{1,0:T(8,128)(2,1)}, bf16[512,512]{1,0:T(8,128)(2,1)S(1)}, u32[]{:S(2)}, u32[]{:S(2)}) collective-permute-start(bf16[512,512]{1,0:T(8,128)(2,1)} %ew_a.1), channel_id=1, source_target_pairs={{0,1},{1,0},{2,3},{3,2},{4,5},{5,4},{6,7},{7,6},{8,9},{9,8},{10,11... | collective-permute-start | bytes 1572872 | tf_op jit(solution)/shard_map/ppermute | solution.py:293
  0.7 1.0 %rim.1 = bf16[16,1024]{1,0:T(8,128)(2,1)S(1)} custom-call(f32[6,512]{1,0:T(8,128)S(1)} %broadcast_in_dim.60.after.masks, bf16[2048,1024]{1,0:T(8,128)(2,1)} %sig.1), custom_call_target="tpu_custom_call" | custom-call | flops 8589934592 | bytes 1048576 | tf_op jit(solution)/shard_map/rim/pallas_call | solution.py:36
  1.8 2.5 %collective-permute-start.1 = (bf16[16,1024]{1,0:T(8,128)(2,1)S(1)}, bf16[16,1024]{1,0:T(8,128)(2,1)S(1)}, u32[]{:S(2)}, u32[]{:S(2)}) collective-permute-start(bf16[16,1024]{1,0:T(8,128)(2,1)S(1)} %rim.1), channel_id=1, source_target_pairs={{0,2},{2,4},{4,6},{6,8},{8,10},{10,12},{12,14},{14,15},{3,1},{5,3}... | collective-permute-start | bytes 98312 | tf_op jit(solution)/shard_map/ppermute | solution.py:363
  4.3 0.0 collective-permute-start.2
  4.3 0.5 %collective-permute-start.3 = (f32[3,4,256]{2,1,0:T(4,128)S(1)}, f32[3,4,256]{2,1,0:T(4,128)S(1)}, u32[]{:S(2)}, u32[]{:S(2)}) collective-permute-start(f32[3,4,256]{2,1,0:T(4,128)S(1)} %bitcast.22), channel_id=1, source_target_pairs={{0,1},{1,0},{2,3},{3,2},{4,5},{5,4},{6,7},{7,6},{8,9},{9,8},{10,11... | collective-permute-start | bytes 36872 | tf_op jit(solution)/shard_map/ppermute | solution.py:293
  4.8 0.1 collective-permute-start.4
  4.9 0.0 collective-permute-done.ew_b
  4.9 1.4 %embed.1 = (bf16[1024,512]{1,0:T(8,128)(2,1)S(1)}, bf16[16,1024]{1,0:T(8,128)(2,1)S(1)}) custom-call(bf16[2048,1024]{1,0:T(8,128)(2,1)S(1)} %copy-done, bf16[512,512]{1,0:T(8,128)(2,1)S(1)} %copy-done.2, bf16[512,512]{1,0:T(8,128)(2,1)S(1)} %collective-permute-done.ew_b, f32[1,512]{1,0:T(1,128)S(1)} %bitcast.25), custom_call_target="tpu_custom_call" | custom-call | flops 8589934592 | bytes 4194304 | tf_op jit(solution)/shard_map/embed/pallas_call | solution.py:36
  6.3 0.3 collective-permute-done.3.taps
  6.6 0.0 collective-permute-done.1.far_rim
  6.6 0.1 collective-permute-done.4.feat_w
  6.7 2.4 %keys_other.1 = (bf16[16,512]{1,0:T(8,128)(2,1)S(1)}, bf16[1024,512]{1,0:T(8,128)(2,1)S(1)}, bf16[1024,256]{1,0:T(8,128)(2,1)S(1)}, f32[4,272,128]{2,1,0:T(8,128...) custom-call(f32[6,512]{1,0:T(8,128)S(1)} %broadcast_in_dim.60.after.masks, ...), custom_call_target="tpu_custom_call" | custom-call | flops 12884901888 | bytes 4194304 | tf_op jit(solution)/shard_map/keys_other/pallas_call | solution.py:36
  9.1 0.2 collective-permute-start.5
  9.3 2.1 %keys_own.1 = (bf16[1024,512]{1,0:T(8,128)(2,1)S(1)}, bf16[1024,256]{1,0:T(8,128)(2,1)S(1)}, f32[4,272,128]{2,1,0:T(8,128)S(1)}, f32[272,128]{1,0:T(8,128)S(1)},...) custom-call(f32[6,512]{1,0:T(8,128)S(1)} %broadcast_in_dim.60.after.masks, ...), custom_call_target="tpu_custom_call" | custom-call | flops 12884901888 | bytes 4194304 | tf_op jit(solution)/shard_map/keys_own/pallas_call | solution.py:36
  11.4 2.9 %collective-permute-start.6 = (bf16[272,128]{1,0:T(8,128)(2,1)S(1)}, bf16[272,128]{1,0:T(8,128)(2,1)S(1)}, u32[]{:S(2)}, u32[]{:S(2)}) collective-permute-start(bf16[272,128]{1,0:T(8,128)(2,1)S(1)} %fusion.5.after), channel_id=1, source_target_pairs={{0,6},{2,4},{4,2},{6,0},{8,14},{10,12},{12,10},{14,8},{1,7},{3,5},... | collective-permute-start | bytes 208904 | tf_op jit(solution)/shard_map/ppermute | solution.py:293
  14.4 0.4 %collective-permute-start.7 = (bf16[272,128]{1,0:T(8,128)(2,1)S(1)}, bf16[272,128]{1,0:T(8,128)(2,1)S(1)}, u32[]{:S(2)}, u32[]{:S(2)}) collective-permute-start(bf16[272,128]{1,0:T(8,128)(2,1)S(1)} %fusion.5.after), channel_id=1, source_target_pairs={{0,4},{2,6},{4,0},{6,2},{8,12},{10,14},{12,8},{14,10},{1,5},{3,7},... | collective-permute-start | bytes 208904 | tf_op jit(solution)/shard_map/ppermute | solution.py:293
  14.8 0.5 %collective-permute-start.8 = (bf16[272,128]{1,0:T(8,128)(2,1)S(1)}, bf16[272,128]{1,0:T(8,128)(2,1)S(1)}, u32[]{:S(2)}, u32[]{:S(2)}) collective-permute-start(bf16[272,128]{1,0:T(8,128)(2,1)S(1)} %fusion.5.after), channel_id=1, source_target_pairs={{0,2},{2,0},{4,6},{6,4},{8,10},{10,8},{12,14},{14,12},{1,3},{3,1},... | collective-permute-start | bytes 208904 | tf_op jit(solution)/shard_map/ppermute | solution.py:293
  15.3 2.6 %queries.3 = (bf16[1024,512]{1,0:T(8,128)(2,1)S(1)}, f32[1024,512]{1,0:T(8,128)S(1)}) custom-call(f32[6,512]{1,0:T(8,128)S(1)} %broadcast_in_dim.60.after.masks, bf16[272,128]{1,0:T(8,128)(2,1)S(1)} %fusion.5.after, bf16[1024,512]{1,0:T(8,128)(2,1)S(1)} %get-tuple-element.37.normed, bf16[16,512]{1,0:T(8,128)(2,1)S(1)} %get-tuple-element.42.nrim, ...), custom_call_target="tpu_custom_call" | custom-call | flops 6442450944 | bytes 4194304 | tf_op jit(solution)/shard_map/queries/pallas_call | solution.py:36
  17.9 0.8 %collective-permute-done.7 = bf16[272,128]{1,0:T(8,128)(2,1)S(1)} collective-permute-done((bf16[272,128]{1,0:T(8,128)(2,1)S(1)}, bf16[272,128]{1,0:T(8,128)(2,1)S(1)}, u32[]{:S(2)}, u32[]{:S(2)}) %collective-permute-start.7) | collective-permute-done | bytes 69664 | tf_op jit(solution)/shard_map/ppermute | solution.py:293
  18.7 0.4 %collective-permute-done.8 = bf16[272,128]{1,0:T(8,128)(2,1)S(1)} collective-permute-done((bf16[272,128]{1,0:T(8,128)(2,1)S(1)}, bf16[272,128]{1,0:T(8,128)(2,1)S(1)}, u32[]{:S(2)}, u32[]{:S(2)}) %collective-permute-start.8) | collective-permute-done | bytes 69664 | tf_op jit(solution)/shard_map/ppermute | solution.py:293
  19.2 2.8 %collective-permute-start.9 = (bf16[272,128]{1,0:T(8,128)(2,1)S(1)}, bf16[272,128]{1,0:T(8,128)(2,1)S(1)}, u32[]{:S(2)}, u32[]{:S(2)}) collective-permute-start(bf16[272,128]{1,0:T(8,128)(2,1)S(1)} %fusion.4.after), channel_id=1, source_target_pairs={{0,8},{2,10},{4,12},{6,14},{8,0},{10,2},{12,4},{14,6},{1,9},{3,11}... | collective-permute-start | bytes 208904 | tf_op jit(solution)/shard_map/ppermute | solution.py:293
  22.0 2.5 %queries.2 = (bf16[1024,512]{1,0:T(8,128)(2,1)S(1)}, f32[1024,512]{1,0:T(8,128)S(1)}) custom-call(f32[6,512]{1,0:T(8,128)S(1)} %broadcast_in_dim.60.after.masks, bf16[272,128]{1,0:T(8,128)(2,1)S(1)} %fusion.4.after, bf16[1024,512]{1,0:T(8,128)(2,1)S(1)} %get-tuple-element.37.normed, bf16[16,512]{1,0:T(8,128)(2,1)S(1)} %get-tuple-element.42.nrim, ...), custom_call_target="tpu_custom_call" | custom-call | flops 6442450944 | bytes 4194304 | tf_op jit(solution)/shard_map/queries/pallas_call | solution.py:36
  24.5 1.4 %collective-permute-done.9 = bf16[272,128]{1,0:T(8,128)(2,1)S(1)} collective-permute-done((bf16[272,128]{1,0:T(8,128)(2,1)S(1)}, bf16[272,128]{1,0:T(8,128)(2,1)S(1)}, u32[]{:S(2)}, u32[]{:S(2)}) %collective-permute-start.9) | collective-permute-done | bytes 69664 | tf_op jit(solution)/shard_map/ppermute | solution.py:293
  25.9 0.1 fusion
  26.0 0.1 collective-permute-start.10
  26.1 0.8 %attend_own.1.partial = f32[1024,512]{1,0:T(8,128)S(1)} custom-call(bf16[1024,512]{1,0:T(8,128)(2,1)S(1)} %get-tuple-element.58.qf, f32[1024,512]{1,0:T(8,128)S(1)} %get-tuple-element.59.local, f32[4,272,128]{2,1,0:T(8,128)S(1)} %get-tuple-element.60.before, f32[272,128]{1,0:T(8,128)S(1)} %get-tuple-element.61.state, ...), custom_call_target="tpu_custom_call" | custom-call | flops 4294967296 | bytes 4194304 | tf_op jit(solution)/shard_map/attend_own/pallas_call | solution.py:36
  26.8 0.5 %collective-permute-done.10.state = bf16[272,128]{1,0:T(8,128)(2,1)S(1)} collective-permute-done((bf16[272,128]{1,0:T(8,128)(2,1)S(1)}, bf16[272,128]{1,0:T(8,128)(2,1)S(1)}, u32[]{:S(2)}, u32[]{:S(2)}) %collective-permute-start.10) | collective-permute-done | bytes 69664 | tf_op jit(solution)/shard_map/ppermute | solution.py:293
  27.3 1.6 %attend_other.1 = bf16[1024,512]{1,0:T(8,128)(2,1)} custom-call(bf16[1024,512]{1,0:T(8,128)(2,1)S(1)} %get-tuple-element.49.qf, f32[1024,512]{1,0:T(8,128)S(1)} %get-tuple-element.50.local, f32[4,272,128]{2,1,0:T(8,128)S(1)} %get-tuple-element.51.before, bf16[272,128]{1,0:T(8,128)(2,1)S(1)} %collective-permute-done.10.state, ...), custom_call_target="tpu_custom_call" | custom-call | flops 4294967296 | bytes 4194304 | tf_op jit(solution)/shard_map/attend_other/pallas_call | solution.py:36
  (20 shorter events, 0.1 us)
Async XLA Ops:
  0.2 4.1 %copy-start.1 = (bf16[512,3,256]{2,0,1:T(8,128)(2,1)S(1)}, bf16[512,3,256]{2,0,1:T(8,128)(2,1)}, u32[]{:S(2)}) copy-start(bf16[512,3,256]{2,0,1:T(8,128)(2,1)} %param.10) | copy-start | bytes 2359300
  0.2 4.1 %copy-start.4 = (f32[4,3,256]{2,0,1:T(4,128)S(1)}, f32[4,3,256]{2,0,1:T(4,128)}, u32[]{:S(2)}) copy-start(f32[4,3,256]{2,0,1:T(4,128)} %param.11) | copy-start | bytes 36868
  0.2 4.6 %copy-start.3 = (bf16[4,64,128]{2,1,0:T(8,128)(2,1)S(1)}, bf16[4,64,128]{2,1,0:T(8,128)(2,1)}, u32[]{:S(2)}) copy-start(bf16[4,64,128]{2,1,0:T(8,128)(2,1)} %feat_w) | copy-start | bytes 196612
  0.2 4.7 %copy-start = (bf16[2048,1024]{1,0:T(8,128)(2,1)S(1)}, bf16[2048,1024]{1,0:T(8,128)(2,1)}, u32[]{:S(2)}) copy-start(bf16[2048,1024]{1,0:T(8,128)(2,1)} %sig.1) | copy-start | bytes 12582916
  0.2 4.7 %copy-start.2 = (bf16[512,512]{1,0:T(8,128)(2,1)S(1)}, bf16[512,512]{1,0:T(8,128)(2,1)}, u32[]{:S(2)}) copy-start(bf16[512,512]{1,0:T(8,128)(2,1)} %ew_a.1) | copy-start | bytes 1572868
  0.2 4.7 %copy-start.5 = (f32[512]{0:T(512)S(1)}, f32[512]{0:T(512)}, u32[]{:S(2)}) copy-start(f32[512]{0:T(512)} %param.9) | copy-start | bytes 6148
  0.2 4.6 %collective-permute-start = (bf16[512,512]{1,0:T(8,128)(2,1)}, bf16[512,512]{1,0:T(8,128)(2,1)S(1)}, u32[]{:S(2)}, u32[]{:S(2)}) collective-permute-start(bf16[512,512]{1,0:T(8,128)(2,1)} %ew_a.1), channel_id=1, source_target_pairs={{0,1},{1,0},{2,3},{3,2},{4,5},{5,4},{6,7},{7,6},{8,9},{9,8},{10,11... | collective-permute-start | bytes 1572872 | tf_op jit(solution)/shard_map/ppermute | solution.py:293
  1.8 4.8 %collective-permute-start.1 = (bf16[16,1024]{1,0:T(8,128)(2,1)S(1)}, bf16[16,1024]{1,0:T(8,128)(2,1)S(1)}, u32[]{:S(2)}, u32[]{:S(2)}) collective-permute-start(bf16[16,1024]{1,0:T(8,128)(2,1)S(1)} %rim.1), channel_id=1, source_target_pairs={{0,2},{2,4},{4,6},{6,8},{8,10},{10,12},{12,14},{14,15},{3,1},{5,3}... | collective-permute-start | bytes 98312 | tf_op jit(solution)/shard_map/ppermute | solution.py:363
  4.3 2.4 %collective-permute-start.2 = (bf16[3,512,256]{2,1,0:T(8,128)(2,1)S(1)}, bf16[3,512,256]{2,1,0:T(8,128)(2,1)S(1)}, u32[]{:S(2)}, u32[]{:S(2)}) collective-permute-start(bf16[3,512,256]{2,1,0:T(8,128)(2,1)S(1)} %bitcast.19), channel_id=1, source_target_pairs={{0,1},{1,0},{2,3},{3,2},{4,5},{5,4},{6,7},{7,6},{8,9},{9,8},{10,11... | collective-permute-start | bytes 2359304 | tf_op jit(solution)/shard_map/ppermute | solution.py:293
  4.3 2.3 %collective-permute-start.3 = (f32[3,4,256]{2,1,0:T(4,128)S(1)}, f32[3,4,256]{2,1,0:T(4,128)S(1)}, u32[]{:S(2)}, u32[]{:S(2)}) collective-permute-start(f32[3,4,256]{2,1,0:T(4,128)S(1)} %bitcast.22), channel_id=1, source_target_pairs={{0,1},{1,0},{2,3},{3,2},{4,5},{5,4},{6,7},{7,6},{8,9},{9,8},{10,11... | collective-permute-start | bytes 36872 | tf_op jit(solution)/shard_map/ppermute | solution.py:293
  4.8 1.9 %collective-permute-start.4 = (bf16[4,64,128]{2,1,0:T(8,128)(2,1)S(1)}, bf16[4,64,128]{2,1,0:T(8,128)(2,1)S(1)}, u32[]{:S(2)}, u32[]{:S(2)}) collective-permute-start(bf16[4,64,128]{2,1,0:T(8,128)(2,1)S(1)} %copy-done.3), channel_id=1, source_target_pairs={{0,1},{1,0},{2,3},{3,2},{4,5},{5,4},{6,7},{7,6},{8,9},{9,8},{10,11... | collective-permute-start | bytes 196616 | tf_op jit(solution)/shard_map/ppermute | solution.py:293
  9.1 2.4 %collective-permute-start.5 = (bf16[272,128]{1,0:T(8,128)(2,1)S(1)}, bf16[272,128]{1,0:T(8,128)(2,1)S(1)}, u32[]{:S(2)}, u32[]{:S(2)}) collective-permute-start(bf16[272,128]{1,0:T(8,128)(2,1)S(1)} %convert_element_type.35), channel_id=1, source_target_pairs={{0,1},{1,0},{2,3},{3,2},{4,5},{5,4},{6,7},{7,6},{8,9},{9,8},{10,11... | collective-permute-start | bytes 208904 | tf_op jit(solution)/shard_map/ppermute | solution.py:293
  11.4 6.5 %collective-permute-start.6 = (bf16[272,128]{1,0:T(8,128)(2,1)S(1)}, bf16[272,128]{1,0:T(8,128)(2,1)S(1)}, u32[]{:S(2)}, u32[]{:S(2)}) collective-permute-start(bf16[272,128]{1,0:T(8,128)(2,1)S(1)} %fusion.5.after), channel_id=1, source_target_pairs={{0,6},{2,4},{4,2},{6,0},{8,14},{10,12},{12,10},{14,8},{1,7},{3,5},... | collective-permute-start | bytes 208904 | tf_op jit(solution)/shard_map/ppermute | solution.py:293
  14.4 4.3 %collective-permute-start.7 = (bf16[272,128]{1,0:T(8,128)(2,1)S(1)}, bf16[272,128]{1,0:T(8,128)(2,1)S(1)}, u32[]{:S(2)}, u32[]{:S(2)}) collective-permute-start(bf16[272,128]{1,0:T(8,128)(2,1)S(1)} %fusion.5.after), channel_id=1, source_target_pairs={{0,4},{2,6},{4,0},{6,2},{8,12},{10,14},{12,8},{14,10},{1,5},{3,7},... | collective-permute-start | bytes 208904 | tf_op jit(solution)/shard_map/ppermute | solution.py:293
  14.8 4.3 %collective-permute-start.8 = (bf16[272,128]{1,0:T(8,128)(2,1)S(1)}, bf16[272,128]{1,0:T(8,128)(2,1)S(1)}, u32[]{:S(2)}, u32[]{:S(2)}) collective-permute-start(bf16[272,128]{1,0:T(8,128)(2,1)S(1)} %fusion.5.after), channel_id=1, source_target_pairs={{0,2},{2,0},{4,6},{6,4},{8,10},{10,8},{12,14},{14,12},{1,3},{3,1},... | collective-permute-start | bytes 208904 | tf_op jit(solution)/shard_map/ppermute | solution.py:293
  19.2 6.7 %collective-permute-start.9 = (bf16[272,128]{1,0:T(8,128)(2,1)S(1)}, bf16[272,128]{1,0:T(8,128)(2,1)S(1)}, u32[]{:S(2)}, u32[]{:S(2)}) collective-permute-start(bf16[272,128]{1,0:T(8,128)(2,1)S(1)} %fusion.4.after), channel_id=1, source_target_pairs={{0,8},{2,10},{4,12},{6,14},{8,0},{10,2},{12,4},{14,6},{1,9},{3,11}... | collective-permute-start | bytes 208904 | tf_op jit(solution)/shard_map/ppermute | solution.py:293
  22.0 5.4 %collective-permute-start.11 = (bf16[256,512]{1,0:T(8,128)(2,1)S(1)}, bf16[256,512]{1,0:T(8,128)(2,1)S(1)}, u32[]{:S(2)}, u32[]{:S(2)}) collective-permute-start(bf16[256,512]{1,0:T(8,128)(2,1)S(1)} %get-tuple-element.53.weight), channel_id=1, source_target_pairs={{0,1},{1,0},{2,3},{3,2},{4,5},{5,4},{6,7},{7,6},{8,9},{9,8},{10,11... | collective-permute-start | bytes 786440 | tf_op jit(solution)/shard_map/ppermute | solution.py:293
  26.0 1.3 %collective-permute-start.10 = (bf16[272,128]{1,0:T(8,128)(2,1)S(1)}, bf16[272,128]{1,0:T(8,128)(2,1)S(1)}, u32[]{:S(2)}, u32[]{:S(2)}) collective-permute-start(bf16[272,128]{1,0:T(8,128)(2,1)S(1)} %get-tuple-element.62), channel_id=1, source_target_pairs={{0,1},{1,0},{2,3},{3,2},{4,5},{5,4},{6,7},{7,6},{8,9},{9,8},{10,11... | collective-permute-start | bytes 208904 | tf_op jit(solution)/shard_map/ppermute | solution.py:293

commit v7 on v6

--- a/solution.py
+++ b/solution.py
@@ -15,6 +15,7 @@
 RIM = 16
 PAD = 8
 LANES = 128
+TILE = 8
 F32 = jnp.float32
 BF16 = jnp.bfloat16
 NN = (((1,), (0,)), ((), ()))
@@ -54,11 +55,26 @@
     return (emb * lax.rsqrt(mean + EPS) * gain).astype(BF16)
 
 
-def rim_kernel(after, sig, rim, sem):
+def rim_kernel(after, sig, feat_hbm, taps_hbm, rim, small, feat_w, taps, sem):
     del after
-    copy = pltpu.make_async_copy(sig.at[pl.ds(sig.shape[0] - RIM, RIM), :], rim, sem)
-    copy.start()
-    copy.wait()
+    copies = [
+        pltpu.make_async_copy(sig.at[pl.ds(sig.shape[0] - RIM, RIM), :], rim, sem.at[0]),
+        pltpu.make_async_copy(feat_hbm, feat_w, sem.at[1]),
+        pltpu.make_async_copy(taps_hbm, taps, sem.at[2]),
+    ]
+    for copy in copies:
+        copy.start()
+    for copy in copies:
+        copy.wait()
+    heads, head_dim, _ = feat_w.shape
+    for h in range(heads):
+        small[h * head_dim : (h + 1) * head_dim, :] = feat_w[h].astype(F32)
+    parts, count, cols = taps.shape
+    small[heads * head_dim :, :] = jnp.zeros((small.shape[0] - heads * head_dim, LANES), F32)
+    for part in range(parts):
+        for j in range(cols // LANES):
+            at = heads * head_dim + TILE * (part * (cols // LANES) + j)
+            small[at : at + count, :] = taps[part, :, j * LANES : (j + 1) * LANES]
 
 
 def embed_kernel(sig, ew_a, ew_b, gain, normed, near_rim):
@@ -85,14 +101,15 @@
             c += 1
 
 
-def convolve(pad, taps, part, first, count, start, rows):
+def convolve(pad, small, dims, part, first, count, start, rows):
+    heads, head_dim, _, taps = dims
     out = []
     for j in range(count):
         total = None
-        for tap in range(taps.shape[1]):
-            at = start - taps.shape[1] + 1 + tap
-            weight = taps[part, tap : tap + 1, j * LANES : (j + 1) * LANES]
-            term = weight * pad[first + j, at : at + rows, :]
+        row = heads * head_dim + TILE * (part * count + j)
+        for tap in range(taps):
+            at = start - taps + 1 + tap
+            term = small[row + tap : row + tap + 1, :] * pad[first + j, at : at + rows, :]
             total = term if total is None else total + term
         out.append(total.astype(BF16))
     return jnp.concatenate(out, 1)
@@ -125,8 +142,8 @@
             c += 1
 
 
-def key_body(masks, normed, nrim, weight, taps, feat_w, kf, val, before, total, diag, ones, pad):
-    heads, head_dim, feat = feat_w.shape
+def key_body(masks, normed, nrim, weight, small, kf, val, before, total, diag, ones, pad, dims):
+    heads, head_dim, feat, _ = dims
     cols = val.shape[1]
     tiles = cols // LANES
     diag[...] = jnp.zeros_like(diag)
@@ -135,14 +152,15 @@
     of_col = lax.broadcasted_iota(jnp.int32, ones.shape, 1) // share
     ones[...] = jnp.where(of_row == of_col, 1.0, 0.0).astype(BF16)
     for h in range(heads):
-        diag[h * head_dim : (h + 1) * head_dim, h * feat : (h + 1) * feat] = feat_w[h]
+        here = slice(h * head_dim, (h + 1) * head_dim)
+        diag[here, h * feat : (h + 1) * feat] = small[here, :].astype(BF16)
     weights = (weight[1], weight[2])
     total[...] = jnp.zeros_like(total)
     rows = normed.shape[0]
     store_proj(pad, normed[...], weights, PAD)
     rim_rows(pad, nrim(), weights, masks)
-    key = convolve(pad, taps, 1, 0, tiles, PAD, rows)
-    value = convolve(pad, taps, 2, tiles, tiles, PAD, rows)
+    key = convolve(pad, small, dims, 1, 0, tiles, PAD, rows)
+    value = convolve(pad, small, dims, 2, tiles, tiles, PAD, rows)
     val[...] = value
     key_feat = features(key, diag, ones, heads, 2)
     kf[...] = key_feat
@@ -165,8 +183,8 @@
 
 
 def first_key_kernel(
-    masks, far_rim, near_rim, ew_a, ew_b, gain, normed, weight, taps, feat_w,
-    nrim, kf, val, before, total, diag, ones, pad,
+    masks, far_rim, near_rim, ew_a, ew_b, gain, normed, weight, small,
+    nrim, kf, val, before, total, diag, ones, pad, *, dims,
 ):
     half = ew_a.shape[0]
     own = jnp.broadcast_to(masks[0:1, :], (RIM, half)) == 0
@@ -183,29 +201,30 @@
         nrim[...] = normalize(dot(mine, ew_a[...]) + dot(other, ew_b[...]), gain[...])
         return nrim[...]
 
-    key_body(masks, normed, rows_ahead, weight, taps, feat_w, kf, val, before, total, diag, ones, pad)
+    key_body(
+        masks, normed, rows_ahead, weight, small, kf, val, before, total, diag, ones, pad, dims
+    )
 
 
 def key_kernel(
-    masks, normed, nrim, weight, taps, feat_w, ow_hbm,
-    kf, val, before, total, diag, ones, ow, pad, sem,
+    masks, normed, nrim, weight, small, ow_hbm,
+    kf, val, before, total, diag, ones, ow, pad, sem, *, dims,
 ):
     copy = pltpu.make_async_copy(ow_hbm, ow, sem)
     copy.start()
     key_body(
-        masks, normed, lambda: nrim[...], weight, taps, feat_w,
-        kf, val, before, total, diag, ones, pad,
+        masks, normed, lambda: nrim[...], weight, small,
+        kf, val, before, total, diag, ones, pad, dims,
     )
     copy.wait()
 
 
 def query_kernel(
-    masks, after, normed, nrim, weight, taps, diag, ones, kf, val, qf, out, pad, *, heads
+    masks, after, normed, nrim, weight, small, diag, ones, kf, val, qf, out, pad, *, dims
 ):
     del after
     rows = normed.shape[0]
-    feat = qf.shape[1] // heads
-    width = val.shape[1] // heads
+    heads, width, feat, _ = dims
     row = lax.broadcasted_iota(jnp.int32, (SUB, SUB), 0)
     col = lax.broadcasted_iota(jnp.int32, (SUB, SUB), 1)
     causal = row >= col
@@ -213,7 +232,7 @@
     one = jnp.ones((SUB, 2 * width), BF16)
     rim_rows(pad, nrim[...], (weight[0],), masks)
     store_proj(pad, normed[...], (weight[0],), PAD)
-    query = convolve(pad, taps, 0, 0, weight.shape[2] // LANES, PAD, rows)
+    query = convolve(pad, small, dims, 0, 0, weight.shape[2] // LANES, PAD, rows)
     query_feat = features(query, diag, ones, heads, heads)
     qf[...] = query_feat
     for b in range(rows // SUB):
@@ -350,20 +369,26 @@
     )
     second = masks[:1, :feat] > 0
     ew_other = swap(embed_weight, "rep", 1)
-    (far_rim,) = call(
+    conv_parts = conv_weight.transpose(1, 0, 2)
+    small_rows = heads * head_dim + TILE * conv_parts.shape[0] * (cols // LANES)
+    far_rim, small_own = call(
         rim_kernel,
-        [(masks, None), (signal, hbm)],
-        [((RIM, depth), BF16, None)],
+        [(masks, None), (signal, hbm), (feature_weight, hbm), (conv_parts, hbm)],
+        [((RIM, depth), BF16, None), ((small_rows, LANES), F32, None)],
         "rim",
-        [pltpu.SemaphoreType.DMA],
+        [
+            pltpu.VMEM(feature_weight.shape, BF16),
+            pltpu.VMEM(conv_parts.shape, F32),
+            pltpu.SemaphoreType.DMA((3,)),
+        ],
         (1 << 30, 1 << 20),
     )
     ring = [(2 * i, 2 * i + 2) for i in range(devices - 1)] + [(2 * devices - 2, 2 * devices - 1)]
     ring += [(2 * i + 1, 2 * i - 1) for i in range(1, devices)] + [(1, 0)]
     far_rim = lax.ppermute(far_rim, ("tm", "rep"), ring)
     wqkv = [qkv_weight.transpose(1, 0, 2), swap(qkv_weight.transpose(1, 0, 2), "rep", 1)]
-    taps = [conv_weight.transpose(1, 0, 2), swap(conv_weight.transpose(1, 0, 2), "rep", 1)]
-    feat_w = [feature_weight, swap(feature_weight, "rep", 1)]
+    small = [small_own, swap(lax.optimization_barrier((small_own, ew_other))[0], "rep", 1)]
+    dims = (heads, head_dim, feat, conv_weight.shape[0])
     gain = norm_gain.reshape(1, width)
 
     normed, near_rim = call(
@@ -386,10 +411,10 @@
     pads = pltpu.VMEM((2 * cols // LANES, PAD + rows, LANES), F32)
     key_work = (6 * rows * width * 2 * cols, 4 << 20)
     nrim, *other = call(
-        first_key_kernel,
+        functools.partial(first_key_kernel, dims=dims),
         [
             *vmem(masks, far_rim, near_rim, embed_weight, ew_other, gain, normed),
-            *vmem(wqkv[1], taps[1], feat_w[1]),
+            *vmem(wqkv[1], small[1]),
         ],
         [((RIM, width), BF16, None), *key_outs],
         "keys_other",
@@ -398,8 +423,8 @@
     )
     back = swap(other[3].astype(BF16), "rep", 1).astype(F32)
     own = call(
-        key_kernel,
-        [*vmem(masks, normed, nrim, wqkv[0], taps[0], feat_w[0]), (out_weight, hbm)],
+        functools.partial(key_kernel, dims=dims),
+        [*vmem(masks, normed, nrim, wqkv[0], small[0]), (out_weight, hbm)],
         [*key_outs, (out_weight.shape, BF16, None)],
         "keys_own",
         [pads, pltpu.SemaphoreType.DMA],
@@ -409,8 +434,8 @@
 
     def query(k, keys, after):
         qf[k], local[k] = call(
-            functools.partial(query_kernel, heads=heads),
-            vmem(masks, after, normed, nrim, wqkv[k], taps[k], *keys[4:6], *keys[:2]),
+            functools.partial(query_kernel, dims=dims),
+            vmem(masks, after, normed, nrim, wqkv[k], small[k], *keys[4:6], *keys[:2]),
             [((rows, feats), BF16, None), ((rows, 2 * cols), F32, None)],
             "queries",
             [pltpu.VMEM((cols // LANES, PAD + rows, LANES), F32)],

time: 29 us -> 29 us (level)
    ppermute x11 -> x10, waiting for transfers between devices: 3.44 us -> 3.27 us  [swap(): return lax.ppermute(array, axis, [(i, i ^ by) for i in range(devices)])]
    ppermute x11 -> x10, starting transfers between devices: 8.03 us -> 8.06 us  [swap(): return lax.ppermute(array, axis, [(i, i ^ by) for i in range(devices)])]
  transfers between devices with their start and end apart: 12 -> 11, of which waited for: 6 -> 5; matrix products, arithmetic and copies ran while one was open for 0% -> 0% of each run, Pallas kernels for 36% -> 36%
where the time goes in v7:
time: 29 us; the launch traced here: 28.8 us
  Pallas kernels  14.3 us (49%)
  starting transfers between devices  10.7 us (37%)
  waiting for transfers between devices  3.27 us (11%)
    pallas_call x8, Pallas kernels, call(): pl.pallas_call(kernel, in_specs=[spec(p) for _, p in ins], out_specs=[spe...  14.3 us
    ppermute x10, starting transfers between devices, swap(): return lax.ppermute(array, axis, [(i, i ^ by) for i in range(devices)])  8.06 us
    ppermute x10, waiting for transfers between devices, swap(): return lax.ppermute(array, axis, [(i, i ^ by) for i in range(devices)])  3.27 us
    ppermute x1, starting transfers between devices, shards(): far_rim = lax.ppermute(far_rim, ('tm', 'rep'), ring)  2.61 us
  transfers between devices with their start and end apart: 11, of which 5 were waited for; matrix products, arithmetic and copies ran while one was open for 0% of the time, Pallas kernels for 36%

profile of v7, /device:TPU:0, one launch (start us, length us, event | category | flops | bytes accessed | tf_op | source)
XLA Modules:
  0.0 28.8 jit_solution(5662168476697934464)
XLA Ops:
  0.0 0.1 stack.27
  0.1 0.1 broadcast_in_dim.60.after.masks
  0.2 0.5 %collective-permute-start = (bf16[512,512]{1,0:T(8,128)(2,1)}, bf16[512,512]{1,0:T(8,128)(2,1)S(1)}, u32[]{:S(2)}, u32[]{:S(2)}) collective-permute-start(bf16[512,512]{1,0:T(8,128)(2,1)} %ew_a.1), channel_id=1, source_target_pairs={{0,1},{1,0},{2,3},{3,2},{4,5},{5,4},{6,7},{7,6},{8,9},{9,8},{10,11... | collective-permute-start | bytes 1572872 | tf_op jit(solution)/shard_map/ppermute | solution.py:312
  0.7 1.0 %rim.1 = (bf16[16,1024]{1,0:T(8,128)(2,1)S(1)}, f32[304,128]{1,0:T(8,128)S(1)}) custom-call(f32[6,512]{1,0:T(8,128)S(1)} %broadcast_in_dim.60.after.masks, bf16[2048,1024]{1,0:T(8,128)(2,1)} %sig.1, bf16[4,64,128]{2,1,0:T(8,128)(2,1)} %feat_hbm, f32[3,4,256]{2,1,0:T(4,128)} %bitcast.24), custom_call_target="tpu_custom_call" | custom-call | flops 8589934592 | bytes 1048576 | tf_op jit(solution)/shard_map/rim/pallas_call | solution.py:37
  1.7 2.6 %collective-permute-start.1 = (bf16[16,1024]{1,0:T(8,128)(2,1)S(1)}, bf16[16,1024]{1,0:T(8,128)(2,1)S(1)}, u32[]{:S(2)}, u32[]{:S(2)}) collective-permute-start(bf16[16,1024]{1,0:T(8,128)(2,1)S(1)} %get-tuple-element.43), channel_id=1, source_target_pairs={{0,2},{2,4},{4,6},{6,8},{8,10},{10,12},{12,14},{14,15},{3,1},{5,3}... | collective-permute-start | bytes 98312 | tf_op jit(solution)/shard_map/ppermute | solution.py:388
  4.3 0.0 collective-permute-start.2
  4.3 0.0 collective-permute-done.ew_b
  4.3 0.6 %collective-permute-start.3 = (f32[304,128]{1,0:T(8,128)S(1)}, f32[304,128]{1,0:T(8,128)S(1)}, u32[]{:S(2)}, u32[]{:S(2)}) collective-permute-start(f32[304,128]{1,0:T(8,128)S(1)} %get-tuple-element.47.small), channel_id=1, source_target_pairs={{0,1},{1,0},{2,3},{3,2},{4,5},{5,4},{6,7},{7,6},{8,9},{9,8},{10,11... | collective-permute-start | bytes 466952 | tf_op jit(solution)/shard_map/ppermute | solution.py:312
  4.9 1.4 %embed.1 = (bf16[1024,512]{1,0:T(8,128)(2,1)S(1)}, bf16[16,1024]{1,0:T(8,128)(2,1)S(1)}) custom-call(bf16[2048,1024]{1,0:T(8,128)(2,1)S(1)} %copy-done, bf16[512,512]{1,0:T(8,128)(2,1)S(1)} %copy-done.2, bf16[512,512]{1,0:T(8,128)(2,1)S(1)} %collective-permute-done.ew_b, f32[1,512]{1,0:T(1,128)S(1)} %bitcast.22), custom_call_target="tpu_custom_call" | custom-call | flops 8589934592 | bytes 4194304 | tf_op jit(solution)/shard_map/embed/pallas_call | solution.py:37
  6.3 0.0 collective-permute-done.1.far_rim
  6.4 0.5 %collective-permute-done.3.small = f32[304,128]{1,0:T(8,128)S(1)} collective-permute-done((f32[304,128]{1,0:T(8,128)S(1)}, f32[304,128]{1,0:T(8,128)S(1)}, u32[]{:S(2)}, u32[]{:S(2)}) %collective-permute-start.3) | collective-permute-done | bytes 155680 | tf_op jit(solution)/shard_map/ppermute | solution.py:312
  6.8 0.0 collective-permute-done.2.weight
  6.8 2.4 %keys_other.1 = (bf16[16,512]{1,0:T(8,128)(2,1)S(1)}, bf16[1024,512]{1,0:T(8,128)(2,1)S(1)}, bf16[1024,256]{1,0:T(8,128)(2,1)S(1)}, f32[4,272,128]{2,1,0:T(8,128...) custom-call(f32[6,512]{1,0:T(8,128)S(1)} %broadcast_in_dim.60.after.masks, ...), custom_call_target="tpu_custom_call" | custom-call | flops 12884901888 | bytes 4194304 | tf_op jit(solution)/shard_map/keys_other/pallas_call | solution.py:37
  9.3 0.2 collective-permute-start.4
  9.5 2.1 %keys_own.1 = (bf16[1024,512]{1,0:T(8,128)(2,1)S(1)}, bf16[1024,256]{1,0:T(8,128)(2,1)S(1)}, f32[4,272,128]{2,1,0:T(8,128)S(1)}, f32[272,128]{1,0:T(8,128)S(1)},...) custom-call(f32[6,512]{1,0:T(8,128)S(1)} %broadcast_in_dim.60.after.masks, ...), custom_call_target="tpu_custom_call" | custom-call | flops 12884901888 | bytes 4194304 | tf_op jit(solution)/shard_map/keys_own/pallas_call | solution.py:37
  11.6 2.6 %collective-permute-start.5 = (bf16[272,128]{1,0:T(8,128)(2,1)S(1)}, bf16[272,128]{1,0:T(8,128)(2,1)S(1)}, u32[]{:S(2)}, u32[]{:S(2)}) collective-permute-start(bf16[272,128]{1,0:T(8,128)(2,1)S(1)} %fusion.5.after), channel_id=1, source_target_pairs={{0,6},{2,4},{4,2},{6,0},{8,14},{10,12},{12,10},{14,8},{1,7},{3,5},... | collective-permute-start | bytes 208904 | tf_op jit(solution)/shard_map/ppermute | solution.py:312
  14.2 0.4 %collective-permute-start.6 = (bf16[272,128]{1,0:T(8,128)(2,1)S(1)}, bf16[272,128]{1,0:T(8,128)(2,1)S(1)}, u32[]{:S(2)}, u32[]{:S(2)}) collective-permute-start(bf16[272,128]{1,0:T(8,128)(2,1)S(1)} %fusion.5.after), channel_id=1, source_target_pairs={{0,4},{2,6},{4,0},{6,2},{8,12},{10,14},{12,8},{14,10},{1,5},{3,7},... | collective-permute-start | bytes 208904 | tf_op jit(solution)/shard_map/ppermute | solution.py:312
  14.7 0.7 %collective-permute-start.7 = (bf16[272,128]{1,0:T(8,128)(2,1)S(1)}, bf16[272,128]{1,0:T(8,128)(2,1)S(1)}, u32[]{:S(2)}, u32[]{:S(2)}) collective-permute-start(bf16[272,128]{1,0:T(8,128)(2,1)S(1)} %fusion.5.after), channel_id=1, source_target_pairs={{0,2},{2,0},{4,6},{6,4},{8,10},{10,8},{12,14},{14,12},{1,3},{3,1},... | collective-permute-start | bytes 208904 | tf_op jit(solution)/shard_map/ppermute | solution.py:312
  15.4 2.5 %queries.3 = (bf16[1024,512]{1,0:T(8,128)(2,1)S(1)}, f32[1024,512]{1,0:T(8,128)S(1)}) custom-call(f32[6,512]{1,0:T(8,128)S(1)} %broadcast_in_dim.60.after.masks, bf16[272,128]{1,0:T(8,128)(2,1)S(1)} %fusion.5.after, bf16[1024,512]{1,0:T(8,128)(2,1)S(1)} %get-tuple-element.40.normed, bf16[16,512]{1,0:T(8,128)(2,1)S(1)} %get-tuple-element.48.nrim, ...), custom_call_target="tpu_custom_call" | custom-call | flops 6442450944 | bytes 4194304 | tf_op jit(solution)/shard_map/queries/pallas_call | solution.py:37
  17.9 0.0 collective-permute-done.5
  17.9 0.7 %collective-permute-done.6 = bf16[272,128]{1,0:T(8,128)(2,1)S(1)} collective-permute-done((bf16[272,128]{1,0:T(8,128)(2,1)S(1)}, bf16[272,128]{1,0:T(8,128)(2,1)S(1)}, u32[]{:S(2)}, u32[]{:S(2)}) %collective-permute-start.6) | collective-permute-done | bytes 69664 | tf_op jit(solution)/shard_map/ppermute | solution.py:312
  18.6 0.4 %collective-permute-done.7 = bf16[272,128]{1,0:T(8,128)(2,1)S(1)} collective-permute-done((bf16[272,128]{1,0:T(8,128)(2,1)S(1)}, bf16[272,128]{1,0:T(8,128)(2,1)S(1)}, u32[]{:S(2)}, u32[]{:S(2)}) %collective-permute-start.7) | collective-permute-done | bytes 69664 | tf_op jit(solution)/shard_map/ppermute | solution.py:312
  19.0 0.1 fusion.4.after
  19.1 3.0 %collective-permute-start.8 = (bf16[272,128]{1,0:T(8,128)(2,1)S(1)}, bf16[272,128]{1,0:T(8,128)(2,1)S(1)}, u32[]{:S(2)}, u32[]{:S(2)}) collective-permute-start(bf16[272,128]{1,0:T(8,128)(2,1)S(1)} %fusion.4.after), channel_id=1, source_target_pairs={{0,8},{2,10},{4,12},{6,14},{8,0},{10,2},{12,4},{14,6},{1,9},{3,11}... | collective-permute-start | bytes 208904 | tf_op jit(solution)/shard_map/ppermute | solution.py:312
  22.0 0.0 collective-permute-start.10
  22.0 2.5 %queries.2 = (bf16[1024,512]{1,0:T(8,128)(2,1)S(1)}, f32[1024,512]{1,0:T(8,128)S(1)}) custom-call(f32[6,512]{1,0:T(8,128)S(1)} %broadcast_in_dim.60.after.masks, bf16[272,128]{1,0:T(8,128)(2,1)S(1)} %fusion.4.after, bf16[1024,512]{1,0:T(8,128)(2,1)S(1)} %get-tuple-element.40.normed, bf16[16,512]{1,0:T(8,128)(2,1)S(1)} %get-tuple-element.48.nrim, ...), custom_call_target="tpu_custom_call" | custom-call | flops 6442450944 | bytes 4194304 | tf_op jit(solution)/shard_map/queries/pallas_call | solution.py:37
  24.6 1.2 %collective-permute-done.8 = bf16[272,128]{1,0:T(8,128)(2,1)S(1)} collective-permute-done((bf16[272,128]{1,0:T(8,128)(2,1)S(1)}, bf16[272,128]{1,0:T(8,128)(2,1)S(1)}, u32[]{:S(2)}, u32[]{:S(2)}) %collective-permute-start.8) | collective-permute-done | bytes 69664 | tf_op jit(solution)/shard_map/ppermute | solution.py:312
  25.8 0.1 fusion
  25.9 0.1 collective-permute-start.9
  26.0 0.8 %attend_own.1.partial = f32[1024,512]{1,0:T(8,128)S(1)} custom-call(bf16[1024,512]{1,0:T(8,128)(2,1)S(1)} %get-tuple-element.64.qf, f32[1024,512]{1,0:T(8,128)S(1)} %get-tuple-element.65.local, f32[4,272,128]{2,1,0:T(8,128)S(1)} %get-tuple-element.66.before, f32[272,128]{1,0:T(8,128)S(1)} %get-tuple-element.67.state, ...), custom_call_target="tpu_custom_call" | custom-call | flops 4294967296 | bytes 4194304 | tf_op jit(solution)/shard_map/attend_own/pallas_call | solution.py:37
  26.7 0.5 %collective-permute-done.9.state = bf16[272,128]{1,0:T(8,128)(2,1)S(1)} collective-permute-done((bf16[272,128]{1,0:T(8,128)(2,1)S(1)}, bf16[272,128]{1,0:T(8,128)(2,1)S(1)}, u32[]{:S(2)}, u32[]{:S(2)}) %collective-permute-start.9) | collective-permute-done | bytes 69664 | tf_op jit(solution)/shard_map/ppermute | solution.py:312
  27.2 1.6 %attend_other.1 = bf16[1024,512]{1,0:T(8,128)(2,1)} custom-call(bf16[1024,512]{1,0:T(8,128)(2,1)S(1)} %get-tuple-element.55.qf, f32[1024,512]{1,0:T(8,128)S(1)} %get-tuple-element.56.local, f32[4,272,128]{2,1,0:T(8,128)S(1)} %get-tuple-element.57.before, bf16[272,128]{1,0:T(8,128)(2,1)S(1)} %collective-permute-done.9.state, ...), custom_call_target="tpu_custom_call" | custom-call | flops 4294967296 | bytes 4194304 | tf_op jit(solution)/shard_map/attend_other/pallas_call | solution.py:37
  (14 shorter events, 0.1 us)
Async XLA Ops:
  0.2 4.2 %collective-permute-start = (bf16[512,512]{1,0:T(8,128)(2,1)}, bf16[512,512]{1,0:T(8,128)(2,1)S(1)}, u32[]{:S(2)}, u32[]{:S(2)}) collective-permute-start(bf16[512,512]{1,0:T(8,128)(2,1)} %ew_a.1), channel_id=1, source_target_pairs={{0,1},{1,0},{2,3},{3,2},{4,5},{5,4},{6,7},{7,6},{8,9},{9,8},{10,11... | collective-permute-start | bytes 1572872 | tf_op jit(solution)/shard_map/ppermute | solution.py:312
  0.6 3.7 %copy-start.1 = (bf16[512,3,256]{2,0,1:T(8,128)(2,1)S(1)}, bf16[512,3,256]{2,0,1:T(8,128)(2,1)}, u32[]{:S(2)}) copy-start(bf16[512,3,256]{2,0,1:T(8,128)(2,1)} %param.10) | copy-start | bytes 2359300
  0.6 4.3 %copy-start = (bf16[2048,1024]{1,0:T(8,128)(2,1)S(1)}, bf16[2048,1024]{1,0:T(8,128)(2,1)}, u32[]{:S(2)}) copy-start(bf16[2048,1024]{1,0:T(8,128)(2,1)} %sig.1) | copy-start | bytes 12582916
  0.6 4.3 %copy-start.2 = (bf16[512,512]{1,0:T(8,128)(2,1)S(1)}, bf16[512,512]{1,0:T(8,128)(2,1)}, u32[]{:S(2)}) copy-start(bf16[512,512]{1,0:T(8,128)(2,1)} %ew_a.1) | copy-start | bytes 1572868
  0.6 4.3 %copy-start.3 = (f32[512]{0:T(512)S(1)}, f32[512]{0:T(512)}, u32[]{:S(2)}) copy-start(f32[512]{0:T(512)} %param.9) | copy-start | bytes 6148
  1.7 4.6 %collective-permute-start.1 = (bf16[16,1024]{1,0:T(8,128)(2,1)S(1)}, bf16[16,1024]{1,0:T(8,128)(2,1)S(1)}, u32[]{:S(2)}, u32[]{:S(2)}) collective-permute-start(bf16[16,1024]{1,0:T(8,128)(2,1)S(1)} %get-tuple-element.43), channel_id=1, source_target_pairs={{0,2},{2,4},{4,6},{6,8},{8,10},{10,12},{12,14},{14,15},{3,1},{5,3}... | collective-permute-start | bytes 98312 | tf_op jit(solution)/shard_map/ppermute | solution.py:388
  4.3 2.5 %collective-permute-start.2 = (bf16[3,512,256]{2,1,0:T(8,128)(2,1)S(1)}, bf16[3,512,256]{2,1,0:T(8,128)(2,1)S(1)}, u32[]{:S(2)}, u32[]{:S(2)}) collective-permute-start(bf16[3,512,256]{2,1,0:T(8,128)(2,1)S(1)} %bitcast.19), channel_id=1, source_target_pairs={{0,1},{1,0},{2,3},{3,2},{4,5},{5,4},{6,7},{7,6},{8,9},{9,8},{10,11... | collective-permute-start | bytes 2359304 | tf_op jit(solution)/shard_map/ppermute | solution.py:312
  4.3 2.5 %collective-permute-start.3 = (f32[304,128]{1,0:T(8,128)S(1)}, f32[304,128]{1,0:T(8,128)S(1)}, u32[]{:S(2)}, u32[]{:S(2)}) collective-permute-start(f32[304,128]{1,0:T(8,128)S(1)} %get-tuple-element.47.small), channel_id=1, source_target_pairs={{0,1},{1,0},{2,3},{3,2},{4,5},{5,4},{6,7},{7,6},{8,9},{9,8},{10,11... | collective-permute-start | bytes 466952 | tf_op jit(solution)/shard_map/ppermute | solution.py:312
  9.3 2.3 %collective-permute-start.4 = (bf16[272,128]{1,0:T(8,128)(2,1)S(1)}, bf16[272,128]{1,0:T(8,128)(2,1)S(1)}, u32[]{:S(2)}, u32[]{:S(2)}) collective-permute-start(bf16[272,128]{1,0:T(8,128)(2,1)S(1)} %convert_element_type.35), channel_id=1, source_target_pairs={{0,1},{1,0},{2,3},{3,2},{4,5},{5,4},{6,7},{7,6},{8,9},{9,8},{10,11... | collective-permute-start | bytes 208904 | tf_op jit(solution)/shard_map/ppermute | solution.py:312
  11.6 6.3 %collective-permute-start.5 = (bf16[272,128]{1,0:T(8,128)(2,1)S(1)}, bf16[272,128]{1,0:T(8,128)(2,1)S(1)}, u32[]{:S(2)}, u32[]{:S(2)}) collective-permute-start(bf16[272,128]{1,0:T(8,128)(2,1)S(1)} %fusion.5.after), channel_id=1, source_target_pairs={{0,6},{2,4},{4,2},{6,0},{8,14},{10,12},{12,10},{14,8},{1,7},{3,5},... | collective-permute-start | bytes 208904 | tf_op jit(solution)/shard_map/ppermute | solution.py:312
  14.2 4.4 %collective-permute-start.6 = (bf16[272,128]{1,0:T(8,128)(2,1)S(1)}, bf16[272,128]{1,0:T(8,128)(2,1)S(1)}, u32[]{:S(2)}, u32[]{:S(2)}) collective-permute-start(bf16[272,128]{1,0:T(8,128)(2,1)S(1)} %fusion.5.after), channel_id=1, source_target_pairs={{0,4},{2,6},{4,0},{6,2},{8,12},{10,14},{12,8},{14,10},{1,5},{3,7},... | collective-permute-start | bytes 208904 | tf_op jit(solution)/shard_map/ppermute | solution.py:312
  14.7 4.3 %collective-permute-start.7 = (bf16[272,128]{1,0:T(8,128)(2,1)S(1)}, bf16[272,128]{1,0:T(8,128)(2,1)S(1)}, u32[]{:S(2)}, u32[]{:S(2)}) collective-permute-start(bf16[272,128]{1,0:T(8,128)(2,1)S(1)} %fusion.5.after), channel_id=1, source_target_pairs={{0,2},{2,0},{4,6},{6,4},{8,10},{10,8},{12,14},{14,12},{1,3},{3,1},... | collective-permute-start | bytes 208904 | tf_op jit(solution)/shard_map/ppermute | solution.py:312
  19.1 6.8 %collective-permute-start.8 = (bf16[272,128]{1,0:T(8,128)(2,1)S(1)}, bf16[272,128]{1,0:T(8,128)(2,1)S(1)}, u32[]{:S(2)}, u32[]{:S(2)}) collective-permute-start(bf16[272,128]{1,0:T(8,128)(2,1)S(1)} %fusion.4.after), channel_id=1, source_target_pairs={{0,8},{2,10},{4,12},{6,14},{8,0},{10,2},{12,4},{14,6},{1,9},{3,11}... | collective-permute-start | bytes 208904 | tf_op jit(solution)/shard_map/ppermute | solution.py:312
  22.0 5.2 %collective-permute-start.10 = (bf16[256,512]{1,0:T(8,128)(2,1)S(1)}, bf16[256,512]{1,0:T(8,128)(2,1)S(1)}, u32[]{:S(2)}, u32[]{:S(2)}) collective-permute-start(bf16[256,512]{1,0:T(8,128)(2,1)S(1)} %get-tuple-element.59.weight), channel_id=1, source_target_pairs={{0,1},{1,0},{2,3},{3,2},{4,5},{5,4},{6,7},{7,6},{8,9},{9,8},{10,11... | collective-permute-start | bytes 786440 | tf_op jit(solution)/shard_map/ppermute | solution.py:312
  25.9 1.3 %collective-permute-start.9 = (bf16[272,128]{1,0:T(8,128)(2,1)S(1)}, bf16[272,128]{1,0:T(8,128)(2,1)S(1)}, u32[]{:S(2)}, u32[]{:S(2)}) collective-permute-start(bf16[272,128]{1,0:T(8,128)(2,1)S(1)} %get-tuple-element.68), channel_id=1, source_target_pairs={{0,1},{1,0},{2,3},{3,2},{4,5},{5,4},{6,7},{7,6},{8,9},{9,8},{10,11... | collective-permute-start | bytes 208904 | tf_op jit(solution)/shard_map/ppermute | solution.py:312

commit v8 on v6

--- a/solution.py
+++ b/solution.py
@@ -199,8 +199,37 @@
     copy.wait()
 
 
+def pair_rhs(state, pair, heads, width):
+    feat = state.shape[1]
+    zero = jnp.zeros((width, feat), BF16)
+    rows = []
+    for k in range(2):
+        h = pair * 2 + k
+        rows.append((state[h * width : (h + 1) * width], k))
+    for k in range(2):
+        at = heads * width + pair * 2 + k
+        rows.append((jnp.broadcast_to(state[at : at + 1], (width, feat)), k))
+    return jnp.concatenate(
+        [jnp.concatenate([r, zero] if k == 0 else [zero, r], 1) for r, k in rows], 0
+    )
+
+
+def attend(qf, local, state, rows, heads):
+    feat = qf.shape[1] // heads
+    width = local.shape[1] // heads // 2
+    out = []
+    for pair in range(heads // 2):
+        both = local[rows, pair * 4 * width : (pair + 1) * 4 * width] + dot(
+            qf[rows, pair * 2 * feat : (pair + 1) * 2 * feat],
+            pair_rhs(state, pair, heads, width),
+            NT,
+        )
+        out.append((both[:, : 2 * width] / both[:, 2 * width :]).astype(BF16))
+    return jnp.concatenate(out, 1)
+
+
 def query_kernel(
-    masks, after, normed, nrim, weight, taps, diag, ones, kf, val, qf, out, pad, *, heads
+    masks, after, normed, nrim, weight, taps, diag, ones, kf, val, before, qf, out, pad, *, heads
 ):
     del after
     rows = normed.shape[0]
@@ -226,62 +255,30 @@
                 weights.append(jnp.where(causal, scores, 0.0).astype(BF16))
             vp = val[sub, pair * 2 * width : (pair + 1) * 2 * width]
             both = dot(jnp.concatenate(weights, 0), jnp.concatenate([vp, one], 1))
-            out[sub, pair * 4 * width : (pair + 1) * 4 * width] = jnp.where(
-                left, both[:SUB], both[SUB:]
-            )
-
-
-def attend(qf, local, before, state_in, b, heads):
-    feat = qf.shape[1] // heads
-    width = local.shape[1] // heads // 2
-    zero = jnp.zeros((width, feat), BF16)
-    rows = slice(b * SUB, (b + 1) * SUB)
-    state = (before[b] + state_in).astype(BF16)
-    out = []
-    for pair in range(heads // 2):
-        h = pair * 2
-        s0, s1 = (state[(h + k) * width : (h + k + 1) * width] for k in range(2))
-        t0, t1 = (
-            jnp.broadcast_to(
-                state[heads * width + h + k : heads * width + h + k + 1], (width, feat)
-            )
-            for k in range(2)
-        )
-        rhs = jnp.concatenate(
-            [
-                jnp.concatenate([s0, zero], 1),
-                jnp.concatenate([zero, s1], 1),
-                jnp.concatenate([t0, zero], 1),
-                jnp.concatenate([zero, t1], 1),
-            ],
-            0,
-        )
-        both = local[rows, pair * 4 * width : (pair + 1) * 4 * width] + dot(
-            qf[rows, pair * 2 * feat : (pair + 1) * 2 * feat], rhs, NT
-        )
-        out.append((both[:, : 2 * width] / both[:, 2 * width :]).astype(BF16))
-    return jnp.concatenate(out, 1)
-
-
-def own_kernel(qf, local, before, state, weight, out, *, heads):
-    attended = [
-        attend(qf, local, before, state[...], b, heads) for b in range(qf.shape[0] // SUB)
-    ]
-    out[...] = dot(jnp.concatenate(attended, 0), weight[...])
-
-
-def last_kernel(qf, local, before, state, weight, partial, out, buf, sem, *, heads):
+            total = jnp.where(left, both[:SUB], both[SUB:])
+            if b > 0:
+                total = total + dot(
+                    query_feat[sub, pair * 2 * feat : (pair + 1) * 2 * feat],
+                    pair_rhs(before[b].astype(BF16), pair, heads, width),
+                    NT,
+                )
+            out[sub, pair * 4 * width : (pair + 1) * 4 * width] = total
+
+
+def own_kernel(qf, local, state, weight, out, *, heads):
+    attended = attend(qf, local, state[...].astype(BF16), slice(None), heads)
+    out[...] = dot(attended, weight[...])
+
+
+def last_kernel(qf, local, state, weight, partial, out, buf, sem, *, heads):
     copies = []
-    state_in = state[...].astype(F32)
-    per = buf.shape[1] // SUB
+    per = buf.shape[1]
     for s in range(buf.shape[0]):
-        attended = [
-            attend(qf, local, before, state_in, s * per + b, heads) for b in range(per)
-        ]
-        rows = slice(s * per * SUB, (s + 1) * per * SUB)
-        buf[s] = (partial[rows, :] + dot(jnp.concatenate(attended, 0), weight[...])).astype(BF16)
+        rows = slice(s * per, (s + 1) * per)
+        attended = attend(qf, local, state[...], rows, heads)
+        buf[s] = (partial[rows, :] + dot(attended, weight[...])).astype(BF16)
         copies.append(
-            pltpu.make_async_copy(buf.at[s], out.at[pl.ds(s * per * SUB, per * SUB), :], sem.at[s])
+            pltpu.make_async_copy(buf.at[s], out.at[pl.ds(s * per, per), :], sem.at[s])
         )
         copies[-1].start()
     for copy in copies:
@@ -410,7 +407,7 @@
     def query(k, keys, after):
         qf[k], local[k] = call(
             functools.partial(query_kernel, heads=heads),
-            vmem(masks, after, normed, nrim, wqkv[k], taps[k], *keys[4:6], *keys[:2]),
+            vmem(masks, after, normed, nrim, wqkv[k], taps[k], *keys[4:6], *keys[:3]),
             [((rows, feats), BF16, None), ((rows, 2 * cols), F32, None)],
             "queries",
             [pltpu.VMEM((cols // LANES, PAD + rows, LANES), F32)],
@@ -426,7 +423,7 @@
 
     (partial,) = call(
         functools.partial(own_kernel, heads=heads),
-        vmem(qf[0], local[0], own[2], state_own, ow[0]),
+        vmem(qf[0], local[0], state_own, ow[0]),
         [((rows, width), F32, None)],
         "attend_own",
         (),
@@ -434,7 +431,7 @@
     )
     return call(
         functools.partial(last_kernel, heads=heads),
-        vmem(qf[1], local[1], other[2], state_other, ow[1], partial),
+        vmem(qf[1], local[1], state_other, ow[1], partial),
         [((rows, width), BF16, hbm)],
         "attend_other",
         [pltpu.VMEM((2, rows // 2, width), BF16), pltpu.SemaphoreType.DMA((2,))],

time: 29 us -> 29 us (level)
  waiting for transfers between devices: 3.44 us -> 2.74 us
  Pallas kernels: 14.4 us -> 15.1 us
    pallas_call x8, Pallas kernels: 14.4 us -> 15.1 us  [call(): pl.pallas_call(kernel, in_specs=[spec(p) for _, p in ins], out_specs=[spe...]
    ppermute x11, waiting for transfers between devices: 3.44 us -> 2.74 us  [swap(): return lax.ppermute(array, axis, [(i, i ^ by) for i in range(devices)])]
  transfers between devices with their start and end apart: 12 -> 12, of which waited for: 6 -> 6; matrix products, arithmetic and copies ran while one was open for 0% -> 0% of each run, Pallas kernels for 36% -> 39%
where the time goes in v8:
time: 29 us; the launch traced here: 28.9 us
  Pallas kernels  15.1 us (52%)
  starting transfers between devices  10.5 us (36%)
  waiting for transfers between devices  2.74 us (9%)
    pallas_call x8, Pallas kernels, call(): pl.pallas_call(kernel, in_specs=[spec(p) for _, p in ins], out_specs=[spe...  15.1 us
    ppermute x11, starting transfers between devices, swap(): return lax.ppermute(array, axis, [(i, i ^ by) for i in range(devices)])  8.03 us
    ppermute x11, waiting for transfers between devices, swap(): return lax.ppermute(array, axis, [(i, i ^ by) for i in range(devices)])  2.74 us
    ppermute x1, starting transfers between devices, shards(): far_rim = lax.ppermute(far_rim, ('tm', 'rep'), ring)  2.46 us
  transfers between devices with their start and end apart: 12, of which 6 were waited for; matrix products, arithmetic and copies ran while one was open for 0% of the time, Pallas kernels for 39%

profile of v8, /device:TPU:0, one launch (start us, length us, event | category | flops | bytes accessed | tf_op | source)
XLA Modules:
  0.0 28.9 jit_solution(7777101984012050053)
XLA Ops:
  0.0 0.1 stack.27
  0.1 0.1 broadcast_in_dim.60.after.masks
  0.2 0.0 copy-start.2
  0.2 0.0 copy-start.5
  0.2 0.5 %collective-permute-start = (bf16[512,512]{1,0:T(8,128)(2,1)}, bf16[512,512]{1,0:T(8,128)(2,1)S(1)}, u32[]{:S(2)}, u32[]{:S(2)}) collective-permute-start(bf16[512,512]{1,0:T(8,128)(2,1)} %ew_a.1), channel_id=1, source_target_pairs={{0,1},{1,0},{2,3},{3,2},{4,5},{5,4},{6,7},{7,6},{8,9},{9,8},{10,11... | collective-permute-start | bytes 1572872 | tf_op jit(solution)/shard_map/ppermute | solution.py:290
  0.7 1.0 %rim.1 = bf16[16,1024]{1,0:T(8,128)(2,1)S(1)} custom-call(f32[6,512]{1,0:T(8,128)S(1)} %broadcast_in_dim.60.after.masks, bf16[2048,1024]{1,0:T(8,128)(2,1)} %sig.1), custom_call_target="tpu_custom_call" | custom-call | flops 8589934592 | bytes 1048576 | tf_op jit(solution)/shard_map/rim/pallas_call | solution.py:36
  1.8 2.5 %collective-permute-start.1 = (bf16[16,1024]{1,0:T(8,128)(2,1)S(1)}, bf16[16,1024]{1,0:T(8,128)(2,1)S(1)}, u32[]{:S(2)}, u32[]{:S(2)}) collective-permute-start(bf16[16,1024]{1,0:T(8,128)(2,1)S(1)} %rim.1), channel_id=1, source_target_pairs={{0,2},{2,4},{4,6},{6,8},{8,10},{10,12},{12,14},{14,15},{3,1},{5,3}... | collective-permute-start | bytes 98312 | tf_op jit(solution)/shard_map/ppermute | solution.py:360
  4.3 0.0 collective-permute-start.2
  4.3 0.5 %collective-permute-start.3 = (f32[3,4,256]{2,1,0:T(4,128)S(1)}, f32[3,4,256]{2,1,0:T(4,128)S(1)}, u32[]{:S(2)}, u32[]{:S(2)}) collective-permute-start(f32[3,4,256]{2,1,0:T(4,128)S(1)} %bitcast.22), channel_id=1, source_target_pairs={{0,1},{1,0},{2,3},{3,2},{4,5},{5,4},{6,7},{7,6},{8,9},{9,8},{10,11... | collective-permute-start | bytes 36872 | tf_op jit(solution)/shard_map/ppermute | solution.py:290
  4.8 0.1 collective-permute-start.4
  4.9 0.0 collective-permute-done.ew_b
  4.9 1.4 %embed.1 = (bf16[1024,512]{1,0:T(8,128)(2,1)S(1)}, bf16[16,1024]{1,0:T(8,128)(2,1)S(1)}) custom-call(bf16[2048,1024]{1,0:T(8,128)(2,1)S(1)} %copy-done, bf16[512,512]{1,0:T(8,128)(2,1)S(1)} %copy-done.2, bf16[512,512]{1,0:T(8,128)(2,1)S(1)} %collective-permute-done.ew_b, f32[1,512]{1,0:T(1,128)S(1)} %bitcast.25), custom_call_target="tpu_custom_call" | custom-call | flops 8589934592 | bytes 4194304 | tf_op jit(solution)/shard_map/embed/pallas_call | solution.py:36
  6.3 0.3 collective-permute-done.3.taps
  6.6 0.1 collective-permute-done.4.feat_w
  6.7 2.4 %keys_other.1 = (bf16[16,512]{1,0:T(8,128)(2,1)S(1)}, bf16[1024,512]{1,0:T(8,128)(2,1)S(1)}, bf16[1024,256]{1,0:T(8,128)(2,1)S(1)}, f32[4,272,128]{2,1,0:T(8,128...) custom-call(f32[6,512]{1,0:T(8,128)S(1)} %broadcast_in_dim.60.after.masks, ...), custom_call_target="tpu_custom_call" | custom-call | flops 12884901888 | bytes 4194304 | tf_op jit(solution)/shard_map/keys_other/pallas_call | solution.py:36
  9.1 0.2 collective-permute-start.5
  9.3 2.1 %keys_own.1 = (bf16[1024,512]{1,0:T(8,128)(2,1)S(1)}, bf16[1024,256]{1,0:T(8,128)(2,1)S(1)}, f32[4,272,128]{2,1,0:T(8,128)S(1)}, f32[272,128]{1,0:T(8,128)S(1)},...) custom-call(f32[6,512]{1,0:T(8,128)S(1)} %broadcast_in_dim.60.after.masks, ...), custom_call_target="tpu_custom_call" | custom-call | flops 12884901888 | bytes 4194304 | tf_op jit(solution)/shard_map/keys_own/pallas_call | solution.py:36
  11.4 2.9 %collective-permute-start.6 = (bf16[272,128]{1,0:T(8,128)(2,1)S(1)}, bf16[272,128]{1,0:T(8,128)(2,1)S(1)}, u32[]{:S(2)}, u32[]{:S(2)}) collective-permute-start(bf16[272,128]{1,0:T(8,128)(2,1)S(1)} %fusion.5.after), channel_id=1, source_target_pairs={{0,6},{2,4},{4,2},{6,0},{8,14},{10,12},{12,10},{14,8},{1,7},{3,5},... | collective-permute-start | bytes 208904 | tf_op jit(solution)/shard_map/ppermute | solution.py:290
  14.4 0.4 %collective-permute-start.7 = (bf16[272,128]{1,0:T(8,128)(2,1)S(1)}, bf16[272,128]{1,0:T(8,128)(2,1)S(1)}, u32[]{:S(2)}, u32[]{:S(2)}) collective-permute-start(bf16[272,128]{1,0:T(8,128)(2,1)S(1)} %fusion.5.after), channel_id=1, source_target_pairs={{0,4},{2,6},{4,0},{6,2},{8,12},{10,14},{12,8},{14,10},{1,5},{3,7},... | collective-permute-start | bytes 208904 | tf_op jit(solution)/shard_map/ppermute | solution.py:290
  14.8 0.5 %collective-permute-start.8 = (bf16[272,128]{1,0:T(8,128)(2,1)S(1)}, bf16[272,128]{1,0:T(8,128)(2,1)S(1)}, u32[]{:S(2)}, u32[]{:S(2)}) collective-permute-start(bf16[272,128]{1,0:T(8,128)(2,1)S(1)} %fusion.5.after), channel_id=1, source_target_pairs={{0,2},{2,0},{4,6},{6,4},{8,10},{10,8},{12,14},{14,12},{1,3},{3,1},... | collective-permute-start | bytes 208904 | tf_op jit(solution)/shard_map/ppermute | solution.py:290
  15.3 2.9 %queries.3 = (bf16[1024,512]{1,0:T(8,128)(2,1)S(1)}, f32[1024,512]{1,0:T(8,128)S(1)}) custom-call(f32[6,512]{1,0:T(8,128)S(1)} %broadcast_in_dim.60.after.masks, bf16[272,128]{1,0:T(8,128)(2,1)S(1)} %fusion.5.after, bf16[1024,512]{1,0:T(8,128)(2,1)S(1)} %get-tuple-element.37.normed, bf16[16,512]{1,0:T(8,128)(2,1)S(1)} %get-tuple-element.42.nrim, ...), custom_call_target="tpu_custom_call" | custom-call | flops 6442450944 | bytes 4194304 | tf_op jit(solution)/shard_map/queries/pallas_call | solution.py:36
  18.3 0.4 %collective-permute-done.7 = bf16[272,128]{1,0:T(8,128)(2,1)S(1)} collective-permute-done((bf16[272,128]{1,0:T(8,128)(2,1)S(1)}, bf16[272,128]{1,0:T(8,128)(2,1)S(1)}, u32[]{:S(2)}, u32[]{:S(2)}) %collective-permute-start.7) | collective-permute-done | bytes 69664 | tf_op jit(solution)/shard_map/ppermute | solution.py:290
  18.7 0.4 %collective-permute-done.8 = bf16[272,128]{1,0:T(8,128)(2,1)S(1)} collective-permute-done((bf16[272,128]{1,0:T(8,128)(2,1)S(1)}, bf16[272,128]{1,0:T(8,128)(2,1)S(1)}, u32[]{:S(2)}, u32[]{:S(2)}) %collective-permute-start.8) | collective-permute-done | bytes 69664 | tf_op jit(solution)/shard_map/ppermute | solution.py:290
  19.1 0.1 fusion.4.after
  19.2 2.8 %collective-permute-start.9 = (bf16[272,128]{1,0:T(8,128)(2,1)S(1)}, bf16[272,128]{1,0:T(8,128)(2,1)S(1)}, u32[]{:S(2)}, u32[]{:S(2)}) collective-permute-start(bf16[272,128]{1,0:T(8,128)(2,1)S(1)} %fusion.4.after), channel_id=1, source_target_pairs={{0,8},{2,10},{4,12},{6,14},{8,0},{10,2},{12,4},{14,6},{1,9},{3,11}... | collective-permute-start | bytes 208904 | tf_op jit(solution)/shard_map/ppermute | solution.py:290
  22.0 2.9 %queries.2 = (bf16[1024,512]{1,0:T(8,128)(2,1)S(1)}, f32[1024,512]{1,0:T(8,128)S(1)}) custom-call(f32[6,512]{1,0:T(8,128)S(1)} %broadcast_in_dim.60.after.masks, bf16[272,128]{1,0:T(8,128)(2,1)S(1)} %fusion.4.after, bf16[1024,512]{1,0:T(8,128)(2,1)S(1)} %get-tuple-element.37.normed, bf16[16,512]{1,0:T(8,128)(2,1)S(1)} %get-tuple-element.42.nrim, ...), custom_call_target="tpu_custom_call" | custom-call | flops 6442450944 | bytes 4194304 | tf_op jit(solution)/shard_map/queries/pallas_call | solution.py:36
  24.9 1.0 %collective-permute-done.9 = bf16[272,128]{1,0:T(8,128)(2,1)S(1)} collective-permute-done((bf16[272,128]{1,0:T(8,128)(2,1)S(1)}, bf16[272,128]{1,0:T(8,128)(2,1)S(1)}, u32[]{:S(2)}, u32[]{:S(2)}) %collective-permute-start.9) | collective-permute-done | bytes 69664 | tf_op jit(solution)/shard_map/ppermute | solution.py:290
  25.9 0.1 fusion
  26.0 0.1 collective-permute-start.10
  26.1 0.7 %attend_own.1.partial = f32[1024,512]{1,0:T(8,128)S(1)} custom-call(bf16[1024,512]{1,0:T(8,128)(2,1)S(1)} %get-tuple-element.59.qf, f32[1024,512]{1,0:T(8,128)S(1)} %get-tuple-element.60.local, f32[272,128]{1,0:T(8,128)S(1)} %get-tuple-element.61.state, bf16[256,512]{1,0:T(8,128)(2,1)S(1)} %get-tuple-element.53.weight), custom_call_target="tpu_custom_call" | custom-call | flops 4294967296 | bytes 4194304 | tf_op jit(solution)/shard_map/attend_own/pallas_call | solution.py:36
  26.8 0.5 %collective-permute-done.10.state = bf16[272,128]{1,0:T(8,128)(2,1)S(1)} collective-permute-done((bf16[272,128]{1,0:T(8,128)(2,1)S(1)}, bf16[272,128]{1,0:T(8,128)(2,1)S(1)}, u32[]{:S(2)}, u32[]{:S(2)}) %collective-permute-start.10) | collective-permute-done | bytes 69664 | tf_op jit(solution)/shard_map/ppermute | solution.py:290
  27.3 1.6 %attend_other.1 = bf16[1024,512]{1,0:T(8,128)(2,1)} custom-call(bf16[1024,512]{1,0:T(8,128)(2,1)S(1)} %get-tuple-element.50.qf, f32[1024,512]{1,0:T(8,128)S(1)} %get-tuple-element.51.local, bf16[272,128]{1,0:T(8,128)(2,1)S(1)} %collective-permute-done.10.state, bf16[256,512]{1,0:T(8,128)(2,1)S(1)} %collective-permute-done.11.weight, ...), custom_call_target="tpu_custom_call" | custom-call | flops 4294967296 | bytes 4194304 | tf_op jit(solution)/shard_map/attend_other/pallas_call | solution.py:36
  (20 shorter events, 0.1 us)
Async XLA Ops:
  0.2 4.1 %copy-start.1 = (bf16[512,3,256]{2,0,1:T(8,128)(2,1)S(1)}, bf16[512,3,256]{2,0,1:T(8,128)(2,1)}, u32[]{:S(2)}) copy-start(bf16[512,3,256]{2,0,1:T(8,128)(2,1)} %param.10) | copy-start | bytes 2359300
  0.2 4.1 %copy-start.4 = (f32[4,3,256]{2,0,1:T(4,128)S(1)}, f32[4,3,256]{2,0,1:T(4,128)}, u32[]{:S(2)}) copy-start(f32[4,3,256]{2,0,1:T(4,128)} %param.11) | copy-start | bytes 36868
  0.2 4.6 %copy-start.3 = (bf16[4,64,128]{2,1,0:T(8,128)(2,1)S(1)}, bf16[4,64,128]{2,1,0:T(8,128)(2,1)}, u32[]{:S(2)}) copy-start(bf16[4,64,128]{2,1,0:T(8,128)(2,1)} %feat_w) | copy-start | bytes 196612
  0.2 4.7 %copy-start = (bf16[2048,1024]{1,0:T(8,128)(2,1)S(1)}, bf16[2048,1024]{1,0:T(8,128)(2,1)}, u32[]{:S(2)}) copy-start(bf16[2048,1024]{1,0:T(8,128)(2,1)} %sig.1) | copy-start | bytes 12582916
  0.2 4.7 %copy-start.2 = (bf16[512,512]{1,0:T(8,128)(2,1)S(1)}, bf16[512,512]{1,0:T(8,128)(2,1)}, u32[]{:S(2)}) copy-start(bf16[512,512]{1,0:T(8,128)(2,1)} %ew_a.1) | copy-start | bytes 1572868
  0.2 4.7 %copy-start.5 = (f32[512]{0:T(512)S(1)}, f32[512]{0:T(512)}, u32[]{:S(2)}) copy-start(f32[512]{0:T(512)} %param.9) | copy-start | bytes 6148
  0.2 4.6 %collective-permute-start = (bf16[512,512]{1,0:T(8,128)(2,1)}, bf16[512,512]{1,0:T(8,128)(2,1)S(1)}, u32[]{:S(2)}, u32[]{:S(2)}) collective-permute-start(bf16[512,512]{1,0:T(8,128)(2,1)} %ew_a.1), channel_id=1, source_target_pairs={{0,1},{1,0},{2,3},{3,2},{4,5},{5,4},{6,7},{7,6},{8,9},{9,8},{10,11... | collective-permute-start | bytes 1572872 | tf_op jit(solution)/shard_map/ppermute | solution.py:290
  1.8 4.8 %collective-permute-start.1 = (bf16[16,1024]{1,0:T(8,128)(2,1)S(1)}, bf16[16,1024]{1,0:T(8,128)(2,1)S(1)}, u32[]{:S(2)}, u32[]{:S(2)}) collective-permute-start(bf16[16,1024]{1,0:T(8,128)(2,1)S(1)} %rim.1), channel_id=1, source_target_pairs={{0,2},{2,4},{4,6},{6,8},{8,10},{10,12},{12,14},{14,15},{3,1},{5,3}... | collective-permute-start | bytes 98312 | tf_op jit(solution)/shard_map/ppermute | solution.py:360
  4.3 2.4 %collective-permute-start.2 = (bf16[3,512,256]{2,1,0:T(8,128)(2,1)S(1)}, bf16[3,512,256]{2,1,0:T(8,128)(2,1)S(1)}, u32[]{:S(2)}, u32[]{:S(2)}) collective-permute-start(bf16[3,512,256]{2,1,0:T(8,128)(2,1)S(1)} %bitcast.19), channel_id=1, source_target_pairs={{0,1},{1,0},{2,3},{3,2},{4,5},{5,4},{6,7},{7,6},{8,9},{9,8},{10,11... | collective-permute-start | bytes 2359304 | tf_op jit(solution)/shard_map/ppermute | solution.py:290
  4.3 2.3 %collective-permute-start.3 = (f32[3,4,256]{2,1,0:T(4,128)S(1)}, f32[3,4,256]{2,1,0:T(4,128)S(1)}, u32[]{:S(2)}, u32[]{:S(2)}) collective-permute-start(f32[3,4,256]{2,1,0:T(4,128)S(1)} %bitcast.22), channel_id=1, source_target_pairs={{0,1},{1,0},{2,3},{3,2},{4,5},{5,4},{6,7},{7,6},{8,9},{9,8},{10,11... | collective-permute-start | bytes 36872 | tf_op jit(solution)/shard_map/ppermute | solution.py:290
  4.8 1.9 %collective-permute-start.4 = (bf16[4,64,128]{2,1,0:T(8,128)(2,1)S(1)}, bf16[4,64,128]{2,1,0:T(8,128)(2,1)S(1)}, u32[]{:S(2)}, u32[]{:S(2)}) collective-permute-start(bf16[4,64,128]{2,1,0:T(8,128)(2,1)S(1)} %copy-done.3), channel_id=1, source_target_pairs={{0,1},{1,0},{2,3},{3,2},{4,5},{5,4},{6,7},{7,6},{8,9},{9,8},{10,11... | collective-permute-start | bytes 196616 | tf_op jit(solution)/shard_map/ppermute | solution.py:290
  9.1 2.4 %collective-permute-start.5 = (bf16[272,128]{1,0:T(8,128)(2,1)S(1)}, bf16[272,128]{1,0:T(8,128)(2,1)S(1)}, u32[]{:S(2)}, u32[]{:S(2)}) collective-permute-start(bf16[272,128]{1,0:T(8,128)(2,1)S(1)} %convert_element_type.35), channel_id=1, source_target_pairs={{0,1},{1,0},{2,3},{3,2},{4,5},{5,4},{6,7},{7,6},{8,9},{9,8},{10,11... | collective-permute-start | bytes 208904 | tf_op jit(solution)/shard_map/ppermute | solution.py:290
  11.4 6.8 %collective-permute-start.6 = (bf16[272,128]{1,0:T(8,128)(2,1)S(1)}, bf16[272,128]{1,0:T(8,128)(2,1)S(1)}, u32[]{:S(2)}, u32[]{:S(2)}) collective-permute-start(bf16[272,128]{1,0:T(8,128)(2,1)S(1)} %fusion.5.after), channel_id=1, source_target_pairs={{0,6},{2,4},{4,2},{6,0},{8,14},{10,12},{12,10},{14,8},{1,7},{3,5},... | collective-permute-start | bytes 208904 | tf_op jit(solution)/shard_map/ppermute | solution.py:290
  14.4 4.3 %collective-permute-start.7 = (bf16[272,128]{1,0:T(8,128)(2,1)S(1)}, bf16[272,128]{1,0:T(8,128)(2,1)S(1)}, u32[]{:S(2)}, u32[]{:S(2)}) collective-permute-start(bf16[272,128]{1,0:T(8,128)(2,1)S(1)} %fusion.5.after), channel_id=1, source_target_pairs={{0,4},{2,6},{4,0},{6,2},{8,12},{10,14},{12,8},{14,10},{1,5},{3,7},... | collective-permute-start | bytes 208904 | tf_op jit(solution)/shard_map/ppermute | solution.py:290
  14.8 4.3 %collective-permute-start.8 = (bf16[272,128]{1,0:T(8,128)(2,1)S(1)}, bf16[272,128]{1,0:T(8,128)(2,1)S(1)}, u32[]{:S(2)}, u32[]{:S(2)}) collective-permute-start(bf16[272,128]{1,0:T(8,128)(2,1)S(1)} %fusion.5.after), channel_id=1, source_target_pairs={{0,2},{2,0},{4,6},{6,4},{8,10},{10,8},{12,14},{14,12},{1,3},{3,1},... | collective-permute-start | bytes 208904 | tf_op jit(solution)/shard_map/ppermute | solution.py:290
  19.2 6.7 %collective-permute-start.9 = (bf16[272,128]{1,0:T(8,128)(2,1)S(1)}, bf16[272,128]{1,0:T(8,128)(2,1)S(1)}, u32[]{:S(2)}, u32[]{:S(2)}) collective-permute-start(bf16[272,128]{1,0:T(8,128)(2,1)S(1)} %fusion.4.after), channel_id=1, source_target_pairs={{0,8},{2,10},{4,12},{6,14},{8,0},{10,2},{12,4},{14,6},{1,9},{3,11}... | collective-permute-start | bytes 208904 | tf_op jit(solution)/shard_map/ppermute | solution.py:290
  22.0 5.4 %collective-permute-start.11 = (bf16[256,512]{1,0:T(8,128)(2,1)S(1)}, bf16[256,512]{1,0:T(8,128)(2,1)S(1)}, u32[]{:S(2)}, u32[]{:S(2)}) collective-permute-start(bf16[256,512]{1,0:T(8,128)(2,1)S(1)} %get-tuple-element.53.weight), channel_id=1, source_target_pairs={{0,1},{1,0},{2,3},{3,2},{4,5},{5,4},{6,7},{7,6},{8,9},{9,8},{10,11... | collective-permute-start | bytes 786440 | tf_op jit(solution)/shard_map/ppermute | solution.py:290
  26.0 1.3 %collective-permute-start.10 = (bf16[272,128]{1,0:T(8,128)(2,1)S(1)}, bf16[272,128]{1,0:T(8,128)(2,1)S(1)}, u32[]{:S(2)}, u32[]{:S(2)}) collective-permute-start(bf16[272,128]{1,0:T(8,128)(2,1)S(1)} %get-tuple-element.62), channel_id=1, source_target_pairs={{0,1},{1,0},{2,3},{3,2},{4,5},{5,4},{6,7},{7,6},{8,9},{9,8},{10,11... | collective-permute-start | bytes 208904 | tf_op jit(solution)/shard_map/ppermute | solution.py:290
